TPU v7x, 128 devices: a whole 4x4x4 slice. The times are simulated.
128 devices in a mesh: tp: 4 (over y_lo, core), dp: 32 (over x, z, y_hi).
Axes of the slice: x: 4, y: 4 (y_hi: 2, y_lo: 2; y = y_hi * 2 + y_lo), z: 4, core: 2. Of those that a mesh axis runs over, the one named last changes fastest.
Arguments:
- teacher_query: bfloat16 [8192, 8192], P('dp', 'tp'), may hold values from -8 to 8
- student_hidden: bfloat16 [8192, 4096], P('dp', 'tp'), may hold values from -16 to 16
- query_weight: bfloat16 [4096, 4096], P('dp', 'tp'), may hold values from -0.039794922 to 0.039794922
Outputs:
- kl_rows: float32 [128, 2048], P(('tp', 'dp'))
- weight_grad: float32 [4096, 4096], P('dp', 'tp')
All inputs are finite; a program needn't handle non-finite values.
Results may differ from a plain program's by a relative error of at most 0.0029.
Values may be sent and summed in bfloat16 or wider, within the bound.
No kernel may reach another device: no remote copies, remote signals or barrier semaphores. Data moves between devices by JAX's collectives and lax.ppermute only.
A program may use at most 64 MiB of HBM per device.

v0:
```python
import jax
import jax.numpy as jnp
from jax import lax
from jax.sharding import PartitionSpec as P

RHEADS = 32
NSEQ = 2
SEQ = 4096


def from_everyone(value, axis):
    copies = jnp.broadcast_to(value, (lax.axis_size(axis), *value.shape))
    return lax.all_to_all(copies, axis, split_axis=0, concat_axis=0, tiled=True)


def laid_out(parts, dim):
    lengths = list(parts.shape[1:])
    lengths[dim] *= parts.shape[0]
    return jnp.moveaxis(parts, 0, dim).reshape(lengths)


def gather_directly(value, axis, dim):
    parts = from_everyone(value, axis)
    return laid_out(parts, dim)


def in_one_piece(arrays, axis, split_dim, concat_dim, along):
    ends, at = ([], 0)
    for a in arrays[:-1]:
        at += a.shape[along]
        ends.append(at)
    both = jnp.concatenate(arrays, axis=along)
    return tuple(
        jnp.split(
            lax.all_to_all(both, axis, split_axis=split_dim, concat_axis=concat_dim, tiled=True),
            ends,
            axis=along,
        )
    )


def spread_heads(queries, heads, copies):
    rows = queries.shape[0]
    width = queries.shape[1] // heads
    shaped = queries.reshape(rows, heads, 1, width)
    return jnp.broadcast_to(shaped, (rows, heads, copies, width)).reshape(
        rows, heads * copies, width
    )


def local(teacher_query, student_hidden, query_weight):
    heads_here = RHEADS // lax.axis_size("tp")
    copies = lax.axis_size("dp") // heads_here
    rows = teacher_query.shape[0]
    teacher_width = teacher_query.shape[1] // heads_here
    hidden_full = gather_directly(student_hidden, "tp", 1)
    teacher_send = spread_heads(teacher_query, heads_here, copies)
    projected = jnp.dot(
        hidden_full,
        lax.all_gather(query_weight, "dp", axis=0, tiled=True),
        preferred_element_type=jnp.float32,
    )
    student_query = projected.astype(jnp.bfloat16)
    student_width = student_query.shape[1] // heads_here
    student_send = spread_heads(student_query, heads_here, copies)
    teacher_all, student_all = in_one_piece((teacher_send, student_send), "dp", 1, 0, 2)
    total_rows = teacher_all.shape[0]
    teacher_all = teacher_all.reshape(total_rows, teacher_width)
    student_all = student_all.reshape(total_rows, student_width)
    teacher_scale = teacher_width ** (-0.5)
    student_scale = student_width ** (-0.5)
    query_rows = SEQ // copies
    first_row = lax.axis_index("dp") % copies * query_rows
    block = min(512, query_rows)
    blocks_each = query_rows // block

    def relation_step(step, carry):
        kl_store, grad_store = carry
        sequence = step // blocks_each
        offset = step % blocks_each * block
        base = sequence * SEQ
        start = base + first_row + offset
        teacher_keys = lax.dynamic_slice_in_dim(teacher_all, base, SEQ, 0)
        student_keys = lax.dynamic_slice_in_dim(student_all, base, SEQ, 0)
        teacher_rows = lax.dynamic_slice_in_dim(teacher_all, start, block, 0)
        student_rows = lax.dynamic_slice_in_dim(student_all, start, block, 0)
        teacher_scores = (
            lax.dot_general(
                teacher_rows,
                teacher_keys,
                (((1,), (1,)), ((), ())),
                preferred_element_type=jnp.float32,
            )
            * teacher_scale
        )
        student_scores = (
            lax.dot_general(
                student_rows,
                student_keys,
                (((1,), (1,)), ((), ())),
                preferred_element_type=jnp.float32,
            )
            * student_scale
        )
        teacher_log = jax.nn.log_softmax(teacher_scores, axis=-1)
        student_log = jax.nn.log_softmax(student_scores, axis=-1)
        teacher_prob = jnp.exp(teacher_log)
        divergence = jnp.sum(teacher_prob * (teacher_log - student_log), axis=-1)
        score_grad = (jnp.exp(student_log) - teacher_prob).astype(jnp.bfloat16)
        key_part = (
            lax.dot_general(
                score_grad,
                student_rows,
                (((0,), (0,)), ((), ())),
                preferred_element_type=jnp.float32,
            )
            * student_scale
        )
        row_part = (
            jnp.dot(score_grad, student_keys, preferred_element_type=jnp.float32) * student_scale
        )
        seq_grad = lax.dynamic_slice_in_dim(grad_store, base, SEQ, 0)
        grad_store = lax.dynamic_update_slice_in_dim(grad_store, seq_grad + key_part, base, 0)
        current = lax.dynamic_slice_in_dim(grad_store, start, block, 0)
        grad_store = lax.dynamic_update_slice_in_dim(grad_store, current + row_part, start, 0)
        kl_store = lax.dynamic_update_slice_in_dim(
            kl_store, divergence, sequence * query_rows + offset, 0
        )
        return (kl_store, grad_store)

    kl_init = jnp.zeros((NSEQ * query_rows,), jnp.float32)
    grad_init = jnp.zeros((total_rows, student_width), jnp.float32)
    kl_store, grad_store = lax.fori_loop(0, NSEQ * blocks_each, relation_step, (kl_init, grad_init))
    returned = lax.all_to_all(
        grad_store.reshape(heads_here * copies, rows, student_width),
        "dp",
        split_axis=0,
        concat_axis=2,
        tiled=True,
    )
    summed = jnp.sum(returned.reshape(rows, heads_here, copies, student_width), axis=2)
    query_grad = summed.reshape(rows, heads_here * student_width).astype(jnp.bfloat16)
    feature_block = lax.all_to_all(hidden_full, "dp", split_axis=1, concat_axis=0, tiled=True)
    weight_grad = lax.dot_general(
        feature_block,
        lax.all_gather(query_grad, "dp", axis=0, tiled=True),
        (((0,), (0,)), ((), ())),
        preferred_element_type=jnp.float32,
    )
    return (kl_store.reshape(1, NSEQ * query_rows), weight_grad)


def solution(mesh):
    placed = (P("dp", "tp"), P("dp", "tp"), P("dp", "tp"))
    return jax.shard_map(
        local,
        mesh=mesh,
        in_specs=placed,
        out_specs=(P(("tp", "dp"), None), P("dp", "tp")),
        check_vma=False,
    )
```

profile of v0, /device:TPU:8, one launch (start us, length us, event | category | flops | bytes accessed | tf_op | source)
XLA Modules:
  0.0 571.5 jit_solution(10103598577909109360)
XLA Ops:
  10.7 3.9 all-to-all-start
  15.9 24.6 %all-to-all-done = bf16[4,256,1024]{1,2,0:T(8,128)(2,1)S(1)} async-done(((bf16[4,256,1024]{1,2,0:T(8,128)(2,1)}), bf16[4,256,1024]{1,2,0:T(8,128)(2,1)S(1)}, u32[]{:S(2)}, u32[]{:S(2)}) %all-to-all-start) | async-done | bytes 2097184 | tf_op jit(solution)/shard_map/all_to_all | solution.py:13
  40.5 78.1 %all-gather.3.cloned.1.call-done = bf16[4096,1024]{1,0:T(8,128)(2,1)} async-done(((bf16[128,1024]{1,0:T(8,128)(2,1)}), bf16[4096,1024]{1,0:T(8,128)(2,1)}) %all-gather.3.cloned.1.call-update) | async-done | bytes 8388624 | tf_op jit(solution)/shard_map/all_gather | solution.py:60
  118.6 5.7 %fusion.16 = bf16[32,8,8,128]{3,2,1,0:T(8,128)(2,1)S(1)} fusion(bf16[256,4096]{0,1:T(8,128)(2,1)S(1)} %bitcast.49, bf16[4096,1024]{1,0:T(8,128)(2,1)} %all-gather.3.cloned.1.call-done), kind=kOutput, calls=%fused_computation.32 | convolution fusion | flops 2147745792 | bytes 11010048 | tf_op jit(solution)/shard_map/dot_general | solution.py:58
  125.5 3.4 pad_maximum_fusion
  128.9 6.5 %all-to-all-start.1 = ((bf16[256,32,384]{2,0,1:T(8,128)(2,1)}), bf16[256,32,384]{2,0,1:T(8,128)(2,1)}, u32[]{:S(2)}, u32[]{:S(2)}) async-start(bf16[256,32,384]{2,0,1:T(8,128)(2,1)} %pad_maximum_fusion), calls=%async_computation.1 | async-start | bytes 12582912 | tf_op jit(solution)/shard_map/all_to_all | solution.py:35
  135.7 96.9 %all-to-all-done.1 = bf16[256,32,384]{2,0,1:T(8,128)(2,1)} async-done(((bf16[256,32,384]{2,0,1:T(8,128)(2,1)}), bf16[256,32,384]{2,0,1:T(8,128)(2,1)}, u32[]{:S(2)}, u32[]{:S(2)}) %all-to-all-start.1) | async-done | bytes 6291488 | tf_op jit(solution)/shard_map/all_to_all | solution.py:35
  234.3 4.5 slice_bitcast_fusion
  241.1 87.4 %while.17 = (s32[]{:T(128)}, f32[2048]{0:T(1024)S(1)}, f32[8192,128]{1,0:T(8,128)}, s32[]{:T(128)}, bf16[8192,256]{1,0:T(8,128)(2,1)}, /*index=5*/bf16[8192,128]...) while((s32[]{:T(128)}, f32[2048]{0:T(1024)S(1)}, ...), condition=%wide.region_4.6_spmd, body=%wide.region_0.5_spmd.sunk | while | flops 2729571840 | bytes 89164272 | solution.py:133
  248.5 5.7 subtract_convert_fusion.2
  254.4 5.6 fusion.33
  270.4 5.7 subtract_convert_fusion.2
  276.2 5.6 fusion.33
  284.8 3.1 multiply_reduce_fusion.5
  292.2 5.7 subtract_convert_fusion.2
  298.0 5.6 fusion.33
  306.6 3.1 multiply_reduce_fusion.5
  314.0 5.7 subtract_convert_fusion.2
  319.9 5.6 fusion.33
  328.5 56.0 %all_to_all.57 = f32[32,256,128]{2,1,0:T(8,128)S(1)} all-to-all(f32[32,256,128]{2,1,0:T(8,128)} %bitcast.48), channel_id=1, replica_groups=mesh['tp'=4,'dp'=32] {'dp'}, dimensions={0} | all-to-all | bytes 8388608 | tf_op jit(solution)/shard_map/all_to_all | solution.py:134
  385.8 41.3 %all_to_all.58 = bf16[256,32,128]{0,2,1:T(8,128)(2,1)} all-to-all(bf16[256,32,128]{0,2,1:T(8,128)(2,1)S(1)} %bitcast.50), channel_id=1, replica_groups=mesh['tp'=4,'dp'=32] {'dp'}, dimensions={1} | all-to-all | bytes 4194304 | tf_op jit(solution)/shard_map/all_to_all | solution.py:143
  427.1 3.2 copy.22
  430.3 125.2 %all-gather.5.cloned.1.call-done = bf16[8192,1024]{0,1:T(8,128)(2,1)} async-done(((bf16[256,1024]{0,1:T(8,128)(2,1)}), bf16[8192,1024]{0,1:T(8,128)(2,1)}) %all-gather.5.cloned.1.call-update) | async-done | bytes 16777232 | tf_op jit(solution)/shard_map/all_gather | solution.py:146
  555.6 8.1 %convolution_bitcast_fusion = f32[128,1024]{0,1:T(8,128)S(1)} fusion(bf16[8192,1024]{0,1:T(8,128)(2,1)} %all-gather.5.cloned.1.call-done, bf16[8192,128]{1,0:T(8,128)(2,1)S(1)} %bitcast.56), kind=kOutput, calls=%fused_computation.33 | convolution fusion | flops 2147483648 | bytes 19398656 | tf_op jit(solution)/shard_map/dot_general | solution.py:144
  (60 shorter events, 48.5 us)
Async XLA Ops:
  7.2 111.4 %all-gather.3.cloned.1.call-start = ((), (), s32[]{:S(2)}) async-start(), calls=%async_computation.4 | async-start | bytes 8650752 | tf_op jit(solution)/shard_map/all_gather | solution.py:60
  10.7 29.8 %all-to-all-start = ((bf16[4,256,1024]{1,2,0:T(8,128)(2,1)}), bf16[4,256,1024]{1,2,0:T(8,128)(2,1)S(1)}, u32[]{:S(2)}, u32[]{:S(2)}) async-start(bf16[4,256,1024]{1,2,0:T(8,128)(2,1)} %broadcast_in_dim.29), calls=%async_computation | async-start | bytes 4194304 | tf_op jit(solution)/shard_map/all_to_all | solution.py:13
  40.5 83.8 %copy-start.1 = (bf16[4,256,1024]{1,2,0:T(8,128)(2,1)}, bf16[4,256,1024]{1,2,0:T(8,128)(2,1)S(1)}, u32[]{:S(2)}) copy-start(bf16[4,256,1024]{1,2,0:T(8,128)(2,1)S(1)} %all-to-all-done) | copy-start | bytes 6291460
  128.9 103.6 %all-to-all-start.1 = ((bf16[256,32,384]{2,0,1:T(8,128)(2,1)}), bf16[256,32,384]{2,0,1:T(8,128)(2,1)}, u32[]{:S(2)}, u32[]{:S(2)}) async-start(bf16[256,32,384]{2,0,1:T(8,128)(2,1)} %pad_maximum_fusion), calls=%async_computation.1 | async-start | bytes 12582912 | tf_op jit(solution)/shard_map/all_to_all | solution.py:35
  135.4 420.2 %all-gather.5.cloned.1.call-start = ((), (), s32[]{:S(2)}) async-start(), calls=%async_computation.5 | async-start | bytes 17301504 | tf_op jit(solution)/shard_map/all_gather | solution.py:146
  254.4 5.6 copy-start
  276.2 5.6 copy-start
  298.0 5.6 copy-start
  319.9 5.6 copy-start
  328.5 56.3 %copy-start.3 = (f32[2048]{0:T(1024)}, f32[2048]{0:T(1024)S(1)}, u32[]{:S(2)}) copy-start(f32[2048]{0:T(1024)S(1)} %get-tuple-element.161) | copy-start | bytes 24580
  328.5 57.3 %copy-start.2 = (bf16[4,256,1024]{1,2,0:T(8,128)(2,1)S(1)}, bf16[4,256,1024]{1,2,0:T(8,128)(2,1)}, u32[]{:S(2)}) copy-start(bf16[4,256,1024]{1,2,0:T(8,128)(2,1)} %copy-done.1) | copy-start | bytes 6291460
Sparse Core Ops, SparseCore 0:
  11.0 107.5 all-gather.2
  385.9 169.6 all-gather.4
where the time goes:
time: 573 us; the launch traced here: 572 us
  waiting for transfers between devices  325 us (57%)
  blocking collectives  97.4 us (17%)
  matrix products  65.7 us (11%)
  other arithmetic  38.4 us (7%)
  local copies, waits for them, and re-layouts  19.7 us (3%)
  between operations  14.2 us (2%)
  starting transfers between devices  10.7 us (2%)
    all_gather x1, waiting for transfers between devices, local(): lax.all_gather(query_grad, 'dp', axis=0, tiled=True)  125 us
    all_to_all x1, waiting for transfers between devices, in_one_piece(): lax.all_to_all(both, axis, split_axis=split_dim, concat_axis=concat_dim,...  96.9 us
    all_gather x1, waiting for transfers between devices, local(): lax.all_gather(query_weight, 'dp', axis=0, tiled=True)  78.1 us
    all_to_all x1, blocking collectives, local(): lax.all_to_all(grad_store.reshape(heads_here * copies, rows, student_widt...  56 us
    all_to_all x1, blocking collectives, local(): lax.all_to_all(hidden_full, 'dp', split_axis=1, concat_axis=0, tiled=True)  41.3 us
    all_to_all x1, waiting for transfers between devices, from_everyone(): return lax.all_to_all(copies, axis, split_axis=0, concat_axis=0, tiled=True)  24.6 us
    convert_element_type x4, other arithmetic, relation_step(): score_grad = (jnp.exp(student_log) - teacher_prob).astype(jnp.bfloat16)  22.7 us
    dot_general x4, matrix products, relation_step(): lax.dot_general(score_grad, student_rows, (((0,), (0,)), ((), ())), prefe...  22.5 us
  transfers between devices with their start and end apart: 4, of which 4 were waited for; matrix products, arithmetic and copies ran while one was open for 1% of the time, Pallas kernels for 0%

commit v1 on v0

v1 whole, which is shorter than its diff:
```python
import functools

import jax
import jax.numpy as jnp
from jax import lax
from jax.experimental import pallas as pl
from jax.experimental.pallas import tpu as pltpu
from jax.sharding import Mesh, PartitionSpec as P

RHEADS = 32
NSEQ = 2
SEQ = 4096
LOG2E = 1.4426950408889634
LN2 = 0.6931471805599453
LANES = 128

TP = ("yl", "core")
DP = ("xh", "xl", "zh", "zl", "yh")
BLOCK = ("xl", "zh")
COLUMN = ("zl", "yh")

CONTRACT_LAST = (((1,), (1,)), ((), ()))
CONTRACT_FIRST = (((0,), (0,)), ((), ()))


def lane_fold(x, op):
    acc = x[:, :LANES]
    for j in range(1, x.shape[1] // LANES):
        acc = op(acc, x[:, j * LANES : (j + 1) * LANES])
    return acc


def relation_kernel(block, chunk, sub, t_rows, s_rows, t_all, s_all, kl_ref, grad_ref, u_scr, v_scr, g_scr):
    step = pl.program_id(0)
    seq = t_all.shape[0]
    student_scale = s_all.shape[1] ** -0.5
    t_mul = LOG2E * t_all.shape[1] ** -0.5
    s_mul = LOG2E * student_scale

    @pl.when(step == 0)
    def _():
        grad_ref[...] = jnp.zeros_like(grad_ref)

    tr = t_rows[...]
    sr = s_rows[...]
    mt = ms = None
    for c in range(0, seq, chunk):
        u = t_mul * lax.dot_general(tr, t_all[c : c + chunk, :], CONTRACT_LAST, preferred_element_type=jnp.float32)
        u_scr[:, c : c + chunk] = u
        fold = lane_fold(u, jnp.maximum)
        mt = fold if mt is None else jnp.maximum(mt, fold)
        v = s_mul * lax.dot_general(sr, s_all[c : c + chunk, :], CONTRACT_LAST, preferred_element_type=jnp.float32)
        v_scr[:, c : c + chunk] = v
        fold = lane_fold(v, jnp.maximum)
        ms = fold if ms is None else jnp.maximum(ms, fold)
    mt = jnp.max(mt, axis=1, keepdims=True)
    ms = jnp.max(ms, axis=1, keepdims=True)
    for r in range(0, block, sub):
        rows = slice(r, r + sub)
        m_t = jnp.broadcast_to(mt[rows], (sub, LANES))
        m_s = jnp.broadcast_to(ms[rows], (sub, LANES))
        zero = jnp.zeros((sub, LANES), jnp.float32)
        lt, ls, a = zero, zero, zero
        for c in range(0, seq, LANES):
            x = u_scr[rows, c : c + LANES] - m_t
            y = v_scr[rows, c : c + LANES] - m_s
            et = jnp.exp2(x)
            lt = lt + et
            ls = ls + jnp.exp2(y)
            a = a + et * (x - y)
        lt = jnp.sum(lt, axis=1, keepdims=True)
        ls = jnp.sum(ls, axis=1, keepdims=True)
        a = jnp.sum(a, axis=1, keepdims=True)
        log_t = jnp.log2(lt)
        log_s = jnp.log2(ls)
        kl = (a / lt - log_t + log_s) * LN2
        kl_ref[rows, :] = jnp.broadcast_to(kl, (sub, LANES))
        z_t = jnp.broadcast_to(mt[rows] + log_t, (sub, LANES))
        z_s = jnp.broadcast_to(ms[rows] + log_s, (sub, LANES))
        for c in range(0, seq, LANES):
            g = jnp.exp2(v_scr[rows, c : c + LANES] - z_s) - jnp.exp2(u_scr[rows, c : c + LANES] - z_t)
            g_scr[rows, c : c + LANES] = g.astype(jnp.bfloat16)
    acc = jnp.zeros((block, s_all.shape[1]), jnp.float32)
    for c in range(0, seq, chunk):
        g = g_scr[:, c : c + chunk]
        acc = acc + jnp.dot(g, s_all[c : c + chunk, :], preferred_element_type=jnp.float32)
        grad_ref[c : c + chunk, :] += lax.dot_general(g, sr, CONTRACT_FIRST, preferred_element_type=jnp.float32)
    start = pl.multiple_of(lax.axis_index("zh") * (seq // 2) + step * block, block)
    grad_ref[pl.ds(start, block), :] += acc

    @pl.when(step == pl.num_programs(0) - 1)
    def _():
        grad_ref[...] = grad_ref[...] * student_scale


def relation(t_all, s_all, block=256, chunk=512, sub=32):
    seq, t_width = t_all.shape
    s_width = s_all.shape[1]
    rows = seq // 2
    steps = rows // block

    def row_map(i):
        return (lax.axis_index("zh") * steps + i, 0)

    def whole(i):
        return (0, 0)

    return pl.pallas_call(
        functools.partial(relation_kernel, block, chunk, sub),
        grid=(steps,),
        in_specs=[
            pl.BlockSpec((block, t_width), row_map),
            pl.BlockSpec((block, s_width), row_map),
            pl.BlockSpec((seq, t_width), whole),
            pl.BlockSpec((seq, s_width), whole),
        ],
        out_specs=[
            pl.BlockSpec((block, LANES), lambda i: (i, 0)),
            pl.BlockSpec((seq, s_width), whole),
        ],
        out_shape=[
            jax.ShapeDtypeStruct((rows, LANES), jnp.float32),
            jax.ShapeDtypeStruct((seq, s_width), jnp.float32),
        ],
        scratch_shapes=[
            pltpu.VMEM((block, seq), jnp.float32),
            pltpu.VMEM((block, seq), jnp.float32),
            pltpu.VMEM((block, seq), jnp.bfloat16),
        ],
        compiler_params=pltpu.CompilerParams(vmem_limit_bytes=56 << 20),
    )(t_all, s_all, t_all, s_all)


def exchange(chunks, axes):
    return lax.all_to_all(chunks, axes, split_axis=0, concat_axis=0, tiled=True)


def local(teacher_query, student_hidden, query_weight):
    rows = teacher_query.shape[0]
    depth, columns = query_weight.shape
    t_width = teacher_query.shape[1] // 8
    s_width = columns // 8
    width = columns // 4
    hidden = lax.all_gather(student_hidden, TP + COLUMN, axis=0, tiled=True)
    hidden = hidden.reshape(4, 4 * rows, columns)
    parts = jnp.moveaxis(query_weight.reshape(depth, 4, width), 1, 0)
    weight = exchange(jnp.broadcast_to(parts, (8, 4, depth, width)).reshape(32, depth, width), DP)
    weight = weight.reshape(4, 8 * depth, width)
    heads = jnp.moveaxis(teacher_query.reshape(rows, 4, 2, t_width), 0, 2)
    heads = jnp.moveaxis(heads, 1, 0)[:, None]
    heads = jnp.broadcast_to(heads, (2, 2, 4, rows, t_width)).reshape(16, rows, t_width)
    teacher = exchange(heads, BLOCK + COLUMN).reshape(SEQ, t_width)
    student = lax.dot_general(
        hidden, weight, (((0, 2), (0, 1)), ((), ())), preferred_element_type=jnp.float32
    ).astype(jnp.bfloat16)
    pair = jnp.moveaxis(student.reshape(4 * rows, 2, s_width), 1, 0)[:, None]
    pair = jnp.broadcast_to(pair, (2, 2, 4 * rows, s_width)).reshape(4, 4 * rows, s_width)
    student_all = exchange(pair, BLOCK).reshape(SEQ, s_width)
    kl, grad = relation(teacher, student_all)
    terms = exchange(grad.reshape(4, 4 * rows, s_width), BLOCK)
    terms = terms.reshape(2, 2, 4 * rows, s_width)
    summed = (terms[:, 0] + terms[:, 1]).astype(jnp.bfloat16)
    query_grad = jnp.moveaxis(summed, 0, 1).reshape(4 * rows, width)
    partial = lax.dot_general(
        hidden, query_grad, (((1,), (0,)), ((), ())), preferred_element_type=jnp.float32
    )
    sent = exchange(partial.astype(jnp.bfloat16).reshape(32, depth, width), DP)
    weight_grad = jnp.sum(sent.reshape(8, 4, depth, width).astype(jnp.float32), axis=0)
    weight_grad = jnp.moveaxis(weight_grad, 0, 1).reshape(depth, columns)
    all_kl = lax.all_gather(kl[:, 0], DP, axis=0).reshape(2, 2, 2, 4, 2, SEQ // 4)
    dp = lax.axis_index(DP)
    head, quarter = dp // 4, dp % 4
    row = lax.dynamic_slice(
        all_kl, (0, head % 2, quarter // 2, head // 2, quarter % 2, 0), (2, 1, 1, 1, 1, SEQ // 4)
    )
    return row.reshape(1, NSEQ * (SEQ // 4)), weight_grad


def solution(mesh):
    bits = Mesh(mesh.devices.reshape((2,) * 7), TP + DP)
    return jax.shard_map(
        local,
        mesh=bits,
        in_specs=(P(DP, TP), P(DP, TP), P(DP, TP)),
        out_specs=(P(TP + DP, None), P(DP, TP)),
        check_vma=False,
    )
```

time: 573 us -> 1060 us (1.85)
  the two profiles are of different devices: /device:TPU:8 before, /device:TPU:44 now
where the time goes in v1:
time: 1060 us
  blocking collectives  837 us (79%)
  waiting for transfers between devices  85.3 us (8%)
  Pallas kernels  53.9 us (5%)
  starting transfers between devices  27.4 us (3%)
  other arithmetic  15.7 us (1%)
  between operations  14.3 us (1%)
  matrix products  12.1 us (1%)
  local copies, waits for them, and re-layouts  11.1 us (1%)
    all_gather x1, blocking collectives, local(): lax.all_gather(kl[:, 0], DP, axis=0).reshape(2, 2, 2, 4, 2, SEQ // 4)  790 us
    all_gather x1, waiting for transfers between devices, local(): hidden = lax.all_gather(student_hidden, TP + COLUMN, axis=0, tiled=True)  55.3 us
    pallas_call x1, Pallas kernels, relation(): pl.pallas_call(functools.partial(relation_kernel, block, chunk, sub), gri...  53.9 us
    all_to_all x2, blocking collectives, exchange(): return lax.all_to_all(chunks, axes, split_axis=0, concat_axis=0, tiled=True)  47.8 us
    all_to_all x3, waiting for transfers between devices, exchange(): return lax.all_to_all(chunks, axes, split_axis=0, concat_axis=0, tiled=True)  29.3 us
    all_to_all x3, starting transfers between devices, exchange(): return lax.all_to_all(chunks, axes, split_axis=0, concat_axis=0, tiled=True)  27.3 us
  transfers between devices with their start and end apart: 4, of which 2 were waited for; matrix products, arithmetic and copies ran while one was open for 3% of the time, Pallas kernels for 0%

profile of v1, /device:TPU:44, one launch (start us, length us, event | category | flops | bytes accessed | tf_op | source)
XLA Modules:
  0.0 1057.2 jit_solution(6481815540704196745)
XLA Ops:
  7.2 0.7 all-gather.3.cloned.1.call-update
  7.9 1.1 reshape.66
  9.1 1.6 broadcast_in_dim.7
  10.6 9.9 all-to-all-start.1
  20.6 0.8 reshape.62
  21.6 29.3 %all-to-all-done.1 = bf16[32,128,256]{2,1,0:T(8,128)(2,1)} async-done(((bf16[32,128,256]{2,1,0:T(8,128)(2,1)}), bf16[32,128,256]{2,1,0:T(8,128)(2,1)}, u32[]{:S(2)}, u32[]{:S(2)}) %all-to-all-start.1) | async-done | bytes 2097184 | tf_op jit(solution)/shard_map/all_to_all | solution.py:135
  50.9 1.6 broadcast_in_dim.6
  52.5 7.1 all-to-all-start
  59.6 55.3 %all-gather.3.cloned.1.call-done = bf16[4096,1024]{1,0:T(8,128)(2,1)} async-done(((bf16[256,1024]{1,0:T(8,128)(2,1)}), bf16[4096,1024]{1,0:T(8,128)(2,1)}) %all-gather.3.cloned.1.call-update) | async-done | bytes 8388624 | tf_op jit(solution)/shard_map/all_gather | solution.py:144
  114.9 6.3 fusion
  121.3 0.3 copy.27
  121.7 18.7 %all_to_all.25 = bf16[4,1024,128]{2,1,0:T(8,128)(2,1)} all-to-all(bf16[4,1024,128]{2,1,0:T(8,128)(2,1)S(1)} %bitcast.46), channel_id=1, replica_groups=mesh['yl'=2,'core'=2,'xh'=2,'xl'=2,'zh'=2,'zl'=2,'yh'=2] {'xl','zh'}, dimensions={0} | all-to-all | bytes 2097152 | tf_op jit(solution)/shard_map/all_to_all | solution.py:135
  140.4 53.9 %shard_map.50 = (f32[2048,128]{1,0:T(8,128)}, f32[4096,128]{1,0:T(8,128)}) custom-call(bf16[4096,256]{1,0:T(8,128)(2,1)} %bitcast.38, bf16[4096,128]{1,0:T(8,128)(2,1)} %bitcast.40, bf16[4096,256]{1,0:T(8,128)(2,1)} %bitcast.39, bf16[4096,128]{1,0:T(8,128)(2,1)} %bitcast.41), custom_call_target="tpu_custom_call" | custom-call | tf_op jit(solution)/shard_map/pallas_call | solution.py:108
  194.3 29.1 %all_to_all.26 = f32[4,1024,128]{2,1,0:T(8,128)S(1)} all-to-all(f32[4,1024,128]{2,1,0:T(8,128)} %bitcast.49), channel_id=1, replica_groups=mesh['yl'=2,'core'=2,'xh'=2,'xl'=2,'zh'=2,'zl'=2,'yh'=2] {'xl','zh'}, dimensions={0} | all-to-all | bytes 4194304 | tf_op jit(solution)/shard_map/all_to_all | solution.py:135
  223.5 0.3 copy.35
  223.9 0.3 copy.34
  224.4 5.7 convert_bitcast_fusion
  230.1 2.6 copy.30
  232.7 10.3 all-to-all-start.4
  243.1 789.7 %all-gather = f32[65536,1]{1,0:T(8,128)} all-gather(f32[2048,1]{1,0:T(8,128)S(1)} %bitcast.51), channel_id=2, replica_groups=mesh['yl'=2,'core'=2,'xh'=2,'xl'=2,'zh'=2,'zl'=2,'yh'=2] {'xh','xl','zh'..., dimensions={0}, use_global_device_ids=true | all-gather | bytes 270336 | tf_op jit(solution)/shard_map/all_gather | solution.py:170
  1032.8 15.3 %reduce = f32[65536]{0:T(1024)S(1)} reduce(f32[65536,1]{1,0:T(8,128)} %all-gather, f32[]{:T(128)} %constant.78), dimensions={1}, to_apply=%all-gather.reduce_sub_computation | reduce | bytes 524292 | tf_op jit(solution)/shard_map/all_gather | solution.py:170
  1048.2 0.6 constant_dynamic-slice_fusion
  1048.9 0.3 convert_reduce_fusion
  1049.3 1.0 copy.32
  (16 shorter events, 1.1 us)
Async XLA Ops:
  7.2 107.8 %all-gather.3.cloned.1.call-start = ((), (), s32[]{:S(2)}) async-start(), calls=%async_computation.5 | async-start | bytes 8912896 | tf_op jit(solution)/shard_map/all_gather | solution.py:144
  10.6 9.9 copy-start.2
  10.6 40.3 %all-to-all-start.1 = ((bf16[32,128,256]{2,1,0:T(8,128)(2,1)}), bf16[32,128,256]{2,1,0:T(8,128)(2,1)}, u32[]{:S(2)}, u32[]{:S(2)}) async-start(bf16[32,128,256]{2,1,0:T(8,128)(2,1)} %bitcast.5), calls=%async_computation.1 | async-start | bytes 4194304 | tf_op jit(solution)/shard_map/all_to_all | solution.py:135
  52.5 69.1 %all-to-all-start = ((bf16[16,256,256]{2,1,0:T(8,128)(2,1)}), bf16[16,256,256]{2,1,0:T(8,128)(2,1)S(1)}, u32[]{:S(2)}, u32[]{:S(2)}) async-start(bf16[16,256,256]{2,1,0:T(8,128)(2,1)} %bitcast.44), calls=%async_computation | async-start | bytes 4194304 | tf_op jit(solution)/shard_map/all_to_all | solution.py:135
  121.6 18.8 %copy-start = (bf16[16,256,256]{2,1,0:T(8,128)(2,1)}, bf16[16,256,256]{2,1,0:T(8,128)(2,1)S(1)}, u32[]{:S(2)}) copy-start(bf16[16,256,256]{2,1,0:T(8,128)(2,1)S(1)} %all-to-all-done) | copy-start | bytes 6291460
  232.7 10.4 copy-start.1
  232.7 816.2 %all-to-all-start.4 = ((bf16[32,128,256]{2,1,0:T(8,128)(2,1)}), bf16[32,128,256]{2,1,0:T(8,128)(2,1)S(1)}, u32[]{:S(2)}, u32[]{:S(2)}) async-start(bf16[32,128,256]{2,1,0:T(8,128)(2,1)} %bitcast.43), calls=%async_computation.4 | async-start | bytes 4194304 | tf_op jit(solution)/shard_map/all_to_all | solution.py:135
Sparse Core Ops, SparseCore 0:
  9.7 105.2 all-gather.2

commit v2 on v1

--- a/solution.py
+++ b/solution.py
@@ -30,7 +30,7 @@
     return acc
 
 
-def relation_kernel(block, chunk, sub, t_rows, s_rows, t_all, s_all, kl_ref, grad_ref, u_scr, v_scr, g_scr):
+def relation_kernel(block, chunk, sub, t_rows, s_rows, t_all, s_all, kl_ref, grad_ref, u_scr, v_scr, g_scr, kl_scr):
     step = pl.program_id(0)
     seq = t_all.shape[0]
     student_scale = s_all.shape[1] ** -0.5
@@ -74,12 +74,13 @@
         log_t = jnp.log2(lt)
         log_s = jnp.log2(ls)
         kl = (a / lt - log_t + log_s) * LN2
-        kl_ref[rows, :] = jnp.broadcast_to(kl, (sub, LANES))
+        kl_scr[rows, :] = jnp.broadcast_to(kl, (sub, LANES))
         z_t = jnp.broadcast_to(mt[rows] + log_t, (sub, LANES))
         z_s = jnp.broadcast_to(ms[rows] + log_s, (sub, LANES))
         for c in range(0, seq, LANES):
             g = jnp.exp2(v_scr[rows, c : c + LANES] - z_s) - jnp.exp2(u_scr[rows, c : c + LANES] - z_t)
             g_scr[rows, c : c + LANES] = g.astype(jnp.bfloat16)
+    kl_ref[pl.ds(step, 1), :] = jnp.transpose(kl_scr[...])[:1]
     acc = jnp.zeros((block, s_all.shape[1]), jnp.float32)
     for c in range(0, seq, chunk):
         g = g_scr[:, c : c + chunk]
@@ -115,17 +116,18 @@
             pl.BlockSpec((seq, s_width), whole),
         ],
         out_specs=[
-            pl.BlockSpec((block, LANES), lambda i: (i, 0)),
+            pl.BlockSpec((steps, block), whole),
             pl.BlockSpec((seq, s_width), whole),
         ],
         out_shape=[
-            jax.ShapeDtypeStruct((rows, LANES), jnp.float32),
+            jax.ShapeDtypeStruct((steps, block), jnp.float32),
             jax.ShapeDtypeStruct((seq, s_width), jnp.float32),
         ],
         scratch_shapes=[
             pltpu.VMEM((block, seq), jnp.float32),
             pltpu.VMEM((block, seq), jnp.float32),
             pltpu.VMEM((block, seq), jnp.bfloat16),
+            pltpu.VMEM((block, LANES), jnp.float32),
         ],
         compiler_params=pltpu.CompilerParams(vmem_limit_bytes=56 << 20),
     )(t_all, s_all, t_all, s_all)
@@ -133,6 +135,21 @@
 
 def exchange(chunks, axes):
     return lax.all_to_all(chunks, axes, split_axis=0, concat_axis=0, tiled=True)
+
+
+def owned_rows(kl):
+    mine = lax.axis_index("xh")
+
+    def moved(flip):
+        pairs = []
+        for source in range(32):
+            xh, xl, zh, zl, yh = ((source >> k) & 1 for k in (4, 3, 2, 1, 0))
+            pairs.append((source, zl * 16 + yh * 8 + xl * 4 + zh * 2 + (xh ^ flip)))
+        return lax.ppermute(jnp.where(mine == flip, kl[0], kl[1])[None], DP, pairs)
+
+    same, other = moved(0), moved(1)
+    first = lax.axis_index("yh") == 0
+    return jnp.concatenate([jnp.where(first, same, other), jnp.where(first, other, same)], axis=1)
 
 
 def local(teacher_query, student_hidden, query_weight):
@@ -165,15 +182,12 @@
         hidden, query_grad, (((1,), (0,)), ((), ())), preferred_element_type=jnp.float32
     )
     sent = exchange(partial.astype(jnp.bfloat16).reshape(32, depth, width), DP)
-    weight_grad = jnp.sum(sent.reshape(8, 4, depth, width).astype(jnp.float32), axis=0)
-    weight_grad = jnp.moveaxis(weight_grad, 0, 1).reshape(depth, columns)
-    all_kl = lax.all_gather(kl[:, 0], DP, axis=0).reshape(2, 2, 2, 4, 2, SEQ // 4)
-    dp = lax.axis_index(DP)
-    head, quarter = dp // 4, dp % 4
-    row = lax.dynamic_slice(
-        all_kl, (0, head % 2, quarter // 2, head // 2, quarter % 2, 0), (2, 1, 1, 1, 1, SEQ // 4)
-    )
-    return row.reshape(1, NSEQ * (SEQ // 4)), weight_grad
+    sent = sent.reshape(8, 4, depth, width)
+    total = sent[0].astype(jnp.float32)
+    for i in range(1, 8):
+        total = total + sent[i].astype(jnp.float32)
+    weight_grad = jnp.moveaxis(total, 0, 1).reshape(depth, columns)
+    return owned_rows(kl.reshape(2, SEQ // 4)), weight_grad
 
 
 def solution(mesh):

time: 1060 us -> 284 us (0.27)
  the two profiles are of different devices: /device:TPU:44 before, /device:TPU:8 now
where the time goes in v2:
time: 284 us; the launch traced here: 283 us
  waiting for transfers between devices  110 us (39%)
  Pallas kernels  53.2 us (19%)
  blocking collectives  50.9 us (18%)
  starting transfers between devices  30.9 us (11%)
  between operations  14.2 us (5%)
  matrix products  12.1 us (4%)
  local copies, waits for them, and re-layouts  10.3 us (4%)
    all_gather x1, waiting for transfers between devices, local(): hidden = lax.all_gather(student_hidden, TP + COLUMN, axis=0, tiled=True)  53.5 us
    pallas_call x1, Pallas kernels, relation(): pl.pallas_call(functools.partial(relation_kernel, block, chunk, sub), gri...  53.2 us
    all_to_all x2, blocking collectives, exchange(): return lax.all_to_all(chunks, axes, split_axis=0, concat_axis=0, tiled=True)  50.9 us
    all_to_all x3, waiting for transfers between devices, exchange(): return lax.all_to_all(chunks, axes, split_axis=0, concat_axis=0, tiled=True)  36.2 us
    all_to_all x3, starting transfers between devices, exchange(): return lax.all_to_all(chunks, axes, split_axis=0, concat_axis=0, tiled=True)  24.2 us
    ppermute x2, waiting for transfers between devices, moved(): return lax.ppermute(jnp.where(mine == flip, kl[0], kl[1])[None], DP, pairs)  20.1 us
    ppermute x2, starting transfers between devices, moved(): return lax.ppermute(jnp.where(mine == flip, kl[0], kl[1])[None], DP, pairs)  6.74 us
    dot_general x1, matrix products, local(): lax.dot_general(hidden, weight, (((0, 2), (0, 1)), ((), ())), preferred_e...  6.34 us
  transfers between devices with their start and end apart: 6, of which 4 were waited for; matrix products, arithmetic and copies ran while one was open for 4% of the time, Pallas kernels for 0%

profile of v2, /device:TPU:8, one launch (start us, length us, event | category | flops | bytes accessed | tf_op | source)
XLA Modules:
  0.0 283.1 jit_solution(1618281277069244084)
XLA Ops:
  7.2 0.7 all-gather.2.cloned.1.call-update
  7.9 1.1 reshape.117
  9.1 1.6 broadcast_in_dim.7
  10.7 10.2 %all-to-all-start.1 = ((bf16[32,128,256]{2,1,0:T(8,128)(2,1)}), bf16[32,128,256]{2,1,0:T(8,128)(2,1)}, u32[]{:S(2)}, u32[]{:S(2)}) async-start(bf16[32,128,256]{2,1,0:T(8,128)(2,1)} %bitcast.5), calls=%async_computation.1 | async-start | bytes 4194304 | tf_op jit(solution)/shard_map/all_to_all | solution.py:137
  20.8 0.8 reshape.113
  21.8 31.4 %all-to-all-done.1 = bf16[32,128,256]{2,1,0:T(8,128)(2,1)} async-done(((bf16[32,128,256]{2,1,0:T(8,128)(2,1)}), bf16[32,128,256]{2,1,0:T(8,128)(2,1)}, u32[]{:S(2)}, u32[]{:S(2)}) %all-to-all-start.1) | async-done | bytes 2097184 | tf_op jit(solution)/shard_map/all_to_all | solution.py:137
  53.3 1.5 broadcast_in_dim.6
  54.8 5.5 %all-to-all-start = ((bf16[16,256,256]{2,1,0:T(8,128)(2,1)}), bf16[16,256,256]{2,1,0:T(8,128)(2,1)S(1)}, u32[]{:S(2)}, u32[]{:S(2)}) async-start(bf16[16,256,256]{2,1,0:T(8,128)(2,1)} %bitcast.48), calls=%async_computation | async-start | bytes 4194304 | tf_op jit(solution)/shard_map/all_to_all | solution.py:137
  60.4 53.5 %all-gather.2.cloned.1.call-done = bf16[4096,1024]{1,0:T(8,128)(2,1)} async-done(((bf16[256,1024]{1,0:T(8,128)(2,1)}), bf16[4096,1024]{1,0:T(8,128)(2,1)}) %all-gather.2.cloned.1.call-update) | async-done | bytes 8388624 | tf_op jit(solution)/shard_map/all_gather | solution.py:161
  113.8 6.3 %fusion = bf16[1024,256]{0,1:T(8,128)(2,1)S(1)} fusion(bf16[4,1024,1024]{2,1,0:T(8,128)(2,1)} %bitcast.59, bf16[4,1024,256]{2,1,0:T(8,128)(2,1)} %bitcast.6), kind=kOutput, calls=%fused_computation.2 | convolution fusion | flops 2147745792 | bytes 11010048 | tf_op jit(solution)/shard_map/dot_general | solution.py:170
  120.6 19.5 %all_to_all.25 = bf16[4,1024,128]{2,1,0:T(8,128)(2,1)} all-to-all(bf16[4,1024,128]{2,1,0:T(8,128)(2,1)S(1)} %bitcast.50), channel_id=1, replica_groups=mesh['yl'=2,'core'=2,'xh'=2,'xl'=2,'zh'=2,'zl'=2,'yh'=2] {'xl','zh'}, dimensions={0} | all-to-all | bytes 2097152 | tf_op jit(solution)/shard_map/all_to_all | solution.py:137
  140.1 53.2 %shard_map.50 = (f32[8,256]{1,0:T(8,128)}, f32[4096,128]{1,0:T(8,128)}) custom-call(bf16[4096,256]{1,0:T(8,128)(2,1)} %bitcast.43, bf16[4096,128]{1,0:T(8,128)(2,1)} %bitcast.45, bf16[4096,256]{1,0:T(8,128)(2,1)} %bitcast.44, bf16[4096,128]{1,0:T(8,128)(2,1)} %bitcast.46), custom_call_target="tpu_custom_call" | custom-call | tf_op jit(solution)/shard_map/pallas_call | solution.py:109
  193.3 31.4 %all_to_all.26 = f32[4,1024,128]{2,1,0:T(8,128)S(1)} all-to-all(f32[4,1024,128]{2,1,0:T(8,128)} %bitcast.52), channel_id=1, replica_groups=mesh['yl'=2,'core'=2,'xh'=2,'xl'=2,'zh'=2,'zl'=2,'yh'=2] {'xl','zh'}, dimensions={0} | all-to-all | bytes 4194304 | tf_op jit(solution)/shard_map/all_to_all | solution.py:137
  224.8 0.3 copy.27
  225.2 0.3 copy.28
  225.7 5.7 %convert_bitcast_fusion = bf16[4,1024,256]{1,2,0:T(8,128)(2,1)S(1)} fusion(bf16[1024,256,1]{0,1,2:T(8,128)(2,1)S(1)} %bitcast.55, bf16[4,1024,1024]{2,1,0:T(8,128)(2,1)} %bitcast.60), kind=kOutput, calls=%fused_computation | convolution fusion | flops 2148532224 | bytes 11010048 | tf_op jit(solution)/shard_map/dot_general | solution.py:181
  231.4 2.6 copy.23
  234.0 8.5 %all-to-all-start.4 = ((bf16[32,128,256]{2,1,0:T(8,128)(2,1)}), bf16[32,128,256]{2,1,0:T(8,128)(2,1)S(1)}, u32[]{:S(2)}, u32[]{:S(2)}) async-start(bf16[32,128,256]{2,1,0:T(8,128)(2,1)} %bitcast.47), calls=%async_computation.4 | async-start | bytes 4194304 | tf_op jit(solution)/shard_map/all_to_all | solution.py:137
  242.5 0.7 collective-permute-start
  243.2 6.1 %collective-permute-start.1 = (f32[1,1024]{1,0:T(1,128)S(1)}, f32[1,1024]{1,0:T(1,128)S(1)}, u32[]{:S(2)}, u32[]{:S(2)}) collective-permute-start(f32[1,1024]{1,0:T(1,128)S(1)} %bitcast.58), channel_id=1, source_target_pairs={{0,1},{1,9},{2,17},{3,25},{4,3},{5,11},{6,19},{7,27},{8,5},{9,13},... | collective-permute-start | bytes 12296 | tf_op jit(solution)/shard_map/ppermute | solution.py:148
  249.3 20.1 %collective-permute-done.1 = f32[1,1024]{1,0:T(1,128)S(1)} collective-permute-done((f32[1,1024]{1,0:T(1,128)S(1)}, f32[1,1024]{1,0:T(1,128)S(1)}, u32[]{:S(2)}, u32[]{:S(2)}) %collective-permute-start.1) | collective-permute-done | bytes 4128 | tf_op jit(solution)/shard_map/ppermute | solution.py:148
  269.4 0.6 pad_maximum_fusion
  270.0 4.7 %all-to-all-done.4 = bf16[32,128,256]{2,1,0:T(8,128)(2,1)S(1)} async-done(((bf16[32,128,256]{2,1,0:T(8,128)(2,1)}), bf16[32,128,256]{2,1,0:T(8,128)(2,1)S(1)}, u32[]{:S(2)}, u32[]{:S(2)}) %all-to-all-start.4) | async-done | bytes 2097184 | tf_op jit(solution)/shard_map/all_to_all | solution.py:137
  275.2 1.0 copy.25
  (21 shorter events, 1.5 us)
Async XLA Ops:
  7.2 106.7 %all-gather.2.cloned.1.call-start = ((), (), s32[]{:S(2)}) async-start(), calls=%async_computation.5 | async-start | bytes 8912896 | tf_op jit(solution)/shard_map/all_gather | solution.py:161
  10.7 10.2 %copy-start.1 = (bf16[256,2048]{1,0:T(8,128)(2,1)S(1)}, bf16[256,2048]{1,0:T(8,128)(2,1)}, u32[]{:S(2)}) copy-start(bf16[256,2048]{1,0:T(8,128)(2,1)} %param.3) | copy-start | bytes 3145732
  10.7 42.6 %all-to-all-start.1 = ((bf16[32,128,256]{2,1,0:T(8,128)(2,1)}), bf16[32,128,256]{2,1,0:T(8,128)(2,1)}, u32[]{:S(2)}, u32[]{:S(2)}) async-start(bf16[32,128,256]{2,1,0:T(8,128)(2,1)} %bitcast.5), calls=%async_computation.1 | async-start | bytes 4194304 | tf_op jit(solution)/shard_map/all_to_all | solution.py:137
  54.8 65.6 %all-to-all-start = ((bf16[16,256,256]{2,1,0:T(8,128)(2,1)}), bf16[16,256,256]{2,1,0:T(8,128)(2,1)S(1)}, u32[]{:S(2)}, u32[]{:S(2)}) async-start(bf16[16,256,256]{2,1,0:T(8,128)(2,1)} %bitcast.48), calls=%async_computation | async-start | bytes 4194304 | tf_op jit(solution)/shard_map/all_to_all | solution.py:137
  120.5 19.6 %copy-start = (bf16[16,256,256]{2,1,0:T(8,128)(2,1)}, bf16[16,256,256]{2,1,0:T(8,128)(2,1)S(1)}, u32[]{:S(2)}) copy-start(bf16[16,256,256]{2,1,0:T(8,128)(2,1)S(1)} %all-to-all-done) | copy-start | bytes 6291460
  234.0 8.5 %copy-start.2 = (f32[8,256]{1,0:T(8,128)S(1)}, f32[8,256]{1,0:T(8,128)}, u32[]{:S(2)}) copy-start(f32[8,256]{1,0:T(8,128)} %get-tuple-element.4) | copy-start | bytes 24580
  234.0 40.7 %all-to-all-start.4 = ((bf16[32,128,256]{2,1,0:T(8,128)(2,1)}), bf16[32,128,256]{2,1,0:T(8,128)(2,1)S(1)}, u32[]{:S(2)}, u32[]{:S(2)}) async-start(bf16[32,128,256]{2,1,0:T(8,128)(2,1)} %bitcast.47), calls=%async_computation.4 | async-start | bytes 4194304 | tf_op jit(solution)/shard_map/all_to_all | solution.py:137
  242.5 6.8 %collective-permute-start = (f32[1,1024]{1,0:T(1,128)S(1)}, f32[1,1024]{1,0:T(1,128)S(1)}, u32[]{:S(2)}, u32[]{:S(2)}) collective-permute-start(f32[1,1024]{1,0:T(1,128)S(1)} %bitcast.57), channel_id=1, source_target_pairs={{0,0},{1,8},{2,16},{3,24},{4,2},{5,10},{6,18},{7,26},{8,4},{9,12},... | collective-permute-start | bytes 12296 | tf_op jit(solution)/shard_map/ppermute | solution.py:148
  243.2 26.2 %collective-permute-start.1 = (f32[1,1024]{1,0:T(1,128)S(1)}, f32[1,1024]{1,0:T(1,128)S(1)}, u32[]{:S(2)}, u32[]{:S(2)}) collective-permute-start(f32[1,1024]{1,0:T(1,128)S(1)} %bitcast.58), channel_id=1, source_target_pairs={{0,1},{1,9},{2,17},{3,25},{4,3},{5,11},{6,19},{7,27},{8,5},{9,13},... | collective-permute-start | bytes 12296 | tf_op jit(solution)/shard_map/ppermute | solution.py:148
Sparse Core Ops, SparseCore 0:
  9.7 104.1 all-gather.1

commit v3 on v2

v3 whole, which is shorter than its diff:
```python
import functools

import jax
import jax.numpy as jnp
from jax import lax
from jax.experimental import pallas as pl
from jax.experimental.pallas import tpu as pltpu
from jax.sharding import Mesh, PartitionSpec as P

LOG2E = 1.4426950408889634
LN2 = 0.6931471805599453
LANES = 128

TP = ("yl", "core")
DP = ("xh", "xl", "zh", "zl", "yh")
BLOCK = ("zh", "yh")
SPREAD = ("zh", "yh", "xl", "zl")
SWAP = [(0, 1), (1, 0)]

CONTRACT_LAST = (((1,), (1,)), ((), ()))
CONTRACT_FIRST = (((0,), (0,)), ((), ()))
WHOLE = pl.BlockSpec(memory_space=pltpu.VMEM)


def swap(value, axis):
    return lax.ppermute(value, axis, SWAP)


def exchange(chunks, axes):
    return lax.all_to_all(chunks, axes, split_axis=0, concat_axis=0, tiled=True)


RUNS = ((0, 96, (0, 1, 2)), (96, 176, (1, 2, 0)), (176, 256, (2, 0, 1)))
CUBE = ("xl", "yl", "zl")


def gather_cube(share):
    held = [share[None, first:last] for first, last, _ in RUNS]
    far = held
    for stage in range(3):
        far = [swap(piece, CUBE[order[stage]]) for piece, (_, _, order) in zip(held, RUNS)]
        if stage < 2:
            held = [jnp.concatenate(both) for both in zip(held, far)]
    return [piece for both in zip(held, far) for piece in both]


def run_piece(refs, run, hops, first, last):
    order = RUNS[run][2]
    place = sum(hops[order[k]] << k for k in range(3))
    return refs[2 * run + place // 4][place % 4, first:last, :]


def hidden_tile(refs, dy, rel):
    rows = []
    for dx in range(2):
        for dz in range(2):
            hops = (dx, dy, dz)
            if rel == 0:
                rows += [run_piece(refs, 0, hops, 0, 96), run_piece(refs, 1, hops, 0, 32)]
            else:
                rows += [run_piece(refs, 1, hops, 32, 80), run_piece(refs, 2, hops, 0, 80)]
    return jnp.concatenate(rows, axis=0)


def token_place(dx, dz):
    return (lax.axis_index("xl") ^ dx) * 2 + (lax.axis_index("zl") ^ dz)


def project_kernel(*refs):
    hidden, (w_own, w_other, out) = refs[:6], refs[6:]
    core = lax.axis_index("core")
    features = w_own.shape[0] // 4
    parts = [None, None]
    for dy in range(2):
        for rel in range(2):
            tile = hidden_tile(hidden, dy, rel)
            block = (lax.axis_index("yl") ^ dy) * 2 + (core ^ rel)
            depth = pl.ds(pl.multiple_of(block * features, features), features)
            for i, weight in enumerate((w_own, w_other)):
                term = jnp.dot(tile, weight[depth, :], preferred_element_type=jnp.float32)
                parts[i] = term if parts[i] is None else parts[i] + term
    for i in range(2):
        value = parts[i].astype(jnp.bfloat16)
        for j in range(2):
            for dx in range(2):
                for dz in range(2):
                    at = (dx * 2 + dz) * 128
                    rows = pl.ds(pl.multiple_of(token_place(dx, dz) * 128, 128), 128)
                    out[(core ^ i) * 2 + j, rows, :] = value[at : at + 128, j * 128 : (j + 1) * 128]


def project(hidden, w_own, w_other):
    return pl.pallas_call(
        project_kernel,
        in_specs=[WHOLE] * 8,
        out_specs=WHOLE,
        out_shape=jax.ShapeDtypeStruct((4, 512, 128), jnp.bfloat16),
        compiler_params=pltpu.CompilerParams(vmem_limit_bytes=48 << 20),
    )(*hidden, w_own, w_other)


def weight_grad_kernel(*refs):
    own, other, (q_own, q_other, out) = refs[:6], refs[6:12], refs[12:]
    core = lax.axis_index("core")

    def in_place(ref):
        rows = []
        for dx in range(2):
            for dz in range(2):
                at = pl.ds(pl.multiple_of(token_place(dx, dz) * 128, 128), 128)
                rows.append(jnp.concatenate([ref[0, at, :], ref[1, at, :]], axis=1))
        return rows

    grad = jnp.concatenate(in_place(q_own) + in_place(q_other), axis=0)
    for dy in range(2):
        for rel in range(2):
            tile = jnp.concatenate([hidden_tile(own, dy, rel), hidden_tile(other, dy, 1 - rel)], axis=0)
            block = (lax.axis_index("yl") ^ dy) * 2 + (core ^ rel)
            value = lax.dot_general(tile, grad, CONTRACT_FIRST, preferred_element_type=jnp.float32)
            count = value.shape[0] // 128
            out[pl.ds(block * count, count)] = value.astype(jnp.bfloat16).reshape(count, 128, value.shape[1])


def weight_grad_part(own, other, q_own, q_other):
    return pl.pallas_call(
        weight_grad_kernel,
        in_specs=[WHOLE] * 14,
        out_specs=WHOLE,
        out_shape=jax.ShapeDtypeStruct((32, 128, 256), jnp.bfloat16),
        compiler_params=pltpu.CompilerParams(vmem_limit_bytes=48 << 20),
    )(*own, *other, q_own, q_other)


def lane_fold(x, op):
    acc = x[:, :LANES]
    for j in range(1, x.shape[1] // LANES):
        acc = op(acc, x[:, j * LANES : (j + 1) * LANES])
    return acc


def relation_kernel(
    block, chunk, sub, t_own, s_own, t_other, s_other, kl_ref, own_ref, other_ref, u_scr, v_scr, g_scr, kl_scr
):
    step = pl.program_id(0)
    half = t_own.shape[0]
    width = s_own.shape[1]
    student_scale = width**-0.5
    t_mul = LOG2E * t_own.shape[1] ** -0.5
    s_mul = LOG2E * student_scale

    @pl.when(step == 0)
    def _():
        own_ref[...] = jnp.zeros_like(own_ref)
        other_ref[...] = jnp.zeros_like(other_ref)

    mine = pl.ds(pl.multiple_of(step * block, block), block)
    tr = t_own[mine, :]
    sr = s_own[mine, :]
    keys = [(t, s, g, c) for t, s, g in ((t_own, s_own, own_ref), (t_other, s_other, other_ref)) for c in range(0, half, chunk)]
    mt = ms = None
    for i, (t_keys, s_keys, _, c) in enumerate(keys):
        at = slice(i * chunk, (i + 1) * chunk)
        u = t_mul * lax.dot_general(tr, t_keys[c : c + chunk, :], CONTRACT_LAST, preferred_element_type=jnp.float32)
        u_scr[:, at] = u
        fold = lane_fold(u, jnp.maximum)
        mt = fold if mt is None else jnp.maximum(mt, fold)
        v = s_mul * lax.dot_general(sr, s_keys[c : c + chunk, :], CONTRACT_LAST, preferred_element_type=jnp.float32)
        v_scr[:, at] = v
        fold = lane_fold(v, jnp.maximum)
        ms = fold if ms is None else jnp.maximum(ms, fold)
    mt = jnp.max(mt, axis=1, keepdims=True)
    ms = jnp.max(ms, axis=1, keepdims=True)
    for r in range(0, block, sub):
        rows = slice(r, r + sub)
        m_t = jnp.broadcast_to(mt[rows], (sub, LANES))
        m_s = jnp.broadcast_to(ms[rows], (sub, LANES))
        zero = jnp.zeros((sub, LANES), jnp.float32)
        lt, ls, a = zero, zero, zero
        for c in range(0, 2 * half, LANES):
            x = u_scr[rows, c : c + LANES] - m_t
            y = v_scr[rows, c : c + LANES] - m_s
            et = jnp.exp2(x)
            lt = lt + et
            ls = ls + jnp.exp2(y)
            a = a + et * (x - y)
        lt = jnp.sum(lt, axis=1, keepdims=True)
        ls = jnp.sum(ls, axis=1, keepdims=True)
        a = jnp.sum(a, axis=1, keepdims=True)
        log_t = jnp.log2(lt)
        log_s = jnp.log2(ls)
        kl = (a / lt - log_t + log_s) * LN2
        kl_scr[rows, :] = jnp.broadcast_to(kl, (sub, LANES))
        z_t = jnp.broadcast_to(mt[rows] + log_t, (sub, LANES))
        z_s = jnp.broadcast_to(ms[rows] + log_s, (sub, LANES))
        for c in range(0, 2 * half, LANES):
            g = jnp.exp2(v_scr[rows, c : c + LANES] - z_s) - jnp.exp2(u_scr[rows, c : c + LANES] - z_t)
            g_scr[rows, c : c + LANES] = g.astype(jnp.bfloat16)
    kl_ref[pl.ds(step, 1), :] = jnp.transpose(kl_scr[...])[:1]
    acc = jnp.zeros((block, width), jnp.float32)
    for i, (_, s_keys, g_ref, c) in enumerate(keys):
        g = g_scr[:, i * chunk : (i + 1) * chunk]
        acc = acc + jnp.dot(g, s_keys[c : c + chunk, :], preferred_element_type=jnp.float32)
        g_ref[c : c + chunk, :] += lax.dot_general(g, sr, CONTRACT_FIRST, preferred_element_type=jnp.float32)
    own_ref[mine, :] += acc

    @pl.when(step == pl.num_programs(0) - 1)
    def _():
        own_ref[...] = own_ref[...] * student_scale
        other_ref[...] = other_ref[...] * student_scale


def relation(t_own, s_own, t_other, s_other, block=256, chunk=512, sub=32):
    half, t_width = t_own.shape
    s_width = s_own.shape[1]
    steps = half // block

    def whole(*shape):
        return pl.BlockSpec(shape, lambda i: (0, 0))

    return pl.pallas_call(
        functools.partial(relation_kernel, block, chunk, sub),
        grid=(steps,),
        in_specs=[whole(half, t_width), whole(half, s_width)] * 2,
        out_specs=[whole(steps, block), whole(half, s_width), whole(half, s_width)],
        out_shape=[
            jax.ShapeDtypeStruct((steps, block), jnp.float32),
            jax.ShapeDtypeStruct((half, s_width), jnp.float32),
            jax.ShapeDtypeStruct((half, s_width), jnp.float32),
        ],
        scratch_shapes=[
            pltpu.VMEM((block, 2 * half), jnp.float32),
            pltpu.VMEM((block, 2 * half), jnp.float32),
            pltpu.VMEM((block, 2 * half), jnp.bfloat16),
            pltpu.VMEM((block, LANES), jnp.float32),
        ],
        compiler_params=pltpu.CompilerParams(vmem_limit_bytes=50 << 20),
    )(t_own, s_own, t_other, s_other)


def owned_rows(kl):
    kl = kl.reshape(2, 2, 2, 2, LANES).transpose(2, 0, 3, 1, 4).reshape(4, 4, LANES)
    source = lax.axis_index("xh") * 2 + lax.axis_index("core")
    got = []
    for turn in range(4):
        pairs = []
        for c in range(2):
            for dp in range(32):
                xh, xl, zh, zl, yh = ((dp >> k) & 1 for k in (4, 3, 2, 1, 0))
                quarter = turn ^ (xh * 2 + c)
                pairs.append((c * 32 + dp, zh * 32 + xl * 16 + zl * 8 + yh * 4 + quarter))
        sent = lax.dynamic_index_in_dim(kl, turn ^ source, 0, keepdims=False)
        got.append(lax.ppermute(sent, ("core",) + DP, pairs))
    got = jnp.stack(got)
    quarter = lax.axis_index(DP) % 4
    rows = [lax.dynamic_index_in_dim(got, f ^ quarter, 0, keepdims=False) for f in range(4)]
    rows = jnp.stack(rows).reshape(2, 2, 4, LANES)
    return rows.transpose(0, 2, 1, 3).reshape(1, 2 * 4 * 2 * LANES)


def local(teacher_query, student_hidden, query_weight):
    rows = teacher_query.shape[0]
    depth, columns = query_weight.shape
    t_width = teacher_query.shape[1] // 8
    width = columns // 4
    core = lax.axis_index("core")
    low = core == 0

    def token_halves(value):
        first, second = value[: rows // 2], value[rows // 2 :]
        return jnp.where(low, first, second), swap(jnp.where(low, second, first), "core")

    hidden = gather_cube(jnp.concatenate(token_halves(student_hidden)))
    parts = jnp.moveaxis(query_weight.reshape(depth, 2, 1, 2, 1, width), 0, 4)
    w_own = exchange(jnp.broadcast_to(parts, (2, 2, 2, 2, 2, depth, width)).reshape(32, depth, width), DP)
    w_own = w_own.reshape(32 * depth, width)
    w_other = swap(w_own, "core")
    student = exchange(project(hidden, w_own, w_other), BLOCK).reshape(2048, -1)
    student_other = swap(student, "core")
    t_own, t_other = token_halves(teacher_query)
    heads = jnp.stack([jnp.where(low, t_own, t_other), jnp.where(low, t_other, t_own)])
    heads = heads.reshape(2, rows // 2, 2, 2, 2, t_width).transpose(0, 4, 2, 3, 1, 5)
    teacher = exchange(heads.reshape(16, rows // 2, t_width), SPREAD).reshape(2048, t_width)
    teacher_other = swap(teacher, "core")

    kl, grad, grad_other = relation(teacher, student, teacher_other, student_other)
    hidden_other = [swap(piece, "core") for piece in hidden]
    query_grad = (grad + swap(grad_other, "core")).astype(jnp.bfloat16)
    query_grad = exchange(query_grad.reshape(4, 512, -1), BLOCK).reshape(2, 2, 512, -1)
    mine = jnp.where(low, query_grad[0], query_grad[1])
    theirs = swap(jnp.where(low, query_grad[1], query_grad[0]), "core")
    sent = exchange(weight_grad_part(hidden, hidden_other, mine, theirs), DP)
    kl_rows = owned_rows(kl)
    sent = sent.reshape(2, 2, 2, 2, 2, depth, width)
    total = None
    for xh in range(2):
        for zh in range(2):
            for yh in range(2):
                term = sent[xh, :, zh, :, yh].astype(jnp.float32)
                total = term if total is None else total + term
    return kl_rows, total.reshape(4, depth, width).transpose(1, 0, 2).reshape(depth, columns)


def solution(mesh):
    bits = Mesh(mesh.devices.reshape((2,) * 7), TP + DP)
    return jax.shard_map(
        local,
        mesh=bits,
        in_specs=(P(DP, TP), P(DP, TP), P(DP, TP)),
        out_specs=(P(TP + DP, None), P(DP, TP)),
        check_vma=False,
    )
```

time: 284 us -> 240 us (0.85)
  blocking collectives: 50.9 us -> 17.3 us
  starting transfers between devices: 30.9 us -> 54.4 us
  waiting for transfers between devices: 110 us -> 88.7 us
  between operations: 14.2 us -> 1.03 us
  matrix products: 12.1 us -> 0 us
  Pallas kernels: 53.2 us -> 62.6 us
  other arithmetic: 1.05 us -> 7.82 us
  local copies, waits for them, and re-layouts: 10.3 us -> 7.2 us
    all_gather x1 -> x0, waiting for transfers between devices: 53.5 us -> none  [local(): hidden = lax.all_gather(student_hidden, TP + COLUMN, axis=0, tiled=True)]
    all_to_all x2 -> x1, blocking collectives: 50.9 us -> 17.3 us  [exchange(): return lax.all_to_all(chunks, axes, split_axis=0, concat_axis=0, tiled=True)]
    ppermute x2 -> x26, waiting for transfers between devices: 20.1 us -> 47.3 us  [the longest x22 36.7 us: swap(): return lax.ppermute(value, axis, SWAP)]
    ppermute x2 -> x26, starting transfers between devices: 6.74 us -> 29.4 us  [the longest x4 16.3 us: owned_rows(): got.append(lax.ppermute(sent, ('core',) + DP, pairs))]
    dot_general x2 -> x0, matrix products: 12.1 us -> none  [the longest x1 6.34 us: local(): lax.dot_general(hidden, weight, (((0, 2), (0, 1)), ((), ())), preferred_e...]
    pallas_call x0 -> x2, Pallas kernels: none -> 11.5 us  [the longest x1 6.47 us: weight_grad_part(): pl.pallas_call(weight_grad_kernel, in_specs=[WHOLE] * 14, out_specs=WHOLE...]
    all_to_all x3 -> x4, waiting for transfers between devices: 36.2 us -> 41.4 us  [exchange(): return lax.all_to_all(chunks, axes, split_axis=0, concat_axis=0, tiled=True)]
    concatenate x1 -> x6, other arithmetic: 0.61 us -> 3.89 us  [gather_cube(): held = [jnp.concatenate(both) for both in zip(held, far)]]
  transfers between devices with their start and end apart: 6 -> 30, of which waited for: 4 -> 11; matrix products, arithmetic and copies ran while one was open for 4% -> 4% of each run, Pallas kernels for 0% -> 2%
where the time goes in v3:
time: 240 us; the launch traced here: 239 us
  waiting for transfers between devices  88.7 us (37%)
  Pallas kernels  62.6 us (26%)
  starting transfers between devices  54.4 us (23%)
  blocking collectives  17.3 us (7%)
  other arithmetic  7.82 us (3%)
  local copies, waits for them, and re-layouts  7.2 us (3%)
    pallas_call x1, Pallas kernels, relation(): pl.pallas_call(functools.partial(relation_kernel, block, chunk, sub), gri...  51 us
    all_to_all x4, waiting for transfers between devices, exchange(): return lax.all_to_all(chunks, axes, split_axis=0, concat_axis=0, tiled=True)  41.4 us
    ppermute x22, waiting for transfers between devices, swap(): return lax.ppermute(value, axis, SWAP)  36.7 us
    all_to_all x4, starting transfers between devices, exchange(): return lax.all_to_all(chunks, axes, split_axis=0, concat_axis=0, tiled=True)  25.1 us
    all_to_all x1, blocking collectives, exchange(): return lax.all_to_all(chunks, axes, split_axis=0, concat_axis=0, tiled=True)  17.3 us
    ppermute x4, starting transfers between devices, owned_rows(): got.append(lax.ppermute(sent, ('core',) + DP, pairs))  16.3 us
    ppermute x22, starting transfers between devices, swap(): return lax.ppermute(value, axis, SWAP)  13 us
    ppermute x4, waiting for transfers between devices, owned_rows(): got.append(lax.ppermute(sent, ('core',) + DP, pairs))  10.6 us
  transfers between devices with their start and end apart: 30, of which 11 were waited for; matrix products, arithmetic and copies ran while one was open for 4% of the time, Pallas kernels for 2%

profile of v3, /device:TPU:8, one launch (start us, length us, event | category | flops | bytes accessed | tf_op | source)
XLA Modules:
  0.0 239.1 jit_solution(1699532617819318095)
XLA Ops:
  3.4 10.2 %all-to-all-start.1 = ((bf16[32,128,256]{2,1,0:T(8,128)(2,1)}), bf16[32,128,256]{2,1,0:T(8,128)(2,1)}, u32[]{:S(2)}, u32[]{:S(2)}) async-start(bf16[32,128,256]{2,1,0:T(8,128)(2,1)} %bitcast.8), calls=%async_computation.1 | async-start | bytes 4194304 | tf_op jit(solution)/shard_map/all_to_all | solution.py:30
  14.4 1.8 collective-permute-start.1
  17.8 26.5 %all-to-all-done.1 = bf16[32,128,256]{2,1,0:T(8,128)(2,1)} async-done(((bf16[32,128,256]{2,1,0:T(8,128)(2,1)}), bf16[32,128,256]{2,1,0:T(8,128)(2,1)}, u32[]{:S(2)}, u32[]{:S(2)}) %all-to-all-start.1) | async-done | bytes 2097184 | tf_op jit(solution)/shard_map/all_to_all | solution.py:30
  47.9 1.9 collective-permute-start.9
  53.4 4.5 %all-to-all-start = ((bf16[16,128,256]{2,1,0:T(8,128)(2,1)}), bf16[16,128,256]{2,1,0:T(8,128)(2,1)}, u32[]{:S(2)}, u32[]{:S(2)}) async-start(bf16[16,128,256]{2,1,0:T(8,128)(2,1)} %bitcast.1), calls=%async_computation | async-start | bytes 2097152 | tf_op jit(solution)/shard_map/all_to_all | solution.py:30
  57.9 3.5 %collective-permute-done.5 = bf16[1,80,1024]{2,1,0:T(8,128)(2,1)S(1)} collective-permute-done((bf16[1,80,1024]{2,1,0:T(8,128)(2,1)S(1)}, bf16[1,80,1024]{2,1,0:T(8,128)(2,1)S(1)}, u32[]{:S(2)}, u32[]{:S(2)}) %collective-permute-start.5) | collective-permute-done | bytes 163872 | tf_op jit(solution)/shard_map/ppermute | solution.py:26
  63.2 1.6 collective-permute-start.3
  66.0 13.3 %collective-permute-done.6 = bf16[2,80,1024]{2,1,0:T(8,128)(2,1)S(1)} collective-permute-done((bf16[2,80,1024]{2,1,0:T(8,128)(2,1)S(1)}, bf16[2,80,1024]{2,1,0:T(8,128)(2,1)S(1)}, u32[]{:S(2)}, u32[]{:S(2)}) %collective-permute-start.6) | collective-permute-done | bytes 327712 | tf_op jit(solution)/shard_map/ppermute | solution.py:26
  80.8 14.4 %collective-permute-done.3.refs_1_ = bf16[4,96,1024]{2,1,0:T(8,128)(2,1)S(1)} collective-permute-done((bf16[4,96,1024]{2,1,0:T(8,128)(2,1)S(1)}, bf16[4,96,1024]{2,1,0:T(8,128)(2,1)S(1)}, u32[]{:S(2)}, u32[]{:S(2)}) %collective-permute-start.3) | collective-permute-done | bytes 786464 | tf_op jit(solution)/shard_map/ppermute | solution.py:26
  95.2 5.1 %shard_map.50 = bf16[4,512,128]{2,1,0:T(8,128)(2,1)S(1)} custom-call(bf16[4,96,1024]{2,1,0:T(8,128)(2,1)S(1)} %pad_maximum_fusion.refs_0_, bf16[4,96,1024]{2,1,0:T(8,128)(2,1)S(1)} %collective-permute-done.3.refs_1_, bf16[4,80,1024]{2,1,0:T(8,128)(2,1)S(1)} %pad_maximum_fusion.1.refs_2_, bf16[4,80,1024]{2,1,0:T(8,128)(2,1)} %collective-permute-done.7.refs_3_, ...), custom_call_target="tpu_custom_call" | custom-call | tf_op jit(solution)/shard_map/pallas_call | solution.py:93
  100.3 17.3 %all_to_all.25 = bf16[4,512,128]{2,1,0:T(8,128)(2,1)S(1)} all-to-all(bf16[4,512,128]{2,1,0:T(8,128)(2,1)S(1)} %shard_map.50), channel_id=1, replica_groups=mesh['yl'=2,'core'=2,'xh'=2,'xl'=2,'zh'=2,'zl'=2,'yh'=2] {'zh','yh'}, dimensions={0} | all-to-all | bytes 1048576 | tf_op jit(solution)/shard_map/all_to_all | solution.py:30
  117.6 1.9 collective-permute-done.13.s_other
  119.5 51.0 %shard_map.51 = (f32[8,256]{1,0:T(8,128)S(1)}, f32[2048,128]{1,0:T(8,128)S(1)}, f32[2048,128]{1,0:T(8,128)S(1)}) custom-call(bf16[2048,256]{1,0:T(8,128)(2,1)} %bitcast.2.t_own, bf16[2048,128]{1,0:T(8,128)(2,1)S(1)} %bitcast.42, bf16[2048,256]{1,0:T(8,128)(2,1)} %copy-done.5, bf16[2048,128]{1,0:T(8,128)(2,1)S(1)} %collective-permute-done.13.s_other), custom_call_target="tpu_custom_call" | custom-call | tf_op jit(solution)/shard_map/pallas_call | solution.py:220
  171.3 2.1 collective-permute-done.24
  174.3 4.1 %all-to-all-start.3 = ((bf16[4,512,128]{2,1,0:T(8,128)(2,1)}), bf16[4,512,128]{2,1,0:T(8,128)(2,1)}, u32[]{:S(2)}, u32[]{:S(2)}) async-start(bf16[4,512,128]{2,1,0:T(8,128)(2,1)} %bitcast.44), calls=%async_computation.3 | async-start | bytes 1048576 | tf_op jit(solution)/shard_map/all_to_all | solution.py:30
  179.5 9.4 %all-to-all-done.3 = bf16[4,512,128]{2,1,0:T(8,128)(2,1)} async-done(((bf16[4,512,128]{2,1,0:T(8,128)(2,1)}), bf16[4,512,128]{2,1,0:T(8,128)(2,1)}, u32[]{:S(2)}, u32[]{:S(2)}) %all-to-all-start.3) | async-done | bytes 524320 | tf_op jit(solution)/shard_map/all_to_all | solution.py:30
  191.7 6.5 %shard_map.52 = bf16[32,128,256]{2,1,0:T(8,128)(2,1)} custom-call(bf16[4,96,1024]{2,1,0:T(8,128)(2,1)} %copy-done, bf16[4,96,1024]{2,1,0:T(8,128)(2,1)} %copy-done.1, bf16[4,80,1024]{2,1,0:T(8,128)(2,1)S(1)} %pad_maximum_fusion.1.refs_2_, bf16[4,80,1024]{2,1,0:T(8,128)(2,1)} %collective-permute-done.7.refs_3_, ...), custom_call_target="tpu_custom_call" | custom-call | tf_op jit(solution)/shard_map/pallas_call | solution.py:125
  198.1 6.3 %all-to-all-start.4 = ((bf16[32,128,256]{2,1,0:T(8,128)(2,1)}), bf16[32,128,256]{2,1,0:T(8,128)(2,1)S(1)}, u32[]{:S(2)}, u32[]{:S(2)}) async-start(bf16[32,128,256]{2,1,0:T(8,128)(2,1)} %shard_map.52), calls=%async_computation.4 | async-start | bytes 4194304 | tf_op jit(solution)/shard_map/all_to_all | solution.py:30
  205.2 7.6 %collective-permute-start.15 = (f32[4,128]{1,0:T(4,128)S(1)}, f32[4,128]{1,0:T(4,128)S(1)}, u32[]{:S(2)}, u32[]{:S(2)}) collective-permute-start(f32[4,128]{1,0:T(4,128)S(1)} %get-tuple-element.23), channel_id=1, source_target_pairs={{0,1},{1,5},{2,9},{3,13},{4,33},{5,37},{6,41},{7,45},{8,17},{9,21}... | collective-permute-start | bytes 6152 | tf_op jit(solution)/shard_map/ppermute | solution.py:252
  212.7 3.3 %collective-permute-start.16 = (f32[4,128]{1,0:T(4,128)S(1)}, f32[4,128]{1,0:T(4,128)S(1)}, u32[]{:S(2)}, u32[]{:S(2)}) collective-permute-start(f32[4,128]{1,0:T(4,128)S(1)} %get-tuple-element.22), channel_id=1, source_target_pairs={{0,2},{1,6},{2,10},{3,14},{4,34},{5,38},{6,42},{7,46},{8,18},{9,22... | collective-permute-start | bytes 6152 | tf_op jit(solution)/shard_map/ppermute | solution.py:252
  216.0 4.8 %collective-permute-start.17 = (f32[4,128]{1,0:T(4,128)S(1)}, f32[4,128]{1,0:T(4,128)S(1)}, u32[]{:S(2)}, u32[]{:S(2)}) collective-permute-start(f32[4,128]{1,0:T(4,128)S(1)} %get-tuple-element.21), channel_id=1, source_target_pairs={{0,3},{1,7},{2,11},{3,15},{4,35},{5,39},{6,43},{7,47},{8,19},{9,23... | collective-permute-start | bytes 6152 | tf_op jit(solution)/shard_map/ppermute | solution.py:252
  220.8 4.5 %collective-permute-done.15 = f32[4,128]{1,0:T(4,128)S(1)} collective-permute-done((f32[4,128]{1,0:T(4,128)S(1)}, f32[4,128]{1,0:T(4,128)S(1)}, u32[]{:S(2)}, u32[]{:S(2)}) %collective-permute-start.15) | collective-permute-done | bytes 2080 | tf_op jit(solution)/shard_map/ppermute | solution.py:252
  225.3 6.1 %collective-permute-done.16 = f32[4,128]{1,0:T(4,128)S(1)} collective-permute-done((f32[4,128]{1,0:T(4,128)S(1)}, f32[4,128]{1,0:T(4,128)S(1)}, u32[]{:S(2)}, u32[]{:S(2)}) %collective-permute-start.16) | collective-permute-done | bytes 2080 | tf_op jit(solution)/shard_map/ppermute | solution.py:252
  232.1 5.5 %all-to-all-done.4 = bf16[32,128,256]{2,1,0:T(8,128)(2,1)S(1)} async-done(((bf16[32,128,256]{2,1,0:T(8,128)(2,1)}), bf16[32,128,256]{2,1,0:T(8,128)(2,1)S(1)}, u32[]{:S(2)}, u32[]{:S(2)}) %all-to-all-start.4) | async-done | bytes 2097184 | tf_op jit(solution)/shard_map/all_to_all | solution.py:30
  (96 shorter events, 25.0 us)
Async XLA Ops:
  3.4 40.8 %all-to-all-start.1 = ((bf16[32,128,256]{2,1,0:T(8,128)(2,1)}), bf16[32,128,256]{2,1,0:T(8,128)(2,1)}, u32[]{:S(2)}, u32[]{:S(2)}) async-start(bf16[32,128,256]{2,1,0:T(8,128)(2,1)} %bitcast.8), calls=%async_computation.1 | async-start | bytes 4194304 | tf_op jit(solution)/shard_map/all_to_all | solution.py:30
  13.8 36.0 %collective-permute-start = (bf16[128,2048]{1,0:T(8,128)(2,1)S(1)}, bf16[128,2048]{1,0:T(8,128)(2,1)S(1)}, u32[]{:S(2)}, u32[]{:S(2)}) collective-permute-start(bf16[128,2048]{1,0:T(8,128)(2,1)S(1)} %broadcast_select_fusion.2), channel_id=1, source_target_pairs={{0,32},{32,0},{1,33},{33,1},{2,34},{34,2},{3,35},{35,3},{4,36},{36... | collective-permute-start | bytes 1572872 | tf_op jit(solution)/shard_map/ppermute | solution.py:26
  14.4 29.9 %collective-permute-start.1 = (bf16[1,96,1024]{2,1,0:T(8,128)(2,1)S(1)}, bf16[1,96,1024]{2,1,0:T(8,128)(2,1)S(1)}, u32[]{:S(2)}, u32[]{:S(2)}) collective-permute-start(bf16[1,96,1024]{2,1,0:T(8,128)(2,1)S(1)} %slice_bitcast_fusion), channel_id=1, source_target_pairs={{0,8},{8,0},{1,9},{9,1},{2,10},{10,2},{3,11},{11,3},{4,12},{12,4},... | collective-permute-start | bytes 589832 | tf_op jit(solution)/shard_map/ppermute | solution.py:26
  16.2 30.9 %collective-permute-start.8 = (bf16[1,80,1024]{2,1,0:T(8,128)(2,1)S(1)}, bf16[1,80,1024]{2,1,0:T(8,128)(2,1)S(1)}, u32[]{:S(2)}, u32[]{:S(2)}) collective-permute-start(bf16[1,80,1024]{2,1,0:T(8,128)(2,1)S(1)} %get-tuple-element.14), channel_id=1, source_target_pairs={{0,2},{2,0},{1,3},{3,1},{4,6},{6,4},{5,7},{7,5},{8,10},{10,8},{9,1... | collective-permute-start | bytes 491528 | tf_op jit(solution)/shard_map/ppermute | solution.py:26
  44.2 50.9 %collective-permute-start.11 = (bf16[4096,256]{1,0:T(8,128)(2,1)}, bf16[4096,256]{1,0:T(8,128)(2,1)}, u32[]{:S(2)}, u32[]{:S(2)}) collective-permute-start(bf16[4096,256]{1,0:T(8,128)(2,1)} %bitcast.9.refs_6_), channel_id=1, source_target_pairs={{0,32},{32,0},{1,33},{33,1},{2,34},{34,2},{3,35},{35,3},{4,36},{36... | collective-permute-start | bytes 6291464 | tf_op jit(solution)/shard_map/ppermute | solution.py:26
  45.1 17.0 %collective-permute-start.2 = (bf16[2,96,1024]{2,1,0:T(8,128)(2,1)}, bf16[2,96,1024]{2,1,0:T(8,128)(2,1)}, u32[]{:S(2)}, u32[]{:S(2)}) collective-permute-start(bf16[2,96,1024]{2,1,0:T(8,128)(2,1)} %pad_maximum_fusion.3), channel_id=1, source_target_pairs={{0,64},{64,0},{1,65},{65,1},{2,66},{66,2},{3,67},{67,3},{4,68},{68... | collective-permute-start | bytes 1179656 | tf_op jit(solution)/shard_map/ppermute | solution.py:26
  45.6 15.8 %collective-permute-start.5 = (bf16[1,80,1024]{2,1,0:T(8,128)(2,1)S(1)}, bf16[1,80,1024]{2,1,0:T(8,128)(2,1)S(1)}, u32[]{:S(2)}, u32[]{:S(2)}) collective-permute-start(bf16[1,80,1024]{2,1,0:T(8,128)(2,1)S(1)} %get-tuple-element.15), channel_id=1, source_target_pairs={{0,64},{64,0},{1,65},{65,1},{2,66},{66,2},{3,67},{67,3},{4,68},{68... | collective-permute-start | bytes 491528 | tf_op jit(solution)/shard_map/ppermute | solution.py:26
  47.9 16.9 %collective-permute-start.9 = (bf16[2,80,1024]{2,1,0:T(8,128)(2,1)}, bf16[2,80,1024]{2,1,0:T(8,128)(2,1)}, u32[]{:S(2)}, u32[]{:S(2)}) collective-permute-start(bf16[2,80,1024]{2,1,0:T(8,128)(2,1)} %pad_maximum_fusion.5), channel_id=1, source_target_pairs={{0,8},{8,0},{1,9},{9,1},{2,10},{10,2},{3,11},{11,3},{4,12},{12,4},... | collective-permute-start | bytes 983048 | tf_op jit(solution)/shard_map/ppermute | solution.py:26
  53.4 27.4 %all-to-all-start = ((bf16[16,128,256]{2,1,0:T(8,128)(2,1)}), bf16[16,128,256]{2,1,0:T(8,128)(2,1)}, u32[]{:S(2)}, u32[]{:S(2)}) async-start(bf16[16,128,256]{2,1,0:T(8,128)(2,1)} %bitcast.1), calls=%async_computation | async-start | bytes 2097152 | tf_op jit(solution)/shard_map/all_to_all | solution.py:30
  61.4 17.8 %collective-permute-start.6 = (bf16[2,80,1024]{2,1,0:T(8,128)(2,1)S(1)}, bf16[2,80,1024]{2,1,0:T(8,128)(2,1)S(1)}, u32[]{:S(2)}, u32[]{:S(2)}) collective-permute-start(bf16[2,80,1024]{2,1,0:T(8,128)(2,1)S(1)} %pad_maximum_fusion.4), channel_id=1, source_target_pairs={{0,2},{2,0},{1,3},{3,1},{4,6},{6,4},{5,7},{7,5},{8,10},{10,8},{9,1... | collective-permute-start | bytes 983048 | tf_op jit(solution)/shard_map/ppermute | solution.py:26
  63.2 32.0 %collective-permute-start.3 = (bf16[4,96,1024]{2,1,0:T(8,128)(2,1)S(1)}, bf16[4,96,1024]{2,1,0:T(8,128)(2,1)S(1)}, u32[]{:S(2)}, u32[]{:S(2)}) collective-permute-start(bf16[4,96,1024]{2,1,0:T(8,128)(2,1)S(1)} %pad_maximum_fusion.refs_0_), channel_id=1, source_target_pairs={{0,2},{2,0},{1,3},{3,1},{4,6},{6,4},{5,7},{7,5},{8,10},{10,8},{9,1... | collective-permute-start | bytes 2359304 | tf_op jit(solution)/shard_map/ppermute | solution.py:26
  65.9 29.3 %collective-permute-start.10 = (bf16[4,80,1024]{2,1,0:T(8,128)(2,1)S(1)}, bf16[4,80,1024]{2,1,0:T(8,128)(2,1)S(1)}, u32[]{:S(2)}, u32[]{:S(2)}) collective-permute-start(bf16[4,80,1024]{2,1,0:T(8,128)(2,1)S(1)} %pad_maximum_fusion.2.refs_4_), channel_id=1, source_target_pairs={{0,64},{64,0},{1,65},{65,1},{2,66},{66,2},{3,67},{67,3},{4,68},{68... | collective-permute-start | bytes 1966088 | tf_op jit(solution)/shard_map/ppermute | solution.py:26
  79.3 15.8 %collective-permute-start.7 = (bf16[4,80,1024]{2,1,0:T(8,128)(2,1)S(1)}, bf16[4,80,1024]{2,1,0:T(8,128)(2,1)}, u32[]{:S(2)}, u32[]{:S(2)}) collective-permute-start(bf16[4,80,1024]{2,1,0:T(8,128)(2,1)S(1)} %pad_maximum_fusion.1.refs_2_), channel_id=1, source_target_pairs={{0,8},{8,0},{1,9},{9,1},{2,10},{10,2},{3,11},{11,3},{4,12},{12,4},... | collective-permute-start | bytes 1966088 | tf_op jit(solution)/shard_map/ppermute | solution.py:26
  80.8 36.8 %collective-permute-start.12 = (bf16[2048,256]{1,0:T(8,128)(2,1)}, bf16[2048,256]{1,0:T(8,128)(2,1)S(1)}, u32[]{:S(2)}, u32[]{:S(2)}) collective-permute-start(bf16[2048,256]{1,0:T(8,128)(2,1)} %bitcast.2.t_own), channel_id=1, source_target_pairs={{0,32},{32,0},{1,33},{33,1},{2,34},{34,2},{3,35},{35,3},{4,36},{36... | collective-permute-start | bytes 3145736 | tf_op jit(solution)/shard_map/ppermute | solution.py:26
  171.1 18.9 %collective-permute-start.20 = (bf16[4,80,1024]{2,1,0:T(8,128)(2,1)S(1)}, bf16[4,80,1024]{2,1,0:T(8,128)(2,1)}, u32[]{:S(2)}, u32[]{:S(2)}) collective-permute-start(bf16[4,80,1024]{2,1,0:T(8,128)(2,1)S(1)} %pad_maximum_fusion.1.refs_2_), channel_id=1, source_target_pairs={{0,32},{32,0},{1,33},{33,1},{2,34},{34,2},{3,35},{35,3},{4,36},{36... | collective-permute-start | bytes 1966088 | tf_op jit(solution)/shard_map/ppermute | solution.py:26
  174.3 14.7 %all-to-all-start.3 = ((bf16[4,512,128]{2,1,0:T(8,128)(2,1)}), bf16[4,512,128]{2,1,0:T(8,128)(2,1)}, u32[]{:S(2)}, u32[]{:S(2)}) async-start(bf16[4,512,128]{2,1,0:T(8,128)(2,1)} %bitcast.44), calls=%async_computation.3 | async-start | bytes 1048576 | tf_op jit(solution)/shard_map/all_to_all | solution.py:30
  178.4 11.8 %collective-permute-start.19 = (bf16[4,96,1024]{2,1,0:T(8,128)(2,1)S(1)}, bf16[4,96,1024]{2,1,0:T(8,128)(2,1)}, u32[]{:S(2)}, u32[]{:S(2)}) collective-permute-start(bf16[4,96,1024]{2,1,0:T(8,128)(2,1)S(1)} %collective-permute-done.3.refs_1_), channel_id=1, source_target_pairs={{0,32},{32,0},{1,33},{33,1},{2,34},{34,2},{3,35},{35,3},{4,36},{36... | collective-permute-start | bytes 2359304 | tf_op jit(solution)/shard_map/ppermute | solution.py:26
  178.6 11.5 %collective-permute-start.22 = (bf16[4,80,1024]{2,1,0:T(8,128)(2,1)S(1)}, bf16[4,80,1024]{2,1,0:T(8,128)(2,1)}, u32[]{:S(2)}, u32[]{:S(2)}) collective-permute-start(bf16[4,80,1024]{2,1,0:T(8,128)(2,1)S(1)} %pad_maximum_fusion.2.refs_4_), channel_id=1, source_target_pairs={{0,32},{32,0},{1,33},{33,1},{2,34},{34,2},{3,35},{35,3},{4,36},{36... | collective-permute-start | bytes 1966088 | tf_op jit(solution)/shard_map/ppermute | solution.py:26
  179.0 11.1 %collective-permute-start.21 = (bf16[4,80,1024]{2,1,0:T(8,128)(2,1)}, bf16[4,80,1024]{2,1,0:T(8,128)(2,1)}, u32[]{:S(2)}, u32[]{:S(2)}) collective-permute-start(bf16[4,80,1024]{2,1,0:T(8,128)(2,1)} %collective-permute-done.7.refs_3_), channel_id=1, source_target_pairs={{0,32},{32,0},{1,33},{33,1},{2,34},{34,2},{3,35},{35,3},{4,36},{36... | collective-permute-start | bytes 1966088 | tf_op jit(solution)/shard_map/ppermute | solution.py:26
  198.1 39.4 %all-to-all-start.4 = ((bf16[32,128,256]{2,1,0:T(8,128)(2,1)}), bf16[32,128,256]{2,1,0:T(8,128)(2,1)S(1)}, u32[]{:S(2)}, u32[]{:S(2)}) async-start(bf16[32,128,256]{2,1,0:T(8,128)(2,1)} %shard_map.52), calls=%async_computation.4 | async-start | bytes 4194304 | tf_op jit(solution)/shard_map/all_to_all | solution.py:30
  204.5 16.3 %collective-permute-start.14 = (f32[4,128]{1,0:T(4,128)S(1)}, f32[4,128]{1,0:T(4,128)S(1)}, u32[]{:S(2)}, u32[]{:S(2)}) collective-permute-start(f32[4,128]{1,0:T(4,128)S(1)} %get-tuple-element.20), channel_id=1, source_target_pairs={{0,0},{1,4},{2,8},{3,12},{4,32},{5,36},{6,40},{7,44},{8,16},{9,20}... | collective-permute-start | bytes 6152 | tf_op jit(solution)/shard_map/ppermute | solution.py:252
  205.2 20.2 %collective-permute-start.15 = (f32[4,128]{1,0:T(4,128)S(1)}, f32[4,128]{1,0:T(4,128)S(1)}, u32[]{:S(2)}, u32[]{:S(2)}) collective-permute-start(f32[4,128]{1,0:T(4,128)S(1)} %get-tuple-element.23), channel_id=1, source_target_pairs={{0,1},{1,5},{2,9},{3,13},{4,33},{5,37},{6,41},{7,45},{8,17},{9,21}... | collective-permute-start | bytes 6152 | tf_op jit(solution)/shard_map/ppermute | solution.py:252
  212.7 18.7 %collective-permute-start.16 = (f32[4,128]{1,0:T(4,128)S(1)}, f32[4,128]{1,0:T(4,128)S(1)}, u32[]{:S(2)}, u32[]{:S(2)}) collective-permute-start(f32[4,128]{1,0:T(4,128)S(1)} %get-tuple-element.22), channel_id=1, source_target_pairs={{0,2},{1,6},{2,10},{3,14},{4,34},{5,38},{6,42},{7,46},{8,18},{9,22... | collective-permute-start | bytes 6152 | tf_op jit(solution)/shard_map/ppermute | solution.py:252
  216.0 15.4 %collective-permute-start.17 = (f32[4,128]{1,0:T(4,128)S(1)}, f32[4,128]{1,0:T(4,128)S(1)}, u32[]{:S(2)}, u32[]{:S(2)}) collective-permute-start(f32[4,128]{1,0:T(4,128)S(1)} %get-tuple-element.21), channel_id=1, source_target_pairs={{0,3},{1,7},{2,11},{3,15},{4,35},{5,39},{6,43},{7,47},{8,19},{9,23... | collective-permute-start | bytes 6152 | tf_op jit(solution)/shard_map/ppermute | solution.py:252
  (19 other events, 352.0 us)

commit v4 on v3

--- a/solution.py
+++ b/solution.py
@@ -34,14 +34,23 @@
 CUBE = ("xl", "yl", "zl")
 
 
-def gather_cube(share):
-    held = [share[None, first:last] for first, last, _ in RUNS]
-    far = held
-    for stage in range(3):
-        far = [swap(piece, CUBE[order[stage]]) for piece, (_, _, order) in zip(held, RUNS)]
-        if stage < 2:
-            held = [jnp.concatenate(both) for both in zip(held, far)]
-    return [piece for both in zip(held, far) for piece in both]
+def hop(held, stage):
+    return [swap(piece, CUBE[order[stage]]) for piece, (_, _, order) in zip(held, RUNS)]
+
+
+def joined(held, far):
+    return [jnp.concatenate(both) for both in zip(held, far)]
+
+
+def trade(chunks):
+    got = [chunks[0]]
+    for r in range(1, 4):
+        got.append(lax.ppermute(chunks[r], BLOCK, [(i, i ^ r) for i in range(4)]))
+    return got
+
+
+def after(value, *others):
+    return lax.optimization_barrier((value, *others))[0]
 
 
 def run_piece(refs, run, hops, first, last):
@@ -86,7 +95,8 @@
                 for dz in range(2):
                     at = (dx * 2 + dz) * 128
                     rows = pl.ds(pl.multiple_of(token_place(dx, dz) * 128, 128), 128)
-                    out[(core ^ i) * 2 + j, rows, :] = value[at : at + 128, j * 128 : (j + 1) * 128]
+                    slot = (core ^ i ^ lax.axis_index("zh")) * 2 + (lax.axis_index("yh") ^ j)
+                    out[slot, rows, :] = value[at : at + 128, j * 128 : (j + 1) * 128]
 
 
 def project(hidden, w_own, w_other):
@@ -95,6 +105,7 @@
         in_specs=[WHOLE] * 8,
         out_specs=WHOLE,
         out_shape=jax.ShapeDtypeStruct((4, 512, 128), jnp.bfloat16),
+        cost_estimate=pl.CostEstimate(flops=2 * 512 * 4096 * 512, bytes_accessed=9 << 20, transcendentals=0),
         compiler_params=pltpu.CompilerParams(vmem_limit_bytes=48 << 20),
     )(*hidden, w_own, w_other)
 
@@ -108,7 +119,8 @@
         for dx in range(2):
             for dz in range(2):
                 at = pl.ds(pl.multiple_of(token_place(dx, dz) * 128, 128), 128)
-                rows.append(jnp.concatenate([ref[0, at, :], ref[1, at, :]], axis=1))
+                yh = lax.axis_index("yh")
+                rows.append(jnp.concatenate([ref[yh, at, :], ref[1 - yh, at, :]], axis=1))
         return rows
 
     grad = jnp.concatenate(in_place(q_own) + in_place(q_other), axis=0)
@@ -127,6 +139,7 @@
         in_specs=[WHOLE] * 14,
         out_specs=WHOLE,
         out_shape=jax.ShapeDtypeStruct((32, 128, 256), jnp.bfloat16),
+        cost_estimate=pl.CostEstimate(flops=2 * 1024 * 4096 * 256, bytes_accessed=11 << 20, transcendentals=0),
         compiler_params=pltpu.CompilerParams(vmem_limit_bytes=48 << 20),
     )(*own, *other, q_own, q_other)
 
@@ -153,14 +166,22 @@
         own_ref[...] = jnp.zeros_like(own_ref)
         other_ref[...] = jnp.zeros_like(other_ref)
 
+    here = lax.axis_index("zh") * 2 + lax.axis_index("yh")
+    part = half // 4
+
+    def in_order(row):
+        return (row // part ^ here) * part + row % part
+
     mine = pl.ds(pl.multiple_of(step * block, block), block)
-    tr = t_own[mine, :]
+    first = pl.multiple_of(in_order(step * block), block)
+    tr = t_own[pl.ds(first, block), :]
     sr = s_own[mine, :]
     keys = [(t, s, g, c) for t, s, g in ((t_own, s_own, own_ref), (t_other, s_other, other_ref)) for c in range(0, half, chunk)]
     mt = ms = None
     for i, (t_keys, s_keys, _, c) in enumerate(keys):
         at = slice(i * chunk, (i + 1) * chunk)
-        u = t_mul * lax.dot_general(tr, t_keys[c : c + chunk, :], CONTRACT_LAST, preferred_element_type=jnp.float32)
+        t_at = pl.ds(pl.multiple_of(in_order(c), chunk), chunk)
+        u = t_mul * lax.dot_general(tr, t_keys[t_at, :], CONTRACT_LAST, preferred_element_type=jnp.float32)
         u_scr[:, at] = u
         fold = lane_fold(u, jnp.maximum)
         mt = fold if mt is None else jnp.maximum(mt, fold)
@@ -195,7 +216,7 @@
         for c in range(0, 2 * half, LANES):
             g = jnp.exp2(v_scr[rows, c : c + LANES] - z_s) - jnp.exp2(u_scr[rows, c : c + LANES] - z_t)
             g_scr[rows, c : c + LANES] = g.astype(jnp.bfloat16)
-    kl_ref[pl.ds(step, 1), :] = jnp.transpose(kl_scr[...])[:1]
+    kl_ref[pl.ds(first // block, 1), :] = jnp.transpose(kl_scr[...])[:1]
     acc = jnp.zeros((block, width), jnp.float32)
     for i, (_, s_keys, g_ref, c) in enumerate(keys):
         g = g_scr[:, i * chunk : (i + 1) * chunk]
@@ -233,6 +254,11 @@
             pltpu.VMEM((block, 2 * half), jnp.bfloat16),
             pltpu.VMEM((block, LANES), jnp.float32),
         ],
+        cost_estimate=pl.CostEstimate(
+            flops=2 * half * 2 * half * (t_width + 3 * s_width),
+            bytes_accessed=6 * half * (t_width + 3 * s_width),
+            transcendentals=8 * half * half,
+        ),
         compiler_params=pltpu.CompilerParams(vmem_limit_bytes=50 << 20),
     )(t_own, s_own, t_other, s_other)
 
@@ -269,27 +295,39 @@
         first, second = value[: rows // 2], value[rows // 2 :]
         return jnp.where(low, first, second), swap(jnp.where(low, second, first), "core")
 
-    hidden = gather_cube(jnp.concatenate(token_halves(student_hidden)))
+    share = jnp.concatenate(token_halves(student_hidden))
+    held = [share[None, first:last] for first, last, _ in RUNS]
+    far = hop(held, 0)
     parts = jnp.moveaxis(query_weight.reshape(depth, 2, 1, 2, 1, width), 0, 4)
-    w_own = exchange(jnp.broadcast_to(parts, (2, 2, 2, 2, 2, depth, width)).reshape(32, depth, width), DP)
-    w_own = w_own.reshape(32 * depth, width)
-    w_other = swap(w_own, "core")
-    student = exchange(project(hidden, w_own, w_other), BLOCK).reshape(2048, -1)
-    student_other = swap(student, "core")
+    parts = jnp.broadcast_to(parts, (2, 2, 2, 2, 2, depth, width)).reshape(32, depth, width)
+    w_own = exchange(after(parts, *far), DP)
+    held = joined(held, far)
+    far = hop(held, 1)
     t_own, t_other = token_halves(teacher_query)
     heads = jnp.stack([jnp.where(low, t_own, t_other), jnp.where(low, t_other, t_own)])
     heads = heads.reshape(2, rows // 2, 2, 2, 2, t_width).transpose(0, 4, 2, 3, 1, 5)
-    teacher = exchange(heads.reshape(16, rows // 2, t_width), SPREAD).reshape(2048, t_width)
+    heads = heads.reshape(16, rows // 2, t_width)
+    held = joined(held, far)
+    w_own = after(w_own, *held).reshape(32 * depth, width)
+    w_other = swap(w_own, "core")
+    far = hop(held, 2)
+    hidden = [piece for both in zip(held, far) for piece in both]
+    teacher = exchange(after(heads, *far), SPREAD).reshape(2048, t_width)
+    student = jnp.concatenate(trade(project(hidden, w_own, w_other)))
+    teacher = after(teacher, student)
+    hidden_other = [swap(piece, "core") for piece in hidden]
     teacher_other = swap(teacher, "core")
-
-    kl, grad, grad_other = relation(teacher, student, teacher_other, student_other)
-    hidden_other = [swap(piece, "core") for piece in hidden]
+    student_other = swap(student, "core")
+
+    kl, grad, grad_other = relation(after(teacher, *hidden_other), student, teacher_other, student_other)
     query_grad = (grad + swap(grad_other, "core")).astype(jnp.bfloat16)
-    query_grad = exchange(query_grad.reshape(4, 512, -1), BLOCK).reshape(2, 2, 512, -1)
-    mine = jnp.where(low, query_grad[0], query_grad[1])
-    theirs = swap(jnp.where(low, query_grad[1], query_grad[0]), "core")
-    sent = exchange(weight_grad_part(hidden, hidden_other, mine, theirs), DP)
+    query_grad = trade(query_grad.reshape(4, 512, -1))
+    near, away = jnp.stack(query_grad[:2]), jnp.stack(query_grad[2:])
+    same = core == lax.axis_index("zh")
+    mine = jnp.where(same, near, away)
+    theirs = swap(jnp.where(same, away, near), "core")
     kl_rows = owned_rows(kl)
+    sent = exchange(weight_grad_part(hidden, hidden_other, mine, after(theirs, kl_rows)), DP)
     sent = sent.reshape(2, 2, 2, 2, 2, depth, width)
     total = None
     for xh in range(2):

time: 240 us -> 241 us (level)
  waiting for transfers between devices: 88.7 us -> 55.8 us
  blocking collectives: 17.3 us -> 37.1 us
  local copies, waits for them, and re-layouts: 7.2 us -> 13.9 us
  starting transfers between devices: 54.4 us -> 58.2 us
    all_to_all x4 -> x2, waiting for transfers between devices: 41.4 us -> 0.01 us  [exchange(): return lax.all_to_all(chunks, axes, split_axis=0, concat_axis=0, tiled=True)]
    all_to_all x1, blocking collectives: 17.3 us -> 37.1 us  [exchange(): return lax.all_to_all(chunks, axes, split_axis=0, concat_axis=0, tiled=True)]
    ppermute x0 -> x6, starting transfers between devices: none -> 13.1 us  [trade(): got.append(lax.ppermute(chunks[r], BLOCK, [(i, i ^ r) for i in range(4)]))]
    ppermute x0 -> x6, waiting for transfers between devices: none -> 10.8 us  [trade(): got.append(lax.ppermute(chunks[r], BLOCK, [(i, i ^ r) for i in range(4)]))]
    ppermute x4, waiting for transfers between devices: 10.6 us -> 0.26 us  [owned_rows(): got.append(lax.ppermute(sent, ('core',) + DP, pairs))]
    ppermute x22, waiting for transfers between devices: 36.7 us -> 44.7 us  [swap(): return lax.ppermute(value, axis, SWAP)]
    all_to_all x4 -> x2, starting transfers between devices: 25.1 us -> 17.6 us  [exchange(): return lax.all_to_all(chunks, axes, split_axis=0, concat_axis=0, tiled=True)]
    ppermute x4, starting transfers between devices: 16.3 us -> 11.5 us  [owned_rows(): got.append(lax.ppermute(sent, ('core',) + DP, pairs))]
  transfers between devices with their start and end apart: 30 -> 34, of which waited for: 11 -> 13; matrix products, arithmetic and copies ran while one was open for 4% -> 6% of each run, Pallas kernels for 2% -> 2%
where the time goes in v4:
time: 241 us; the launch traced here: 238 us
  Pallas kernels  62.2 us (26%)
  starting transfers between devices  58.2 us (24%)
  waiting for transfers between devices  55.8 us (23%)
  blocking collectives  37.1 us (15%)
  local copies, waits for them, and re-layouts  13.9 us (6%)
  other arithmetic  10 us (4%)
    pallas_call x1, Pallas kernels, relation(): pl.pallas_call(functools.partial(relation_kernel, block, chunk, sub), gri...  51.1 us
    ppermute x22, waiting for transfers between devices, swap(): return lax.ppermute(value, axis, SWAP)  44.7 us
    all_to_all x1, blocking collectives, exchange(): return lax.all_to_all(chunks, axes, split_axis=0, concat_axis=0, tiled=True)  37.1 us
    all_to_all x2, starting transfers between devices, exchange(): return lax.all_to_all(chunks, axes, split_axis=0, concat_axis=0, tiled=True)  17.6 us
    ppermute x22, starting transfers between devices, swap(): return lax.ppermute(value, axis, SWAP)  16 us
    ppermute x6, starting transfers between devices, trade(): got.append(lax.ppermute(chunks[r], BLOCK, [(i, i ^ r) for i in range(4)]))  13.1 us
    ppermute x4, starting transfers between devices, owned_rows(): got.append(lax.ppermute(sent, ('core',) + DP, pairs))  11.5 us
    ppermute x6, waiting for transfers between devices, trade(): got.append(lax.ppermute(chunks[r], BLOCK, [(i, i ^ r) for i in range(4)]))  10.8 us
  transfers between devices with their start and end apart: 34, of which 13 were waited for; matrix products, arithmetic and copies ran while one was open for 6% of the time, Pallas kernels for 2%

profile of v4, /device:TPU:8, one launch (start us, length us, event | category | flops | bytes accessed | tf_op | source)
XLA Modules:
  0.0 238.2 jit_solution(2008528977614795361)
XLA Ops:
  6.1 3.1 %collective-permute-done.1 = bf16[1,96,1024]{2,1,0:T(8,128)(2,1)S(1)} collective-permute-done((bf16[1,96,1024]{2,1,0:T(8,128)(2,1)S(1)}, bf16[1,96,1024]{2,1,0:T(8,128)(2,1)S(1)}, u32[]{:S(2)}, u32[]{:S(2)}) %collective-permute-start.1) | collective-permute-done | bytes 196640 | tf_op jit(solution)/shard_map/ppermute | solution.py:26
  11.8 10.0 %all-to-all-start.1 = ((bf16[32,128,256]{2,1,0:T(8,128)(2,1)}), bf16[32,128,256]{2,1,0:T(8,128)(2,1)}, u32[]{:S(2)}, u32[]{:S(2)}) async-start(bf16[32,128,256]{2,1,0:T(8,128)(2,1)} %bitcast.8), calls=%async_computation.1 | async-start | bytes 4194304 | tf_op jit(solution)/shard_map/all_to_all | solution.py:30
  27.2 27.6 %collective-permute-done.2 = bf16[2,96,1024]{2,1,0:T(8,128)(2,1)S(1)} collective-permute-done((bf16[2,96,1024]{2,1,0:T(8,128)(2,1)S(1)}, bf16[2,96,1024]{2,1,0:T(8,128)(2,1)S(1)}, u32[]{:S(2)}, u32[]{:S(2)}) %collective-permute-start.2) | collective-permute-done | bytes 393248 | tf_op jit(solution)/shard_map/ppermute | solution.py:26
  57.0 2.0 collective-permute-start.3
  60.9 2.3 broadcast_select_fusion.1
  63.2 2.3 stack.46
  65.5 2.2 stack.47
  67.7 2.8 %maximum_bitcast_fusion = bf16[2,2,2,2,128,256]{5,1,3,2,4,0:T(2,128)(2,1)S(1)} fusion(bf16[1,128,2,2,2,256]{5,4,3,2,1,0:T(2,128)(2,1)} %stack.47, bf16[1,128,2,2,2,256]{5,4,3,2,1,0:T(2,128)(2,1)} %stack.46), kind=kLoop, calls=%fused_computation | loop fusion | flops 524288 | bytes 2097152 | tf_op jit(solution)/shard_map/transpose | solution.py:308
  71.7 5.1 %collective-permute-done.3.refs_1_ = bf16[4,96,1024]{2,1,0:T(8,128)(2,1)S(1)} collective-permute-done((bf16[4,96,1024]{2,1,0:T(8,128)(2,1)S(1)}, bf16[4,96,1024]{2,1,0:T(8,128)(2,1)S(1)}, u32[]{:S(2)}, u32[]{:S(2)}) %collective-permute-start.3) | collective-permute-done | bytes 786464 | tf_op jit(solution)/shard_map/ppermute | solution.py:26
  76.8 7.7 %all-to-all-start = ((bf16[16,128,256]{2,1,0:T(8,128)(2,1)}), bf16[16,128,256]{2,1,0:T(8,128)(2,1)}, u32[]{:S(2)}, u32[]{:S(2)}) async-start(bf16[16,128,256]{2,1,0:T(8,128)(2,1)} %bitcast.53), calls=%async_computation | async-start | bytes 2097152 | tf_op jit(solution)/shard_map/all_to_all | solution.py:30
  84.6 4.8 %shard_map.50 = bf16[4,512,128]{2,1,0:T(8,128)(2,1)S(1)} custom-call(bf16[4,96,1024]{2,1,0:T(8,128)(2,1)S(1)} %pad_maximum_fusion.refs_0_, bf16[4,96,1024]{2,1,0:T(8,128)(2,1)S(1)} %collective-permute-done.3.refs_1_, bf16[4,80,1024]{2,1,0:T(8,128)(2,1)S(1)} %pad_maximum_fusion.1.refs_2_, bf16[4,80,1024]{2,1,0:T(8,128)(2,1)} %collective-permute-done.7.refs_3_, ...), custom_call_target="tpu_custom_call" | custom-call | flops 2147483648 | bytes 9437184 | tf_op jit(solution)/shard_map/pallas_call | solution.py:103
  89.4 3.4 %collective-permute-start.12 = (bf16[512,128]{1,0:T(8,128)(2,1)S(1)}, bf16[512,128]{1,0:T(8,128)(2,1)S(1)}, u32[]{:S(2)}, u32[]{:S(2)}) collective-permute-start(bf16[512,128]{1,0:T(8,128)(2,1)S(1)} %get-tuple-element.31), channel_id=1, source_target_pairs={{0,1},{1,0},{4,5},{5,4},{2,3},{3,2},{6,7},{7,6},{8,9},{9,8},{12,13... | collective-permute-start | bytes 393224 | tf_op jit(solution)/shard_map/ppermute | solution.py:48
  92.8 3.0 %collective-permute-start.13 = (bf16[512,128]{1,0:T(8,128)(2,1)S(1)}, bf16[512,128]{1,0:T(8,128)(2,1)S(1)}, u32[]{:S(2)}, u32[]{:S(2)}) collective-permute-start(bf16[512,128]{1,0:T(8,128)(2,1)S(1)} %get-tuple-element.30), channel_id=1, source_target_pairs={{0,4},{1,5},{4,0},{5,1},{2,6},{3,7},{6,2},{7,3},{8,12},{9,13},{12,... | collective-permute-start | bytes 393224 | tf_op jit(solution)/shard_map/ppermute | solution.py:48
  96.0 7.0 %collective-permute-done.12 = bf16[512,128]{1,0:T(8,128)(2,1)S(1)} collective-permute-done((bf16[512,128]{1,0:T(8,128)(2,1)S(1)}, bf16[512,128]{1,0:T(8,128)(2,1)S(1)}, u32[]{:S(2)}, u32[]{:S(2)}) %collective-permute-start.12) | collective-permute-done | bytes 131104 | tf_op jit(solution)/shard_map/ppermute | solution.py:48
  104.4 2.4 %collective-permute-done.14 = bf16[512,128]{1,0:T(8,128)(2,1)S(1)} collective-permute-done((bf16[512,128]{1,0:T(8,128)(2,1)S(1)}, bf16[512,128]{1,0:T(8,128)(2,1)S(1)}, u32[]{:S(2)}, u32[]{:S(2)}) %collective-permute-start.14) | collective-permute-done | bytes 131104 | tf_op jit(solution)/shard_map/ppermute | solution.py:48
  109.0 4.1 %collective-permute-done.18.refs_9_ = bf16[4,80,1024]{2,1,0:T(8,128)(2,1)S(1)} collective-permute-done((bf16[4,80,1024]{2,1,0:T(8,128)(2,1)}, bf16[4,80,1024]{2,1,0:T(8,128)(2,1)S(1)}, u32[]{:S(2)}, u32[]{:S(2)}) %collective-permute-start.18) | collective-permute-done | bytes 655392 | tf_op jit(solution)/shard_map/ppermute | solution.py:26
  117.6 51.1 %shard_map.51 = (f32[8,256]{1,0:T(8,128)S(1)}, f32[2048,128]{1,0:T(8,128)S(1)}, f32[2048,128]{1,0:T(8,128)S(1)}) custom-call(bf16[2048,256]{1,0:T(8,128)(2,1)} %bitcast.5.t_own, bf16[2048,128]{1,0:T(8,128)(2,1)S(1)} %copy-done.4, bf16[2048,256]{1,0:T(8,128)(2,1)} %copy-done.7, bf16[2048,128]{1,0:T(8,128)(2,1)S(1)} %collective-permute-done.22.s_other), custom_call_target="tpu_custom_call" | custom-call | flops 10737418240 | bytes 7864320 | tf_op jit(solution)/shard_map/pallas_call | solution.py:241
  169.1 2.4 %collective-permute-done.27 = f32[2048,128]{1,0:T(8,128)S(1)} collective-permute-done((f32[2048,128]{1,0:T(8,128)S(1)}, f32[2048,128]{1,0:T(8,128)S(1)}, u32[]{:S(2)}, u32[]{:S(2)}) %collective-permute-start.27) | collective-permute-done | bytes 1048608 | tf_op jit(solution)/shard_map/ppermute | solution.py:26
  173.9 4.9 %collective-permute-start.30 = (bf16[512,128]{1,0:T(8,128)(2,1)}, bf16[512,128]{1,0:T(8,128)(2,1)}, u32[]{:S(2)}, u32[]{:S(2)}) collective-permute-start(bf16[512,128]{1,0:T(8,128)(2,1)} %get-tuple-element.25), channel_id=1, source_target_pairs={{0,5},{1,4},{4,1},{5,0},{2,7},{3,6},{6,3},{7,2},{8,13},{9,12},{12,... | collective-permute-start | bytes 393224 | tf_op jit(solution)/shard_map/ppermute | solution.py:48
  179.6 5.3 %collective-permute-start.24 = (f32[4,128]{1,0:T(4,128)S(1)}, f32[4,128]{1,0:T(4,128)S(1)}, u32[]{:S(2)}, u32[]{:S(2)}) collective-permute-start(f32[4,128]{1,0:T(4,128)S(1)} %get-tuple-element.43), channel_id=1, source_target_pairs={{0,1},{1,5},{2,9},{3,13},{4,33},{5,37},{6,41},{7,45},{8,17},{9,21}... | collective-permute-start | bytes 6152 | tf_op jit(solution)/shard_map/ppermute | solution.py:278
  184.8 2.7 %collective-permute-start.25 = (f32[4,128]{1,0:T(4,128)S(1)}, f32[4,128]{1,0:T(4,128)S(1)}, u32[]{:S(2)}, u32[]{:S(2)}) collective-permute-start(f32[4,128]{1,0:T(4,128)S(1)} %get-tuple-element.42), channel_id=1, source_target_pairs={{0,2},{1,6},{2,10},{3,14},{4,34},{5,38},{6,42},{7,46},{8,18},{9,22... | collective-permute-start | bytes 6152 | tf_op jit(solution)/shard_map/ppermute | solution.py:278
  187.5 2.9 %collective-permute-start.26 = (f32[4,128]{1,0:T(4,128)S(1)}, f32[4,128]{1,0:T(4,128)S(1)}, u32[]{:S(2)}, u32[]{:S(2)}) collective-permute-start(f32[4,128]{1,0:T(4,128)S(1)} %get-tuple-element.41), channel_id=1, source_target_pairs={{0,3},{1,7},{2,11},{3,15},{4,35},{5,39},{6,43},{7,47},{8,19},{9,23... | collective-permute-start | bytes 6152 | tf_op jit(solution)/shard_map/ppermute | solution.py:278
  193.3 6.3 %shard_map.52 = bf16[32,128,256]{2,1,0:T(8,128)(2,1)} custom-call(bf16[4,96,1024]{2,1,0:T(8,128)(2,1)} %copy-done, bf16[4,96,1024]{2,1,0:T(8,128)(2,1)} %copy-done.1, bf16[4,80,1024]{2,1,0:T(8,128)(2,1)S(1)} %pad_maximum_fusion.1.refs_2_, bf16[4,80,1024]{2,1,0:T(8,128)(2,1)} %collective-permute-done.7.refs_3_, ...), custom_call_target="tpu_custom_call" | custom-call | flops 2147483648 | bytes 11534336 | tf_op jit(solution)/shard_map/pallas_call | solution.py:137
  199.5 37.1 %all_to_all.15 = bf16[32,128,256]{2,1,0:T(8,128)(2,1)S(1)} all-to-all(bf16[32,128,256]{2,1,0:T(8,128)(2,1)} %shard_map.52), channel_id=1, replica_groups=mesh['yl'=2,'core'=2,'xh'=2,'xl'=2,'zh'=2,'zl'=2,'yh'=2] {'xh','xl','zh'..., dimensions={0} | all-to-all | bytes 4194304 | tf_op jit(solution)/shard_map/all_to_all | solution.py:30
  (97 shorter events, 34.9 us)
Async XLA Ops:
  1.9 7.4 %collective-permute-start.1 = (bf16[1,96,1024]{2,1,0:T(8,128)(2,1)S(1)}, bf16[1,96,1024]{2,1,0:T(8,128)(2,1)S(1)}, u32[]{:S(2)}, u32[]{:S(2)}) collective-permute-start(bf16[1,96,1024]{2,1,0:T(8,128)(2,1)S(1)} %slice_bitcast_fusion), channel_id=1, source_target_pairs={{0,8},{8,0},{1,9},{9,1},{2,10},{10,2},{3,11},{11,3},{4,12},{12,4},... | collective-permute-start | bytes 589832 | tf_op jit(solution)/shard_map/ppermute | solution.py:26
  3.5 6.4 %collective-permute-start.5 = (bf16[1,80,1024]{2,1,0:T(8,128)(2,1)S(1)}, bf16[1,80,1024]{2,1,0:T(8,128)(2,1)S(1)}, u32[]{:S(2)}, u32[]{:S(2)}) collective-permute-start(bf16[1,80,1024]{2,1,0:T(8,128)(2,1)S(1)} %get-tuple-element.35), channel_id=1, source_target_pairs={{0,64},{64,0},{1,65},{65,1},{2,66},{66,2},{3,67},{67,3},{4,68},{68... | collective-permute-start | bytes 491528 | tf_op jit(solution)/shard_map/ppermute | solution.py:26
  11.8 43.3 %all-to-all-start.1 = ((bf16[32,128,256]{2,1,0:T(8,128)(2,1)}), bf16[32,128,256]{2,1,0:T(8,128)(2,1)}, u32[]{:S(2)}, u32[]{:S(2)}) async-start(bf16[32,128,256]{2,1,0:T(8,128)(2,1)} %bitcast.8), calls=%async_computation.1 | async-start | bytes 4194304 | tf_op jit(solution)/shard_map/all_to_all | solution.py:30
  21.8 32.9 %collective-permute-start.2 = (bf16[2,96,1024]{2,1,0:T(8,128)(2,1)S(1)}, bf16[2,96,1024]{2,1,0:T(8,128)(2,1)S(1)}, u32[]{:S(2)}, u32[]{:S(2)}) collective-permute-start(bf16[2,96,1024]{2,1,0:T(8,128)(2,1)S(1)} %pad_maximum_fusion.4), channel_id=1, source_target_pairs={{0,64},{64,0},{1,65},{65,1},{2,66},{66,2},{3,67},{67,3},{4,68},{68... | collective-permute-start | bytes 1179656 | tf_op jit(solution)/shard_map/ppermute | solution.py:26
  23.8 31.0 %collective-permute-start.6 = (bf16[2,80,1024]{2,1,0:T(8,128)(2,1)S(1)}, bf16[2,80,1024]{2,1,0:T(8,128)(2,1)S(1)}, u32[]{:S(2)}, u32[]{:S(2)}) collective-permute-start(bf16[2,80,1024]{2,1,0:T(8,128)(2,1)S(1)} %pad_maximum_fusion.5), channel_id=1, source_target_pairs={{0,2},{2,0},{1,3},{3,1},{4,6},{6,4},{5,7},{7,5},{8,10},{10,8},{9,1... | collective-permute-start | bytes 983048 | tf_op jit(solution)/shard_map/ppermute | solution.py:26
  25.7 29.3 %collective-permute-start.9 = (bf16[2,80,1024]{2,1,0:T(8,128)(2,1)S(1)}, bf16[2,80,1024]{2,1,0:T(8,128)(2,1)S(1)}, u32[]{:S(2)}, u32[]{:S(2)}) collective-permute-start(bf16[2,80,1024]{2,1,0:T(8,128)(2,1)S(1)} %pad_maximum_fusion.6), channel_id=1, source_target_pairs={{0,8},{8,0},{1,9},{9,1},{2,10},{10,2},{3,11},{11,3},{4,12},{12,4},... | collective-permute-start | bytes 983048 | tf_op jit(solution)/shard_map/ppermute | solution.py:26
  55.1 29.5 %collective-permute-start.11 = (bf16[4096,256]{1,0:T(8,128)(2,1)}, bf16[4096,256]{1,0:T(8,128)(2,1)}, u32[]{:S(2)}, u32[]{:S(2)}) collective-permute-start(bf16[4096,256]{1,0:T(8,128)(2,1)} %bitcast.9.refs_6_), channel_id=1, source_target_pairs={{0,32},{32,0},{1,33},{33,1},{2,34},{34,2},{3,35},{35,3},{4,36},{36... | collective-permute-start | bytes 6291464 | tf_op jit(solution)/shard_map/ppermute | solution.py:26
  57.0 19.8 %collective-permute-start.3 = (bf16[4,96,1024]{2,1,0:T(8,128)(2,1)S(1)}, bf16[4,96,1024]{2,1,0:T(8,128)(2,1)S(1)}, u32[]{:S(2)}, u32[]{:S(2)}) collective-permute-start(bf16[4,96,1024]{2,1,0:T(8,128)(2,1)S(1)} %pad_maximum_fusion.refs_0_), channel_id=1, source_target_pairs={{0,2},{2,0},{1,3},{3,1},{4,6},{6,4},{5,7},{7,5},{8,10},{10,8},{9,1... | collective-permute-start | bytes 2359304 | tf_op jit(solution)/shard_map/ppermute | solution.py:26
  59.0 17.8 %collective-permute-start.10 = (bf16[4,80,1024]{2,1,0:T(8,128)(2,1)S(1)}, bf16[4,80,1024]{2,1,0:T(8,128)(2,1)S(1)}, u32[]{:S(2)}, u32[]{:S(2)}) collective-permute-start(bf16[4,80,1024]{2,1,0:T(8,128)(2,1)S(1)} %pad_maximum_fusion.2.refs_4_), channel_id=1, source_target_pairs={{0,64},{64,0},{1,65},{65,1},{2,66},{66,2},{3,67},{67,3},{4,68},{68... | collective-permute-start | bytes 1966088 | tf_op jit(solution)/shard_map/ppermute | solution.py:26
  59.2 17.6 %collective-permute-start.7 = (bf16[4,80,1024]{2,1,0:T(8,128)(2,1)S(1)}, bf16[4,80,1024]{2,1,0:T(8,128)(2,1)}, u32[]{:S(2)}, u32[]{:S(2)}) collective-permute-start(bf16[4,80,1024]{2,1,0:T(8,128)(2,1)S(1)} %pad_maximum_fusion.1.refs_2_), channel_id=1, source_target_pairs={{0,8},{8,0},{1,9},{9,1},{2,10},{10,2},{3,11},{11,3},{4,12},{12,4},... | collective-permute-start | bytes 1966088 | tf_op jit(solution)/shard_map/ppermute | solution.py:26
  76.8 30.8 %all-to-all-start = ((bf16[16,128,256]{2,1,0:T(8,128)(2,1)}), bf16[16,128,256]{2,1,0:T(8,128)(2,1)}, u32[]{:S(2)}, u32[]{:S(2)}) async-start(bf16[16,128,256]{2,1,0:T(8,128)(2,1)} %bitcast.53), calls=%async_computation | async-start | bytes 2097152 | tf_op jit(solution)/shard_map/all_to_all | solution.py:30
  84.5 23.7 %collective-permute-start.15 = (bf16[4,96,1024]{2,1,0:T(8,128)(2,1)S(1)}, bf16[4,96,1024]{2,1,0:T(8,128)(2,1)}, u32[]{:S(2)}, u32[]{:S(2)}) collective-permute-start(bf16[4,96,1024]{2,1,0:T(8,128)(2,1)S(1)} %pad_maximum_fusion.refs_0_), channel_id=1, source_target_pairs={{0,32},{32,0},{1,33},{33,1},{2,34},{34,2},{3,35},{35,3},{4,36},{36... | collective-permute-start | bytes 2359304 | tf_op jit(solution)/shard_map/ppermute | solution.py:26
  89.4 13.6 %collective-permute-start.12 = (bf16[512,128]{1,0:T(8,128)(2,1)S(1)}, bf16[512,128]{1,0:T(8,128)(2,1)S(1)}, u32[]{:S(2)}, u32[]{:S(2)}) collective-permute-start(bf16[512,128]{1,0:T(8,128)(2,1)S(1)} %get-tuple-element.31), channel_id=1, source_target_pairs={{0,1},{1,0},{4,5},{5,4},{2,3},{3,2},{6,7},{7,6},{8,9},{9,8},{12,13... | collective-permute-start | bytes 393224 | tf_op jit(solution)/shard_map/ppermute | solution.py:48
  92.8 11.6 %collective-permute-start.13 = (bf16[512,128]{1,0:T(8,128)(2,1)S(1)}, bf16[512,128]{1,0:T(8,128)(2,1)S(1)}, u32[]{:S(2)}, u32[]{:S(2)}) collective-permute-start(bf16[512,128]{1,0:T(8,128)(2,1)S(1)} %get-tuple-element.30), channel_id=1, source_target_pairs={{0,4},{1,5},{4,0},{5,1},{2,6},{3,7},{6,2},{7,3},{8,12},{9,13},{12,... | collective-permute-start | bytes 393224 | tf_op jit(solution)/shard_map/ppermute | solution.py:48
  95.8 11.0 %collective-permute-start.14 = (bf16[512,128]{1,0:T(8,128)(2,1)S(1)}, bf16[512,128]{1,0:T(8,128)(2,1)S(1)}, u32[]{:S(2)}, u32[]{:S(2)}) collective-permute-start(bf16[512,128]{1,0:T(8,128)(2,1)S(1)} %get-tuple-element.29), channel_id=1, source_target_pairs={{0,5},{1,4},{4,1},{5,0},{2,7},{3,6},{6,3},{7,2},{8,13},{9,12},{12,... | collective-permute-start | bytes 393224 | tf_op jit(solution)/shard_map/ppermute | solution.py:48
  96.0 12.2 %collective-permute-start.17 = (bf16[4,80,1024]{2,1,0:T(8,128)(2,1)S(1)}, bf16[4,80,1024]{2,1,0:T(8,128)(2,1)}, u32[]{:S(2)}, u32[]{:S(2)}) collective-permute-start(bf16[4,80,1024]{2,1,0:T(8,128)(2,1)S(1)} %pad_maximum_fusion.1.refs_2_), channel_id=1, source_target_pairs={{0,32},{32,0},{1,33},{33,1},{2,34},{34,2},{3,35},{35,3},{4,36},{36... | collective-permute-start | bytes 1966088 | tf_op jit(solution)/shard_map/ppermute | solution.py:26
  107.6 7.9 %collective-permute-start.21 = (bf16[2048,256]{1,0:T(8,128)(2,1)}, bf16[2048,256]{1,0:T(8,128)(2,1)S(1)}, u32[]{:S(2)}, u32[]{:S(2)}) collective-permute-start(bf16[2048,256]{1,0:T(8,128)(2,1)} %bitcast.5.t_own), channel_id=1, source_target_pairs={{0,32},{32,0},{1,33},{33,1},{2,34},{34,2},{3,35},{35,3},{4,36},{36... | collective-permute-start | bytes 3145736 | tf_op jit(solution)/shard_map/ppermute | solution.py:26
  107.7 7.0 %collective-permute-start.16 = (bf16[4,96,1024]{2,1,0:T(8,128)(2,1)S(1)}, bf16[4,96,1024]{2,1,0:T(8,128)(2,1)S(1)}, u32[]{:S(2)}, u32[]{:S(2)}) collective-permute-start(bf16[4,96,1024]{2,1,0:T(8,128)(2,1)S(1)} %collective-permute-done.3.refs_1_), channel_id=1, source_target_pairs={{0,32},{32,0},{1,33},{33,1},{2,34},{34,2},{3,35},{35,3},{4,36},{36... | collective-permute-start | bytes 2359304 | tf_op jit(solution)/shard_map/ppermute | solution.py:26
  172.4 12.5 %collective-permute-start.28 = (bf16[512,128]{1,0:T(8,128)(2,1)}, bf16[512,128]{1,0:T(8,128)(2,1)S(1)}, u32[]{:S(2)}, u32[]{:S(2)}) collective-permute-start(bf16[512,128]{1,0:T(8,128)(2,1)} %get-tuple-element.27), channel_id=1, source_target_pairs={{0,1},{1,0},{4,5},{5,4},{2,3},{3,2},{6,7},{7,6},{8,9},{9,8},{12,13... | collective-permute-start | bytes 393224 | tf_op jit(solution)/shard_map/ppermute | solution.py:48
  173.2 14.4 %collective-permute-start.29 = (bf16[512,128]{1,0:T(8,128)(2,1)}, bf16[512,128]{1,0:T(8,128)(2,1)}, u32[]{:S(2)}, u32[]{:S(2)}) collective-permute-start(bf16[512,128]{1,0:T(8,128)(2,1)} %get-tuple-element.26), channel_id=1, source_target_pairs={{0,4},{1,5},{4,0},{5,1},{2,6},{3,7},{6,2},{7,3},{8,12},{9,13},{12,... | collective-permute-start | bytes 393224 | tf_op jit(solution)/shard_map/ppermute | solution.py:48
  173.9 16.5 %collective-permute-start.30 = (bf16[512,128]{1,0:T(8,128)(2,1)}, bf16[512,128]{1,0:T(8,128)(2,1)}, u32[]{:S(2)}, u32[]{:S(2)}) collective-permute-start(bf16[512,128]{1,0:T(8,128)(2,1)} %get-tuple-element.25), channel_id=1, source_target_pairs={{0,5},{1,4},{4,1},{5,0},{2,7},{3,6},{6,3},{7,2},{8,13},{9,12},{12,... | collective-permute-start | bytes 393224 | tf_op jit(solution)/shard_map/ppermute | solution.py:48
  178.9 12.9 %collective-permute-start.23 = (f32[4,128]{1,0:T(4,128)S(1)}, f32[4,128]{1,0:T(4,128)S(1)}, u32[]{:S(2)}, u32[]{:S(2)}) collective-permute-start(f32[4,128]{1,0:T(4,128)S(1)} %get-tuple-element.40), channel_id=1, source_target_pairs={{0,0},{1,4},{2,8},{3,12},{4,32},{5,36},{6,40},{7,44},{8,16},{9,20}... | collective-permute-start | bytes 6152 | tf_op jit(solution)/shard_map/ppermute | solution.py:278
  179.6 12.2 %collective-permute-start.24 = (f32[4,128]{1,0:T(4,128)S(1)}, f32[4,128]{1,0:T(4,128)S(1)}, u32[]{:S(2)}, u32[]{:S(2)}) collective-permute-start(f32[4,128]{1,0:T(4,128)S(1)} %get-tuple-element.43), channel_id=1, source_target_pairs={{0,1},{1,5},{2,9},{3,13},{4,33},{5,37},{6,41},{7,45},{8,17},{9,21}... | collective-permute-start | bytes 6152 | tf_op jit(solution)/shard_map/ppermute | solution.py:278
  184.8 6.9 %collective-permute-start.25 = (f32[4,128]{1,0:T(4,128)S(1)}, f32[4,128]{1,0:T(4,128)S(1)}, u32[]{:S(2)}, u32[]{:S(2)}) collective-permute-start(f32[4,128]{1,0:T(4,128)S(1)} %get-tuple-element.42), channel_id=1, source_target_pairs={{0,2},{1,6},{2,10},{3,14},{4,34},{5,38},{6,42},{7,46},{8,18},{9,22... | collective-permute-start | bytes 6152 | tf_op jit(solution)/shard_map/ppermute | solution.py:278
  (18 other events, 135.0 us)

commit v5 on v4

--- a/solution.py
+++ b/solution.py
@@ -15,6 +15,7 @@
 DP = ("xh", "xl", "zh", "zl", "yh")
 BLOCK = ("zh", "yh")
 SPREAD = ("zh", "yh", "xl", "zl")
+XZ = (("xh", "xl"), ("zh", "zl"))
 SWAP = [(0, 1), (1, 0)]
 
 CONTRACT_LAST = (((1,), (1,)), ((), ()))
@@ -45,8 +46,51 @@
 def trade(chunks):
     got = [chunks[0]]
     for r in range(1, 4):
-        got.append(lax.ppermute(chunks[r], BLOCK, [(i, i ^ r) for i in range(4)]))
+        step = (r >> 1) * 6 + (r & 1)
+        got.append(lax.ppermute(chunks[r], ("zh", "zl", "yh"), [(i, i ^ step) for i in range(8)]))
     return got
+
+
+def gather_weight(weight):
+    depth, columns = weight.shape
+    parts = jnp.moveaxis(weight.reshape(depth, 4, columns // 4), 1, 0)
+    q = (lax.axis_index("xh") ^ lax.axis_index("xl")) * 2 + (lax.axis_index("zh") ^ lax.axis_index("zl"))
+    near = [lax.dynamic_index_in_dim(parts, q ^ r, 0, keepdims=False) for r in range(4)]
+    got = []
+    for step in range(8):
+        part = near[step >> 1]
+        if step:
+            part = lax.ppermute(part, ("xl", "zl", "yh"), [(i, i ^ step) for i in range(8)])
+        got.append(part)
+    held = [jnp.stack(got[:4])[None], jnp.stack(got[4:])[None]]
+    far = held
+    for stage in range(2):
+        if stage:
+            held = joined(held, far)
+        far = [
+            lax.ppermute(piece, axes, [(i, i ^ 3) for i in range(4)])
+            for piece, axes in zip(held, (XZ, XZ[::-1])[stage])
+        ]
+    return [piece for both in zip(held, far) for piece in both]
+
+
+def weight_in_order(refs, out):
+    depth = refs[0].shape[2]
+    for a in range(2):
+        for ex in range(2):
+            for ez in range(2):
+                first, second = (ez, ex) if a else (ex, ez)
+                for b in range(2):
+                    for y in range(2):
+                        place = (
+                            (lax.axis_index("xh") ^ ex) * 16
+                            + (lax.axis_index("xl") ^ ex ^ a) * 8
+                            + (lax.axis_index("zh") ^ ez) * 4
+                            + (lax.axis_index("zl") ^ ez ^ b) * 2
+                            + (lax.axis_index("yh") ^ y)
+                        )
+                        rows = pl.ds(pl.multiple_of(place * depth, depth), depth)
+                        out[rows, :] = refs[2 * a + second][first, 2 * b + y]
 
 
 def after(value, *others):
@@ -76,7 +120,9 @@
 
 
 def project_kernel(*refs):
-    hidden, (w_own, w_other, out) = refs[:6], refs[6:]
+    hidden, (out, w_own, w_other) = refs[:6], refs[14:]
+    weight_in_order(refs[6:10], w_own)
+    weight_in_order(refs[10:14], w_other)
     core = lax.axis_index("core")
     features = w_own.shape[0] // 4
     parts = [None, None]
@@ -102,12 +148,13 @@
 def project(hidden, w_own, w_other):
     return pl.pallas_call(
         project_kernel,
-        in_specs=[WHOLE] * 8,
+        in_specs=[WHOLE] * 14,
         out_specs=WHOLE,
         out_shape=jax.ShapeDtypeStruct((4, 512, 128), jnp.bfloat16),
+        scratch_shapes=[pltpu.VMEM((4096, 256), jnp.bfloat16)] * 2,
         cost_estimate=pl.CostEstimate(flops=2 * 512 * 4096 * 512, bytes_accessed=9 << 20, transcendentals=0),
         compiler_params=pltpu.CompilerParams(vmem_limit_bytes=48 << 20),
-    )(*hidden, w_own, w_other)
+    )(*hidden, *w_own, *w_other)
 
 
 def weight_grad_kernel(*refs):
@@ -273,7 +320,7 @@
             for dp in range(32):
                 xh, xl, zh, zl, yh = ((dp >> k) & 1 for k in (4, 3, 2, 1, 0))
                 quarter = turn ^ (xh * 2 + c)
-                pairs.append((c * 32 + dp, zh * 32 + xl * 16 + zl * 8 + yh * 4 + quarter))
+                pairs.append((c * 32 + dp, zh * 32 + (xh ^ xl) * 16 + (zh ^ zl) * 8 + yh * 4 + quarter))
         sent = lax.dynamic_index_in_dim(kl, turn ^ source, 0, keepdims=False)
         got.append(lax.ppermute(sent, ("core",) + DP, pairs))
     got = jnp.stack(got)
@@ -298,21 +345,20 @@
     share = jnp.concatenate(token_halves(student_hidden))
     held = [share[None, first:last] for first, last, _ in RUNS]
     far = hop(held, 0)
-    parts = jnp.moveaxis(query_weight.reshape(depth, 2, 1, 2, 1, width), 0, 4)
-    parts = jnp.broadcast_to(parts, (2, 2, 2, 2, 2, depth, width)).reshape(32, depth, width)
-    w_own = exchange(after(parts, *far), DP)
+    w_own = gather_weight(query_weight)
+    w_other = [swap(piece, "core") for piece in w_own]
     held = joined(held, far)
     far = hop(held, 1)
     t_own, t_other = token_halves(teacher_query)
     heads = jnp.stack([jnp.where(low, t_own, t_other), jnp.where(low, t_other, t_own)])
     heads = heads.reshape(2, rows // 2, 2, 2, 2, t_width).transpose(0, 4, 2, 3, 1, 5)
+    heads = jnp.where(lax.axis_index("xh") == 0, heads, heads[:, :, ::-1])
+    heads = jnp.stack([heads[0], heads[1][:, :, ::-1]])
     heads = heads.reshape(16, rows // 2, t_width)
     held = joined(held, far)
-    w_own = after(w_own, *held).reshape(32 * depth, width)
-    w_other = swap(w_own, "core")
     far = hop(held, 2)
     hidden = [piece for both in zip(held, far) for piece in both]
-    teacher = exchange(after(heads, *far), SPREAD).reshape(2048, t_width)
+    teacher = exchange(after(heads, *held), SPREAD).reshape(2048, t_width)
     student = jnp.concatenate(trade(project(hidden, w_own, w_other)))
     teacher = after(teacher, student)
     hidden_other = [swap(piece, "core") for piece in hidden]
@@ -326,16 +372,19 @@
     same = core == lax.axis_index("zh")
     mine = jnp.where(same, near, away)
     theirs = swap(jnp.where(same, away, near), "core")
+    sent = exchange(weight_grad_part(hidden, hidden_other, mine, theirs), DP)
     kl_rows = owned_rows(kl)
-    sent = exchange(weight_grad_part(hidden, hidden_other, mine, after(theirs, kl_rows)), DP)
     sent = sent.reshape(2, 2, 2, 2, 2, depth, width)
-    total = None
-    for xh in range(2):
-        for zh in range(2):
-            for yh in range(2):
-                term = sent[xh, :, zh, :, yh].astype(jnp.float32)
-                total = term if total is None else total + term
-    return kl_rows, total.reshape(4, depth, width).transpose(1, 0, 2).reshape(depth, columns)
+    groups = []
+    for q in range(4):
+        total = None
+        for xh in range(2):
+            for zh in range(2):
+                for yh in range(2):
+                    term = sent[xh, xh ^ (q >> 1), zh, zh ^ (q & 1), yh].astype(jnp.float32)
+                    total = term if total is None else total + term
+        groups.append(total)
+    return kl_rows, jnp.concatenate(groups, axis=1)
 
 
 def solution(mesh):

time: 241 us -> 236 us (0.979)
  blocking collectives: 37.1 us -> 0 us
  starting transfers between devices: 58.2 us -> 77 us
  waiting for transfers between devices: 55.8 us -> 64.3 us
  other arithmetic: 10 us -> 14.5 us
    all_to_all x1 -> x0, blocking collectives: 37.1 us -> none  [exchange(): return lax.all_to_all(chunks, axes, split_axis=0, concat_axis=0, tiled=True)]
    ppermute x6 -> x17, starting transfers between devices: 13.1 us -> 35.1 us  [the longest x7 12.7 us: gather_weight(): lax.ppermute(part, ('xl', 'zl', 'yh'), [(i, i ^ step) for i in range(8)])]
    ppermute x22 -> x25, waiting for transfers between devices: 44.7 us -> 31 us  [swap(): return lax.ppermute(value, axis, SWAP)]
    all_to_all x2, waiting for transfers between devices: 0.01 us -> 8.57 us  [exchange(): return lax.all_to_all(chunks, axes, split_axis=0, concat_axis=0, tiled=True)]
    ppermute x6 -> x17, waiting for transfers between devices: 10.8 us -> 18.4 us  [the longest x6 11.6 us: trade(): lax.ppermute(chunks[r], ('zh', 'zl', 'yh'), [(i, i ^ step) for i in range...]
    ppermute x22 -> x25, starting transfers between devices: 16 us -> 9.07 us  [swap(): return lax.ppermute(value, axis, SWAP)]
    ppermute x4, waiting for transfers between devices: 0.26 us -> 6.33 us  [owned_rows(): got.append(lax.ppermute(sent, ('core',) + DP, pairs))]
    concatenate x6 -> x8, other arithmetic: 0.32 us -> 6.31 us  [joined(): return [jnp.concatenate(both) for both in zip(held, far)]]
  transfers between devices with their start and end apart: 34 -> 48, of which waited for: 13 -> 20; matrix products, arithmetic and copies ran while one was open for 6% -> 7% of each run, Pallas kernels for 2% -> 2%
where the time goes in v5:
time: 236 us; the launch traced here: 235 us
  starting transfers between devices  77 us (33%)
  waiting for transfers between devices  64.3 us (27%)
  Pallas kernels  62.2 us (26%)
  local copies, waits for them, and re-layouts  16.2 us (7%)
  other arithmetic  14.5 us (6%)
    pallas_call x1, Pallas kernels, relation(): pl.pallas_call(functools.partial(relation_kernel, block, chunk, sub), gri...  51.1 us
    ppermute x25, waiting for transfers between devices, swap(): return lax.ppermute(value, axis, SWAP)  31 us
    ppermute x4, starting transfers between devices, owned_rows(): got.append(lax.ppermute(sent, ('core',) + DP, pairs))  17.4 us
    all_to_all x2, starting transfers between devices, exchange(): return lax.all_to_all(chunks, axes, split_axis=0, concat_axis=0, tiled=True)  15.5 us
    ppermute x7, starting transfers between devices, gather_weight(): lax.ppermute(part, ('xl', 'zl', 'yh'), [(i, i ^ step) for i in range(8)])  12.7 us
    ppermute x6, starting transfers between devices, trade(): lax.ppermute(chunks[r], ('zh', 'zl', 'yh'), [(i, i ^ step) for i in range...  12.5 us
    ppermute x6, waiting for transfers between devices, trade(): lax.ppermute(chunks[r], ('zh', 'zl', 'yh'), [(i, i ^ step) for i in range...  11.6 us
    ppermute x4, starting transfers between devices, gather_weight(): lax.ppermute(piece, axes, [(i, i ^ 3) for i in range(4)])  9.91 us
  transfers between devices with their start and end apart: 48, of which 20 were waited for; matrix products, arithmetic and copies ran while one was open for 7% of the time, Pallas kernels for 2%

profile of v5, /device:TPU:8, one launch (start us, length us, event | category | flops | bytes accessed | tf_op | source)
XLA Modules:
  0.0 235.4 jit_solution(1316740485930514307)
XLA Ops:
  6.4 2.9 %collective-permute-start.18 = (bf16[128,256]{1,0:T(8,128)(2,1)S(1)}, bf16[128,256]{1,0:T(8,128)(2,1)S(1)}, u32[]{:S(2)}, u32[]{:S(2)}) collective-permute-start(bf16[128,256]{1,0:T(8,128)(2,1)S(1)} %bitcast.88), channel_id=1, source_target_pairs={{0,10},{1,11},{2,8},{3,9},{8,2},{9,3},{10,0},{11,1},{4,14},{5,15},... | collective-permute-start | bytes 196616 | tf_op jit(solution)/shard_map/ppermute | solution.py:63
  17.8 2.9 %collective-permute-done.11 = bf16[128,256]{1,0:T(8,128)(2,1)S(1)} collective-permute-done((bf16[128,256]{1,0:T(8,128)(2,1)S(1)}, bf16[128,256]{1,0:T(8,128)(2,1)S(1)}, u32[]{:S(2)}, u32[]{:S(2)}) %collective-permute-start.11) | collective-permute-done | bytes 65568 | tf_op jit(solution)/shard_map/ppermute | solution.py:63
  20.7 4.0 %collective-permute-start.20 = (bf16[1,4,128,256]{3,2,1,0:T(8,128)(2,1)S(1)}, bf16[1,4,128,256]{3,2,1,0:T(8,128)(2,1)S(1)}, u32[]{:S(2)}, u32[]{:S(2)}) collective-permute-start(bf16[1,4,128,256]{3,2,1,0:T(8,128)(2,1)S(1)} %maximum_bitcast_fusion.2), channel_id=1, source_target_pairs={{0,6},{2,4},{4,2},{6,0},{1,7},{3,5},{5,3},{7,1},{8,14},{10,12},{12... | collective-permute-start | bytes 786440 | tf_op jit(solution)/shard_map/ppermute | solution.py:71
  24.8 2.8 %collective-permute-start.14 = (bf16[1,4,128,256]{3,2,1,0:T(8,128)(2,1)S(1)}, bf16[1,4,128,256]{3,2,1,0:T(8,128)(2,1)S(1)}, u32[]{:S(2)}, u32[]{:S(2)}) collective-permute-start(bf16[1,4,128,256]{3,2,1,0:T(8,128)(2,1)S(1)} %maximum_bitcast_fusion.1), channel_id=1, source_target_pairs={{0,24},{8,16},{16,8},{24,0},{1,25},{9,17},{17,9},{25,1},{2,26},{10... | collective-permute-start | bytes 786440 | tf_op jit(solution)/shard_map/ppermute | solution.py:71
  38.9 4.2 %collective-permute-done.4 = bf16[1,80,1024]{2,1,0:T(8,128)(2,1)S(1)} collective-permute-done((bf16[1,80,1024]{2,1,0:T(8,128)(2,1)S(1)}, bf16[1,80,1024]{2,1,0:T(8,128)(2,1)S(1)}, u32[]{:S(2)}, u32[]{:S(2)}) %collective-permute-start.4) | collective-permute-done | bytes 163872 | tf_op jit(solution)/shard_map/ppermute | solution.py:27
  47.5 5.9 %collective-permute-done.7 = bf16[2,80,1024]{2,1,0:T(8,128)(2,1)} collective-permute-done((bf16[2,80,1024]{2,1,0:T(8,128)(2,1)}, bf16[2,80,1024]{2,1,0:T(8,128)(2,1)}, u32[]{:S(2)}, u32[]{:S(2)}) %collective-permute-start.7) | collective-permute-done | bytes 327712 | tf_op jit(solution)/shard_map/ppermute | solution.py:27
  57.5 4.0 %collective-permute-done.5 = bf16[2,80,1024]{2,1,0:T(8,128)(2,1)S(1)} collective-permute-done((bf16[2,80,1024]{2,1,0:T(8,128)(2,1)}, bf16[2,80,1024]{2,1,0:T(8,128)(2,1)S(1)}, u32[]{:S(2)}, u32[]{:S(2)}) %collective-permute-start.5) | collective-permute-done | bytes 327712 | tf_op jit(solution)/shard_map/ppermute | solution.py:27
  68.0 6.1 %all-to-all-start = ((bf16[16,128,256]{2,1,0:T(8,128)(2,1)}), bf16[16,128,256]{2,1,0:T(8,128)(2,1)}, u32[]{:S(2)}, u32[]{:S(2)}) async-start(bf16[16,128,256]{2,1,0:T(8,128)(2,1)} %bitcast.82), calls=%async_computation | async-start | bytes 2097152 | tf_op jit(solution)/shard_map/all_to_all | solution.py:31
  74.2 8.6 %collective-permute-done.8.refs_1_ = bf16[4,96,1024]{2,1,0:T(8,128)(2,1)} collective-permute-done((bf16[4,96,1024]{2,1,0:T(8,128)(2,1)}, bf16[4,96,1024]{2,1,0:T(8,128)(2,1)}, u32[]{:S(2)}, u32[]{:S(2)}) %collective-permute-start.8) | collective-permute-done | bytes 786464 | tf_op jit(solution)/shard_map/ppermute | solution.py:27
  84.7 5.3 %shard_map.50 = bf16[4,512,128]{2,1,0:T(8,128)(2,1)S(1)} custom-call(bf16[4,96,1024]{2,1,0:T(8,128)(2,1)} %pad_maximum_fusion.1.refs_0_, bf16[4,96,1024]{2,1,0:T(8,128)(2,1)} %collective-permute-done.8.refs_1_, bf16[4,80,1024]{2,1,0:T(8,128)(2,1)S(1)} %pad_maximum_fusion.2.refs_2_, bf16[4,80,1024]{2,1,0:T(8,128)(2,1)S(1)} %collective-permute-done.9.refs_3_, ...), custom_call_target="tpu_custom_call" | custom-call | flops 2147483648 | bytes 9437184 | tf_op jit(solution)/shard_map/pallas_call | solution.py:149
  92.4 4.0 %collective-permute-start.28 = (bf16[512,128]{1,0:T(8,128)(2,1)S(1)}, bf16[512,128]{1,0:T(8,128)(2,1)S(1)}, u32[]{:S(2)}, u32[]{:S(2)}) collective-permute-start(bf16[512,128]{1,0:T(8,128)(2,1)S(1)} %get-tuple-element.29), channel_id=1, source_target_pairs={{0,7},{1,6},{2,5},{3,4},{4,3},{5,2},{6,1},{7,0},{8,15},{9,14},{10,... | collective-permute-start | bytes 393224 | tf_op jit(solution)/shard_map/ppermute | solution.py:50
  96.9 4.1 %collective-permute-done.28 = bf16[512,128]{1,0:T(8,128)(2,1)S(1)} collective-permute-done((bf16[512,128]{1,0:T(8,128)(2,1)S(1)}, bf16[512,128]{1,0:T(8,128)(2,1)S(1)}, u32[]{:S(2)}, u32[]{:S(2)}) %collective-permute-start.28) | collective-permute-done | bytes 131104 | tf_op jit(solution)/shard_map/ppermute | solution.py:50
  103.2 3.2 %collective-permute-done.32.refs_9_ = bf16[4,80,1024]{2,1,0:T(8,128)(2,1)S(1)} collective-permute-done((bf16[4,80,1024]{2,1,0:T(8,128)(2,1)S(1)}, bf16[4,80,1024]{2,1,0:T(8,128)(2,1)S(1)}, u32[]{:S(2)}, u32[]{:S(2)}) %collective-permute-start.32) | collective-permute-done | bytes 655392 | tf_op jit(solution)/shard_map/ppermute | solution.py:27
  112.1 51.1 %shard_map.51 = (f32[8,256]{1,0:T(8,128)S(1)}, f32[2048,128]{1,0:T(8,128)S(1)}, f32[2048,128]{1,0:T(8,128)S(1)}) custom-call(bf16[2048,256]{1,0:T(8,128)(2,1)} %bitcast.7.t_own, bf16[2048,128]{1,0:T(8,128)(2,1)S(1)} %copy-done.12, bf16[2048,256]{1,0:T(8,128)(2,1)} %copy-done.22, bf16[2048,128]{1,0:T(8,128)(2,1)S(1)} %collective-permute-done.36.s_other), custom_call_target="tpu_custom_call" | custom-call | flops 10737418240 | bytes 7864320 | tf_op jit(solution)/shard_map/pallas_call | solution.py:288
  166.8 3.4 %collective-permute-start.42 = (bf16[512,128]{1,0:T(8,128)(2,1)}, bf16[512,128]{1,0:T(8,128)(2,1)S(1)}, u32[]{:S(2)}, u32[]{:S(2)}) collective-permute-start(bf16[512,128]{1,0:T(8,128)(2,1)} %get-tuple-element.27), channel_id=1, source_target_pairs={{0,1},{1,0},{2,3},{3,2},{4,5},{5,4},{6,7},{7,6},{8,9},{9,8},{10,11... | collective-permute-start | bytes 393224 | tf_op jit(solution)/shard_map/ppermute | solution.py:50
  177.1 3.2 %collective-permute-done.44 = bf16[512,128]{1,0:T(8,128)(2,1)} collective-permute-done((bf16[512,128]{1,0:T(8,128)(2,1)}, bf16[512,128]{1,0:T(8,128)(2,1)}, u32[]{:S(2)}, u32[]{:S(2)}) %collective-permute-start.44) | collective-permute-done | bytes 131104 | tf_op jit(solution)/shard_map/ppermute | solution.py:50
  186.2 5.7 %shard_map.52 = bf16[32,128,256]{2,1,0:T(8,128)(2,1)} custom-call(bf16[4,96,1024]{2,1,0:T(8,128)(2,1)} %pad_maximum_fusion.1.refs_0_, bf16[4,96,1024]{2,1,0:T(8,128)(2,1)} %collective-permute-done.8.refs_1_, bf16[4,80,1024]{2,1,0:T(8,128)(2,1)S(1)} %pad_maximum_fusion.2.refs_2_, bf16[4,80,1024]{2,1,0:T(8,128)(2,1)S(1)} %collective-permute-done.9.refs_3_, ...), custom_call_target="tpu_custom_call" | custom-call | flops 2147483648 | bytes 11534336 | tf_op jit(solution)/shard_map/pallas_call | solution.py:184
  191.9 9.3 %all-to-all-start.1 = ((bf16[32,128,256]{2,1,0:T(8,128)(2,1)}), bf16[32,128,256]{2,1,0:T(8,128)(2,1)S(1)}, u32[]{:S(2)}, u32[]{:S(2)}) async-start(bf16[32,128,256]{2,1,0:T(8,128)(2,1)} %shard_map.52), calls=%async_computation.1 | async-start | bytes 4194304 | tf_op jit(solution)/shard_map/all_to_all | solution.py:31
  202.0 7.6 %collective-permute-start.38 = (f32[4,128]{1,0:T(4,128)S(1)}, f32[4,128]{1,0:T(4,128)S(1)}, u32[]{:S(2)}, u32[]{:S(2)}) collective-permute-start(f32[4,128]{1,0:T(4,128)S(1)} %get-tuple-element.49), channel_id=1, source_target_pairs={{0,1},{1,5},{2,9},{3,13},{4,41},{5,45},{6,33},{7,37},{8,17},{9,21}... | collective-permute-start | bytes 6152 | tf_op jit(solution)/shard_map/ppermute | solution.py:325
  209.6 5.2 %collective-permute-start.39 = (f32[4,128]{1,0:T(4,128)S(1)}, f32[4,128]{1,0:T(4,128)S(1)}, u32[]{:S(2)}, u32[]{:S(2)}) collective-permute-start(f32[4,128]{1,0:T(4,128)S(1)} %get-tuple-element.48), channel_id=1, source_target_pairs={{0,2},{1,6},{2,10},{3,14},{4,42},{5,46},{6,34},{7,38},{8,18},{9,22... | collective-permute-start | bytes 6152 | tf_op jit(solution)/shard_map/ppermute | solution.py:325
  214.7 4.0 %collective-permute-start.40 = (f32[4,128]{1,0:T(4,128)S(1)}, f32[4,128]{1,0:T(4,128)S(1)}, u32[]{:S(2)}, u32[]{:S(2)}) collective-permute-start(f32[4,128]{1,0:T(4,128)S(1)} %get-tuple-element.47), channel_id=1, source_target_pairs={{0,3},{1,7},{2,11},{3,15},{4,43},{5,47},{6,35},{7,39},{8,19},{9,23... | collective-permute-start | bytes 6152 | tf_op jit(solution)/shard_map/ppermute | solution.py:325
  218.7 3.5 %collective-permute-done.38 = f32[4,128]{1,0:T(4,128)S(1)} collective-permute-done((f32[4,128]{1,0:T(4,128)S(1)}, f32[4,128]{1,0:T(4,128)S(1)}, u32[]{:S(2)}, u32[]{:S(2)}) %collective-permute-start.38) | collective-permute-done | bytes 2080 | tf_op jit(solution)/shard_map/ppermute | solution.py:325
  222.2 2.9 %collective-permute-done.39 = f32[4,128]{1,0:T(4,128)S(1)} collective-permute-done((f32[4,128]{1,0:T(4,128)S(1)}, f32[4,128]{1,0:T(4,128)S(1)}, u32[]{:S(2)}, u32[]{:S(2)}) %collective-permute-start.39) | collective-permute-done | bytes 2080 | tf_op jit(solution)/shard_map/ppermute | solution.py:325
  225.7 8.6 %all-to-all-done.1 = bf16[32,128,256]{2,1,0:T(8,128)(2,1)S(1)} async-done(((bf16[32,128,256]{2,1,0:T(8,128)(2,1)}), bf16[32,128,256]{2,1,0:T(8,128)(2,1)S(1)}, u32[]{:S(2)}, u32[]{:S(2)}) %all-to-all-start.1) | async-done | bytes 2097184 | tf_op jit(solution)/shard_map/all_to_all | solution.py:31
  (165 shorter events, 71.6 us)
Async XLA Ops:
  2.5 10.5 %collective-permute-start.16 = (bf16[128,256]{1,0:T(8,128)(2,1)S(1)}, bf16[128,256]{1,0:T(8,128)(2,1)S(1)}, u32[]{:S(2)}, u32[]{:S(2)}) collective-permute-start(bf16[128,256]{1,0:T(8,128)(2,1)S(1)} %bitcast.90), channel_id=1, source_target_pairs={{0,8},{1,9},{2,10},{3,11},{8,0},{9,1},{10,2},{11,3},{4,12},{5,13},... | collective-permute-start | bytes 196616 | tf_op jit(solution)/shard_map/ppermute | solution.py:63
  4.1 10.9 %collective-permute-start.17 = (bf16[128,256]{1,0:T(8,128)(2,1)S(1)}, bf16[128,256]{1,0:T(8,128)(2,1)S(1)}, u32[]{:S(2)}, u32[]{:S(2)}) collective-permute-start(bf16[128,256]{1,0:T(8,128)(2,1)S(1)} %bitcast.91), channel_id=1, source_target_pairs={{0,9},{1,8},{2,11},{3,10},{8,1},{9,0},{10,3},{11,2},{4,13},{5,12},... | collective-permute-start | bytes 196616 | tf_op jit(solution)/shard_map/ppermute | solution.py:63
  10.1 10.7 %collective-permute-start.12 = (bf16[128,256]{1,0:T(8,128)(2,1)S(1)}, bf16[128,256]{1,0:T(8,128)(2,1)S(1)}, u32[]{:S(2)}, u32[]{:S(2)}) collective-permute-start(bf16[128,256]{1,0:T(8,128)(2,1)S(1)} %bitcast.86), channel_id=1, source_target_pairs={{0,2},{1,3},{2,0},{3,1},{8,10},{9,11},{10,8},{11,9},{4,6},{5,7},{6... | collective-permute-start | bytes 196616 | tf_op jit(solution)/shard_map/ppermute | solution.py:63
  13.0 11.7 %collective-permute-start.13 = (bf16[128,256]{1,0:T(8,128)(2,1)S(1)}, bf16[128,256]{1,0:T(8,128)(2,1)S(1)}, u32[]{:S(2)}, u32[]{:S(2)}) collective-permute-start(bf16[128,256]{1,0:T(8,128)(2,1)S(1)} %bitcast.87), channel_id=1, source_target_pairs={{0,3},{1,2},{2,1},{3,0},{8,11},{9,10},{10,9},{11,8},{4,7},{5,6},{6... | collective-permute-start | bytes 196616 | tf_op jit(solution)/shard_map/ppermute | solution.py:63
  16.2 13.6 %collective-permute-start.3 = (bf16[128,1024]{1,0:T(8,128)(2,1)S(1)}, bf16[128,1024]{1,0:T(8,128)(2,1)S(1)}, u32[]{:S(2)}, u32[]{:S(2)}) collective-permute-start(bf16[128,1024]{1,0:T(8,128)(2,1)S(1)} %get-tuple-element.32), channel_id=1, source_target_pairs={{0,32},{32,0},{1,33},{33,1},{2,34},{34,2},{3,35},{35,3},{4,36},{36... | collective-permute-start | bytes 786440 | tf_op jit(solution)/shard_map/ppermute | solution.py:27
  16.9 10.7 %collective-permute-start.1 = (bf16[1,96,1024]{2,1,0:T(8,128)(2,1)S(1)}, bf16[1,96,1024]{2,1,0:T(8,128)(2,1)S(1)}, u32[]{:S(2)}, u32[]{:S(2)}) collective-permute-start(bf16[1,96,1024]{2,1,0:T(8,128)(2,1)S(1)} %slice_bitcast_fusion.1), channel_id=1, source_target_pairs={{0,8},{8,0},{1,9},{9,1},{2,10},{10,2},{3,11},{11,3},{4,12},{12,4},... | collective-permute-start | bytes 589832 | tf_op jit(solution)/shard_map/ppermute | solution.py:27
  20.7 23.5 %collective-permute-start = (bf16[128,2048]{1,0:T(8,128)(2,1)}, bf16[128,2048]{1,0:T(8,128)(2,1)S(1)}, u32[]{:S(2)}, u32[]{:S(2)}) collective-permute-start(bf16[128,2048]{1,0:T(8,128)(2,1)} %broadcast_select_fusion.3), channel_id=1, source_target_pairs={{0,32},{32,0},{1,33},{33,1},{2,34},{34,2},{3,35},{35,3},{4,36},{36... | collective-permute-start | bytes 1572872 | tf_op jit(solution)/shard_map/ppermute | solution.py:27
  20.7 11.0 %collective-permute-start.20 = (bf16[1,4,128,256]{3,2,1,0:T(8,128)(2,1)S(1)}, bf16[1,4,128,256]{3,2,1,0:T(8,128)(2,1)S(1)}, u32[]{:S(2)}, u32[]{:S(2)}) collective-permute-start(bf16[1,4,128,256]{3,2,1,0:T(8,128)(2,1)S(1)} %maximum_bitcast_fusion.2), channel_id=1, source_target_pairs={{0,6},{2,4},{4,2},{6,0},{1,7},{3,5},{5,3},{7,1},{8,14},{10,12},{12... | collective-permute-start | bytes 786440 | tf_op jit(solution)/shard_map/ppermute | solution.py:71
  28.5 18.9 %collective-permute-start.2 = (bf16[2,96,1024]{2,1,0:T(8,128)(2,1)}, bf16[2,96,1024]{2,1,0:T(8,128)(2,1)}, u32[]{:S(2)}, u32[]{:S(2)}) collective-permute-start(bf16[2,96,1024]{2,1,0:T(8,128)(2,1)} %pad_maximum_fusion.8), channel_id=1, source_target_pairs={{0,64},{64,0},{1,65},{65,1},{2,66},{66,2},{3,67},{67,3},{4,68},{68... | collective-permute-start | bytes 1179656 | tf_op jit(solution)/shard_map/ppermute | solution.py:27
  31.7 11.4 %collective-permute-start.4 = (bf16[1,80,1024]{2,1,0:T(8,128)(2,1)S(1)}, bf16[1,80,1024]{2,1,0:T(8,128)(2,1)S(1)}, u32[]{:S(2)}, u32[]{:S(2)}) collective-permute-start(bf16[1,80,1024]{2,1,0:T(8,128)(2,1)S(1)} %get-tuple-element.39), channel_id=1, source_target_pairs={{0,64},{64,0},{1,65},{65,1},{2,66},{66,2},{3,67},{67,3},{4,68},{68... | collective-permute-start | bytes 491528 | tf_op jit(solution)/shard_map/ppermute | solution.py:27
  34.5 27.3 %collective-permute-start.21 = (bf16[2,4,128,256]{3,2,1,0:T(8,128)(2,1)S(1)}, bf16[2,4,128,256]{3,2,1,0:T(8,128)(2,1)}, u32[]{:S(2)}, u32[]{:S(2)}) collective-permute-start(bf16[2,4,128,256]{3,2,1,0:T(8,128)(2,1)S(1)} %pad_maximum_fusion.5.refs_8_), channel_id=1, source_target_pairs={{0,24},{8,16},{16,8},{24,0},{1,25},{9,17},{17,9},{25,1},{2,26},{10... | collective-permute-start | bytes 1572872 | tf_op jit(solution)/shard_map/ppermute | solution.py:71
  38.1 25.5 %collective-permute-start.24 = (bf16[2,4,128,256]{3,2,1,0:T(8,128)(2,1)S(1)}, bf16[2,4,128,256]{3,2,1,0:T(8,128)(2,1)}, u32[]{:S(2)}, u32[]{:S(2)}) collective-permute-start(bf16[2,4,128,256]{3,2,1,0:T(8,128)(2,1)S(1)} %pad_maximum_fusion.5.refs_8_), channel_id=1, source_target_pairs={{0,32},{32,0},{1,33},{33,1},{2,34},{34,2},{3,35},{35,3},{4,36},{36... | collective-permute-start | bytes 1572872 | tf_op jit(solution)/shard_map/ppermute | solution.py:27
  43.2 20.1 %collective-permute-start.15 = (bf16[2,4,128,256]{3,2,1,0:T(8,128)(2,1)}, bf16[2,4,128,256]{3,2,1,0:T(8,128)(2,1)}, u32[]{:S(2)}, u32[]{:S(2)}) collective-permute-start(bf16[2,4,128,256]{3,2,1,0:T(8,128)(2,1)} %pad_maximum_fusion.4.refs_6_), channel_id=1, source_target_pairs={{0,6},{2,4},{4,2},{6,0},{1,7},{3,5},{5,3},{7,1},{8,14},{10,12},{12... | collective-permute-start | bytes 1572872 | tf_op jit(solution)/shard_map/ppermute | solution.py:71
  47.4 16.2 %collective-permute-start.22 = (bf16[2,4,128,256]{3,2,1,0:T(8,128)(2,1)}, bf16[2,4,128,256]{3,2,1,0:T(8,128)(2,1)S(1)}, u32[]{:S(2)}, u32[]{:S(2)}) collective-permute-start(bf16[2,4,128,256]{3,2,1,0:T(8,128)(2,1)} %pad_maximum_fusion.4.refs_6_), channel_id=1, source_target_pairs={{0,32},{32,0},{1,33},{33,1},{2,34},{34,2},{3,35},{35,3},{4,36},{36... | collective-permute-start | bytes 1572872 | tf_op jit(solution)/shard_map/ppermute | solution.py:27
  61.5 21.4 %collective-permute-start.8 = (bf16[4,96,1024]{2,1,0:T(8,128)(2,1)}, bf16[4,96,1024]{2,1,0:T(8,128)(2,1)}, u32[]{:S(2)}, u32[]{:S(2)}) collective-permute-start(bf16[4,96,1024]{2,1,0:T(8,128)(2,1)} %pad_maximum_fusion.1.refs_0_), channel_id=1, source_target_pairs={{0,2},{2,0},{1,3},{3,1},{4,6},{6,4},{5,7},{7,5},{8,10},{10,8},{9,1... | collective-permute-start | bytes 2359304 | tf_op jit(solution)/shard_map/ppermute | solution.py:27
  61.9 21.0 %collective-permute-start.10 = (bf16[4,80,1024]{2,1,0:T(8,128)(2,1)S(1)}, bf16[4,80,1024]{2,1,0:T(8,128)(2,1)S(1)}, u32[]{:S(2)}, u32[]{:S(2)}) collective-permute-start(bf16[4,80,1024]{2,1,0:T(8,128)(2,1)S(1)} %pad_maximum_fusion.3.refs_4_), channel_id=1, source_target_pairs={{0,64},{64,0},{1,65},{65,1},{2,66},{66,2},{3,67},{67,3},{4,68},{68... | collective-permute-start | bytes 1966088 | tf_op jit(solution)/shard_map/ppermute | solution.py:27
  63.3 19.6 %collective-permute-start.9 = (bf16[4,80,1024]{2,1,0:T(8,128)(2,1)S(1)}, bf16[4,80,1024]{2,1,0:T(8,128)(2,1)S(1)}, u32[]{:S(2)}, u32[]{:S(2)}) collective-permute-start(bf16[4,80,1024]{2,1,0:T(8,128)(2,1)S(1)} %pad_maximum_fusion.2.refs_2_), channel_id=1, source_target_pairs={{0,8},{8,0},{1,9},{9,1},{2,10},{10,2},{3,11},{11,3},{4,12},{12,4},... | collective-permute-start | bytes 1966088 | tf_op jit(solution)/shard_map/ppermute | solution.py:27
  63.7 10.6 %collective-permute-start.23 = (bf16[2,4,128,256]{3,2,1,0:T(8,128)(2,1)}, bf16[2,4,128,256]{3,2,1,0:T(8,128)(2,1)}, u32[]{:S(2)}, u32[]{:S(2)}) collective-permute-start(bf16[2,4,128,256]{3,2,1,0:T(8,128)(2,1)} %collective-permute-done.15.refs_7_), channel_id=1, source_target_pairs={{0,32},{32,0},{1,33},{33,1},{2,34},{34,2},{3,35},{35,3},{4,36},{36... | collective-permute-start | bytes 1572872 | tf_op jit(solution)/shard_map/ppermute | solution.py:27
  68.0 33.9 %all-to-all-start = ((bf16[16,128,256]{2,1,0:T(8,128)(2,1)}), bf16[16,128,256]{2,1,0:T(8,128)(2,1)}, u32[]{:S(2)}, u32[]{:S(2)}) async-start(bf16[16,128,256]{2,1,0:T(8,128)(2,1)} %bitcast.82), calls=%async_computation | async-start | bytes 2097152 | tf_op jit(solution)/shard_map/all_to_all | solution.py:31
  74.1 28.2 %collective-permute-start.29 = (bf16[4,96,1024]{2,1,0:T(8,128)(2,1)}, bf16[4,96,1024]{2,1,0:T(8,128)(2,1)}, u32[]{:S(2)}, u32[]{:S(2)}) collective-permute-start(bf16[4,96,1024]{2,1,0:T(8,128)(2,1)} %pad_maximum_fusion.1.refs_0_), channel_id=1, source_target_pairs={{0,32},{32,0},{1,33},{33,1},{2,34},{34,2},{3,35},{35,3},{4,36},{36... | collective-permute-start | bytes 2359304 | tf_op jit(solution)/shard_map/ppermute | solution.py:27
  191.9 42.4 %all-to-all-start.1 = ((bf16[32,128,256]{2,1,0:T(8,128)(2,1)}), bf16[32,128,256]{2,1,0:T(8,128)(2,1)S(1)}, u32[]{:S(2)}, u32[]{:S(2)}) async-start(bf16[32,128,256]{2,1,0:T(8,128)(2,1)} %shard_map.52), calls=%async_computation.1 | async-start | bytes 4194304 | tf_op jit(solution)/shard_map/all_to_all | solution.py:31
  201.3 17.4 %collective-permute-start.37 = (f32[4,128]{1,0:T(4,128)S(1)}, f32[4,128]{1,0:T(4,128)S(1)}, u32[]{:S(2)}, u32[]{:S(2)}) collective-permute-start(f32[4,128]{1,0:T(4,128)S(1)} %get-tuple-element.46), channel_id=1, source_target_pairs={{0,0},{1,4},{2,8},{3,12},{4,40},{5,44},{6,32},{7,36},{8,16},{9,20}... | collective-permute-start | bytes 6152 | tf_op jit(solution)/shard_map/ppermute | solution.py:325
  202.0 20.2 %collective-permute-start.38 = (f32[4,128]{1,0:T(4,128)S(1)}, f32[4,128]{1,0:T(4,128)S(1)}, u32[]{:S(2)}, u32[]{:S(2)}) collective-permute-start(f32[4,128]{1,0:T(4,128)S(1)} %get-tuple-element.49), channel_id=1, source_target_pairs={{0,1},{1,5},{2,9},{3,13},{4,41},{5,45},{6,33},{7,37},{8,17},{9,21}... | collective-permute-start | bytes 6152 | tf_op jit(solution)/shard_map/ppermute | solution.py:325
  209.6 15.5 %collective-permute-start.39 = (f32[4,128]{1,0:T(4,128)S(1)}, f32[4,128]{1,0:T(4,128)S(1)}, u32[]{:S(2)}, u32[]{:S(2)}) collective-permute-start(f32[4,128]{1,0:T(4,128)S(1)} %get-tuple-element.48), channel_id=1, source_target_pairs={{0,2},{1,6},{2,10},{3,14},{4,42},{5,46},{6,34},{7,38},{8,18},{9,22... | collective-permute-start | bytes 6152 | tf_op jit(solution)/shard_map/ppermute | solution.py:325
  (47 other events, 367.7 us)

commit v6 on v5

--- a/solution.py
+++ b/solution.py
@@ -51,46 +51,32 @@
     return got
 
 
-def gather_weight(weight):
-    depth, columns = weight.shape
-    parts = jnp.moveaxis(weight.reshape(depth, 4, columns // 4), 1, 0)
-    q = (lax.axis_index("xh") ^ lax.axis_index("xl")) * 2 + (lax.axis_index("zh") ^ lax.axis_index("zl"))
-    near = [lax.dynamic_index_in_dim(parts, q ^ r, 0, keepdims=False) for r in range(4)]
-    got = []
-    for step in range(8):
-        part = near[step >> 1]
-        if step:
-            part = lax.ppermute(part, ("xl", "zl", "yh"), [(i, i ^ step) for i in range(8)])
-        got.append(part)
-    held = [jnp.stack(got[:4])[None], jnp.stack(got[4:])[None]]
-    far = held
-    for stage in range(2):
-        if stage:
-            held = joined(held, far)
-        far = [
-            lax.ppermute(piece, axes, [(i, i ^ 3) for i in range(4)])
-            for piece, axes in zip(held, (XZ, XZ[::-1])[stage])
-        ]
-    return [piece for both in zip(held, far) for piece in both]
+def hop_weight(held, stage):
+    return [
+        lax.ppermute(piece, axes, [(i, i ^ 3) for i in range(4)]) for piece, axes in zip(held, (XZ, XZ[::-1])[stage])
+    ]
 
 
 def weight_in_order(refs, out):
     depth = refs[0].shape[2]
-    for a in range(2):
-        for ex in range(2):
-            for ez in range(2):
-                first, second = (ez, ex) if a else (ex, ez)
-                for b in range(2):
-                    for y in range(2):
-                        place = (
-                            (lax.axis_index("xh") ^ ex) * 16
-                            + (lax.axis_index("xl") ^ ex ^ a) * 8
-                            + (lax.axis_index("zh") ^ ez) * 4
-                            + (lax.axis_index("zl") ^ ez ^ b) * 2
-                            + (lax.axis_index("yh") ^ y)
-                        )
-                        rows = pl.ds(pl.multiple_of(place * depth, depth), depth)
-                        out[rows, :] = refs[2 * a + second][first, 2 * b + y]
+    for run in range(2):
+        for e in range(8):
+            ex, ez = (e >> 1 & 1, e >> 2) if run == 0 else (e >> 2, e >> 1 & 1)
+            for b in range(2):
+                place = (
+                    (lax.axis_index("xh") ^ ex) * 16
+                    + (lax.axis_index("xl") ^ ex ^ run) * 8
+                    + (lax.axis_index("zh") ^ ez) * 4
+                    + (lax.axis_index("zl") ^ ez ^ b) * 2
+                    + (lax.axis_index("yh") ^ (e & 1))
+                )
+                rows = pl.ds(pl.multiple_of(place * depth, depth), depth)
+                out[rows, :] = refs[2 * run + e // 4][e % 4, b]
+
+
+def together(first, second):
+    both = lax.optimization_barrier((tuple(first), tuple(second)))
+    return list(both[0]), list(both[1])
 
 
 def after(value, *others):
@@ -342,23 +328,34 @@
         first, second = value[: rows // 2], value[rows // 2 :]
         return jnp.where(low, first, second), swap(jnp.where(low, second, first), "core")
 
+    parts = jnp.moveaxis(query_weight.reshape(depth, 4, width), 1, 0)
+    q = (lax.axis_index("xh") ^ lax.axis_index("xl")) * 2 + (lax.axis_index("zh") ^ lax.axis_index("zl"))
+    near = jnp.stack([lax.dynamic_index_in_dim(parts, q ^ r, 0, keepdims=False) for r in range(4)])
     share = jnp.concatenate(token_halves(student_hidden))
     held = [share[None, first:last] for first, last, _ in RUNS]
-    far = hop(held, 0)
-    w_own = gather_weight(query_weight)
-    w_other = [swap(piece, "core") for piece in w_own]
+    far, blocks = together(
+        hop(held, 0),
+        [near[0]] + [lax.ppermute(near[r], ("xl", "zl"), [(i, i ^ r) for i in range(4)]) for r in range(1, 4)],
+    )
     held = joined(held, far)
-    far = hop(held, 1)
+    blocks = jnp.stack(blocks)
+    far, (more,) = together(hop(held, 1), [swap(blocks, "yh")])
+    held = joined(held, far)
+    blocks = jnp.stack([blocks, more])
+    runs = [blocks[:, :2], blocks[:, 2:]]
     t_own, t_other = token_halves(teacher_query)
     heads = jnp.stack([jnp.where(low, t_own, t_other), jnp.where(low, t_other, t_own)])
     heads = heads.reshape(2, rows // 2, 2, 2, 2, t_width).transpose(0, 4, 2, 3, 1, 5)
     heads = jnp.where(lax.axis_index("xh") == 0, heads, heads[:, :, ::-1])
     heads = jnp.stack([heads[0], heads[1][:, :, ::-1]])
     heads = heads.reshape(16, rows // 2, t_width)
-    held = joined(held, far)
     far = hop(held, 2)
     hidden = [piece for both in zip(held, far) for piece in both]
-    teacher = exchange(after(heads, *held), SPREAD).reshape(2048, t_width)
+    passed = hop_weight(runs, 0)
+    teacher = exchange(after(heads, *passed), SPREAD).reshape(2048, t_width)
+    runs = joined(runs, passed)
+    w_own = [piece for both in zip(runs, hop_weight(runs, 1)) for piece in both]
+    w_other = [swap(piece, "core") for piece in w_own]
     student = jnp.concatenate(trade(project(hidden, w_own, w_other)))
     teacher = after(teacher, student)
     hidden_other = [swap(piece, "core") for piece in hidden]

time: 236 us -> 226 us (0.958)
  starting transfers between devices: 77 us -> 67.9 us
  other arithmetic: 14.5 us -> 17.8 us
  local copies, waits for them, and re-layouts: 16.2 us -> 13.1 us
    ppermute x11 -> x7, starting transfers between devices: 22.6 us -> 10.5 us  [the longest x4 6.8 us: hop_weight(): lax.ppermute(piece, axes, [(i, i ^ 3) for i in range(4)])]
    ppermute x25 -> x26, starting transfers between devices: 9.07 us -> 15.1 us  [swap(): return lax.ppermute(value, axis, SWAP)]
    ppermute x6, waiting for transfers between devices: 11.6 us -> 16.2 us  [trade(): lax.ppermute(chunks[r], ('zh', 'zl', 'yh'), [(i, i ^ step) for i in range...]
    ppermute x25 -> x26, waiting for transfers between devices: 31 us -> 26.6 us  [swap(): return lax.ppermute(value, axis, SWAP)]
    all_to_all x2, starting transfers between devices: 15.5 us -> 12.3 us  [exchange(): return lax.all_to_all(chunks, axes, split_axis=0, concat_axis=0, tiled=True)]
    unnamed x50, local copies, waits for them, and re-layouts: 9.86 us -> 6.9 us
    ppermute x11 -> x7, waiting for transfers between devices: 6.84 us -> 4.8 us  [the longest x4 3.27 us: hop_weight(): lax.ppermute(piece, axes, [(i, i ^ 3) for i in range(4)])]
  transfers between devices with their start and end apart: 48 -> 45, of which waited for: 20 -> 18; matrix products, arithmetic and copies ran while one was open for 7% -> 9% of each run, Pallas kernels for 2% -> 2%
where the time goes in v6:
time: 226 us; the launch traced here: 225 us
  starting transfers between devices  67.9 us (30%)
  waiting for transfers between devices  62.6 us (28%)
  Pallas kernels  62.5 us (28%)
  other arithmetic  17.8 us (8%)
  local copies, waits for them, and re-layouts  13.1 us (6%)
    pallas_call x1, Pallas kernels, relation(): pl.pallas_call(functools.partial(relation_kernel, block, chunk, sub), gri...  51.1 us
    ppermute x26, waiting for transfers between devices, swap(): return lax.ppermute(value, axis, SWAP)  26.6 us
    ppermute x4, starting transfers between devices, owned_rows(): got.append(lax.ppermute(sent, ('core',) + DP, pairs))  17.4 us
    ppermute x6, waiting for transfers between devices, trade(): lax.ppermute(chunks[r], ('zh', 'zl', 'yh'), [(i, i ^ step) for i in range...  16.2 us
    ppermute x26, starting transfers between devices, swap(): return lax.ppermute(value, axis, SWAP)  15.1 us
    ppermute x6, starting transfers between devices, trade(): lax.ppermute(chunks[r], ('zh', 'zl', 'yh'), [(i, i ^ step) for i in range...  12.5 us
    all_to_all x2, starting transfers between devices, exchange(): return lax.all_to_all(chunks, axes, split_axis=0, concat_axis=0, tiled=True)  12.3 us
    all_to_all x2, waiting for transfers between devices, exchange(): return lax.all_to_all(chunks, axes, split_axis=0, concat_axis=0, tiled=True)  8.59 us
  transfers between devices with their start and end apart: 45, of which 18 were waited for; matrix products, arithmetic and copies ran while one was open for 9% of the time, Pallas kernels for 2%

profile of v6, /device:TPU:8, one launch (start us, length us, event | category | flops | bytes accessed | tf_op | source)
XLA Modules:
  0.0 225.1 jit_solution(9542150147559585933)
XLA Ops:
  20.7 2.5 %collective-permute-start.11 = (bf16[4,128,256]{2,1,0:T(8,128)(2,1)S(1)}, bf16[4,128,256]{2,1,0:T(8,128)(2,1)}, u32[]{:S(2)}, u32[]{:S(2)}) collective-permute-start(bf16[4,128,256]{2,1,0:T(8,128)(2,1)S(1)} %get-tuple-element.58), channel_id=1, source_target_pairs={{0,1},{1,0},{2,3},{3,2},{4,5},{5,4},{6,7},{7,6},{8,9},{9,8},{10,11... | collective-permute-start | bytes 786440 | tf_op jit(solution)/shard_map/ppermute | solution.py:27
  23.2 11.7 %collective-permute-done.11 = bf16[4,128,256]{2,1,0:T(8,128)(2,1)} collective-permute-done((bf16[4,128,256]{2,1,0:T(8,128)(2,1)S(1)}, bf16[4,128,256]{2,1,0:T(8,128)(2,1)}, u32[]{:S(2)}, u32[]{:S(2)}) %collective-permute-start.11) | collective-permute-done | bytes 262176 | tf_op jit(solution)/shard_map/ppermute | solution.py:27
  36.6 2.7 %collective-permute-start.13 = (bf16[2,2,128,256]{3,2,1,0:T(8,128)(2,1)S(1)}, bf16[2,2,128,256]{3,2,1,0:T(8,128)(2,1)}, u32[]{:S(2)}, u32[]{:S(2)}) collective-permute-start(bf16[2,2,128,256]{3,2,1,0:T(8,128)(2,1)S(1)} %get-tuple-element.54), channel_id=1, source_target_pairs={{0,6},{2,4},{4,2},{6,0},{1,7},{3,5},{5,3},{7,1},{8,14},{10,12},{12... | collective-permute-start | bytes 786440 | tf_op jit(solution)/shard_map/ppermute | solution.py:56
  57.6 2.6 %collective-permute-done.15.refs_3_ = bf16[4,80,1024]{2,1,0:T(8,128)(2,1)S(1)} collective-permute-done((bf16[4,80,1024]{2,1,0:T(8,128)(2,1)S(1)}, bf16[4,80,1024]{2,1,0:T(8,128)(2,1)S(1)}, u32[]{:S(2)}, u32[]{:S(2)}) %collective-permute-start.15) | collective-permute-done | bytes 655392 | tf_op jit(solution)/shard_map/ppermute | solution.py:27
  60.8 2.6 %collective-permute-done.17.refs_7_ = bf16[4,2,128,256]{3,2,1,0:T(8,128)(2,1)} collective-permute-done((bf16[4,2,128,256]{3,2,1,0:T(8,128)(2,1)}, bf16[4,2,128,256]{3,2,1,0:T(8,128)(2,1)}, u32[]{:S(2)}, u32[]{:S(2)}) %collective-permute-start.17) | collective-permute-done | bytes 524320 | tf_op jit(solution)/shard_map/ppermute | solution.py:56
  67.3 4.3 %all-to-all-start = ((bf16[16,128,256]{2,1,0:T(8,128)(2,1)}), bf16[16,128,256]{2,1,0:T(8,128)(2,1)}, u32[]{:S(2)}, u32[]{:S(2)}) async-start(bf16[16,128,256]{2,1,0:T(8,128)(2,1)} %bitcast.76), calls=%async_computation | async-start | bytes 2097152 | tf_op jit(solution)/shard_map/all_to_all | solution.py:31
  71.7 5.5 %shard_map.50 = bf16[4,512,128]{2,1,0:T(8,128)(2,1)S(1)} custom-call(bf16[4,96,1024]{2,1,0:T(8,128)(2,1)} %copy-done.9, bf16[4,96,1024]{2,1,0:T(8,128)(2,1)} %collective-permute-done.14.refs_1_, bf16[4,80,1024]{2,1,0:T(8,128)(2,1)S(1)} %pad_maximum_fusion.2.refs_2_, bf16[4,80,1024]{2,1,0:T(8,128)(2,1)S(1)} %collective-permute-done.15.refs_3_, ...), custom_call_target="tpu_custom_call" | custom-call | flops 2147483648 | bytes 9437184 | tf_op jit(solution)/shard_map/pallas_call | solution.py:135
  77.3 3.3 %collective-permute-start.23 = (bf16[512,128]{1,0:T(8,128)(2,1)S(1)}, bf16[512,128]{1,0:T(8,128)(2,1)S(1)}, u32[]{:S(2)}, u32[]{:S(2)}) collective-permute-start(bf16[512,128]{1,0:T(8,128)(2,1)S(1)} %get-tuple-element.53), channel_id=1, source_target_pairs={{0,1},{1,0},{2,3},{3,2},{4,5},{5,4},{6,7},{7,6},{8,9},{9,8},{10,11... | collective-permute-start | bytes 393224 | tf_op jit(solution)/shard_map/ppermute | solution.py:50
  80.6 2.7 %collective-permute-start.24 = (bf16[512,128]{1,0:T(8,128)(2,1)S(1)}, bf16[512,128]{1,0:T(8,128)(2,1)S(1)}, u32[]{:S(2)}, u32[]{:S(2)}) collective-permute-start(bf16[512,128]{1,0:T(8,128)(2,1)S(1)} %get-tuple-element.52), channel_id=1, source_target_pairs={{0,6},{1,7},{2,4},{3,5},{4,2},{5,3},{6,0},{7,1},{8,14},{9,15},{10,... | collective-permute-start | bytes 393224 | tf_op jit(solution)/shard_map/ppermute | solution.py:50
  84.1 7.7 %collective-permute-done.23 = bf16[512,128]{1,0:T(8,128)(2,1)S(1)} collective-permute-done((bf16[512,128]{1,0:T(8,128)(2,1)S(1)}, bf16[512,128]{1,0:T(8,128)(2,1)S(1)}, u32[]{:S(2)}, u32[]{:S(2)}) %collective-permute-start.23) | collective-permute-done | bytes 131104 | tf_op jit(solution)/shard_map/ppermute | solution.py:50
  91.8 4.6 %collective-permute-done.25 = bf16[512,128]{1,0:T(8,128)(2,1)S(1)} collective-permute-done((bf16[512,128]{1,0:T(8,128)(2,1)S(1)}, bf16[512,128]{1,0:T(8,128)(2,1)S(1)}, u32[]{:S(2)}, u32[]{:S(2)}) %collective-permute-start.25) | collective-permute-done | bytes 131104 | tf_op jit(solution)/shard_map/ppermute | solution.py:50
  98.6 3.2 %collective-permute-done.31.refs_11_ = bf16[4,80,1024]{2,1,0:T(8,128)(2,1)S(1)} collective-permute-done((bf16[4,80,1024]{2,1,0:T(8,128)(2,1)S(1)}, bf16[4,80,1024]{2,1,0:T(8,128)(2,1)S(1)}, u32[]{:S(2)}, u32[]{:S(2)}) %collective-permute-start.31) | collective-permute-done | bytes 655392 | tf_op jit(solution)/shard_map/ppermute | solution.py:27
  107.4 51.1 %shard_map.51 = (f32[8,256]{1,0:T(8,128)S(1)}, f32[2048,128]{1,0:T(8,128)S(1)}, f32[2048,128]{1,0:T(8,128)S(1)}) custom-call(bf16[2048,256]{1,0:T(8,128)(2,1)} %bitcast.17.t_own, bf16[2048,128]{1,0:T(8,128)(2,1)S(1)} %copy-done.8, bf16[2048,256]{1,0:T(8,128)(2,1)} %copy-done.22, bf16[2048,128]{1,0:T(8,128)(2,1)S(1)} %collective-permute-done.33.s_other), custom_call_target="tpu_custom_call" | custom-call | flops 10737418240 | bytes 7864320 | tf_op jit(solution)/shard_map/pallas_call | solution.py:274
  158.8 2.5 %collective-permute-done.38 = f32[2048,128]{1,0:T(8,128)S(1)} collective-permute-done((f32[2048,128]{1,0:T(8,128)S(1)}, f32[2048,128]{1,0:T(8,128)S(1)}, u32[]{:S(2)}, u32[]{:S(2)}) %collective-permute-start.38) | collective-permute-done | bytes 1048608 | tf_op jit(solution)/shard_map/ppermute | solution.py:27
  163.0 5.4 %collective-permute-start.41 = (bf16[512,128]{1,0:T(8,128)(2,1)}, bf16[512,128]{1,0:T(8,128)(2,1)}, u32[]{:S(2)}, u32[]{:S(2)}) collective-permute-start(bf16[512,128]{1,0:T(8,128)(2,1)} %get-tuple-element.47), channel_id=1, source_target_pairs={{0,7},{1,6},{2,5},{3,4},{4,3},{5,2},{6,1},{7,0},{8,15},{9,14},{10,... | collective-permute-start | bytes 393224 | tf_op jit(solution)/shard_map/ppermute | solution.py:50
  169.7 2.6 %collective-permute-done.41 = bf16[512,128]{1,0:T(8,128)(2,1)} collective-permute-done((bf16[512,128]{1,0:T(8,128)(2,1)}, bf16[512,128]{1,0:T(8,128)(2,1)}, u32[]{:S(2)}, u32[]{:S(2)}) %collective-permute-start.41) | collective-permute-done | bytes 131104 | tf_op jit(solution)/shard_map/ppermute | solution.py:50
  177.1 5.8 %shard_map.52 = bf16[32,128,256]{2,1,0:T(8,128)(2,1)} custom-call(bf16[4,96,1024]{2,1,0:T(8,128)(2,1)} %copy-done.9, bf16[4,96,1024]{2,1,0:T(8,128)(2,1)} %collective-permute-done.14.refs_1_, bf16[4,80,1024]{2,1,0:T(8,128)(2,1)S(1)} %pad_maximum_fusion.2.refs_2_, bf16[4,80,1024]{2,1,0:T(8,128)(2,1)S(1)} %collective-permute-done.15.refs_3_, ...), custom_call_target="tpu_custom_call" | custom-call | flops 2147483648 | bytes 11534336 | tf_op jit(solution)/shard_map/pallas_call | solution.py:170
  182.9 8.0 %all-to-all-start.1 = ((bf16[32,128,256]{2,1,0:T(8,128)(2,1)}), bf16[32,128,256]{2,1,0:T(8,128)(2,1)S(1)}, u32[]{:S(2)}, u32[]{:S(2)}) async-start(bf16[32,128,256]{2,1,0:T(8,128)(2,1)} %shard_map.52), calls=%async_computation.1 | async-start | bytes 4194304 | tf_op jit(solution)/shard_map/all_to_all | solution.py:31
  191.6 7.6 %collective-permute-start.35 = (f32[4,128]{1,0:T(4,128)S(1)}, f32[4,128]{1,0:T(4,128)S(1)}, u32[]{:S(2)}, u32[]{:S(2)}) collective-permute-start(f32[4,128]{1,0:T(4,128)S(1)} %get-tuple-element.73), channel_id=1, source_target_pairs={{0,1},{1,5},{2,9},{3,13},{4,41},{5,45},{6,33},{7,37},{8,17},{9,21}... | collective-permute-start | bytes 6152 | tf_op jit(solution)/shard_map/ppermute | solution.py:311
  199.2 5.2 %collective-permute-start.36 = (f32[4,128]{1,0:T(4,128)S(1)}, f32[4,128]{1,0:T(4,128)S(1)}, u32[]{:S(2)}, u32[]{:S(2)}) collective-permute-start(f32[4,128]{1,0:T(4,128)S(1)} %get-tuple-element.72), channel_id=1, source_target_pairs={{0,2},{1,6},{2,10},{3,14},{4,42},{5,46},{6,34},{7,38},{8,18},{9,22... | collective-permute-start | bytes 6152 | tf_op jit(solution)/shard_map/ppermute | solution.py:311
  204.4 4.0 %collective-permute-start.37 = (f32[4,128]{1,0:T(4,128)S(1)}, f32[4,128]{1,0:T(4,128)S(1)}, u32[]{:S(2)}, u32[]{:S(2)}) collective-permute-start(f32[4,128]{1,0:T(4,128)S(1)} %get-tuple-element.71), channel_id=1, source_target_pairs={{0,3},{1,7},{2,11},{3,15},{4,43},{5,47},{6,35},{7,39},{8,19},{9,23... | collective-permute-start | bytes 6152 | tf_op jit(solution)/shard_map/ppermute | solution.py:311
  208.4 3.5 %collective-permute-done.35 = f32[4,128]{1,0:T(4,128)S(1)} collective-permute-done((f32[4,128]{1,0:T(4,128)S(1)}, f32[4,128]{1,0:T(4,128)S(1)}, u32[]{:S(2)}, u32[]{:S(2)}) %collective-permute-start.35) | collective-permute-done | bytes 2080 | tf_op jit(solution)/shard_map/ppermute | solution.py:311
  211.9 2.8 %collective-permute-done.36 = f32[4,128]{1,0:T(4,128)S(1)} collective-permute-done((f32[4,128]{1,0:T(4,128)S(1)}, f32[4,128]{1,0:T(4,128)S(1)}, u32[]{:S(2)}, u32[]{:S(2)}) %collective-permute-start.36) | collective-permute-done | bytes 2080 | tf_op jit(solution)/shard_map/ppermute | solution.py:311
  215.4 8.6 %all-to-all-done.1 = bf16[32,128,256]{2,1,0:T(8,128)(2,1)S(1)} async-done(((bf16[32,128,256]{2,1,0:T(8,128)(2,1)}), bf16[32,128,256]{2,1,0:T(8,128)(2,1)S(1)}, u32[]{:S(2)}, u32[]{:S(2)}) %all-to-all-start.1) | async-done | bytes 2097184 | tf_op jit(solution)/shard_map/all_to_all | solution.py:31
  (159 shorter events, 63.2 us)
Async XLA Ops:
  11.6 27.7 %collective-permute-start = (bf16[128,2048]{1,0:T(8,128)(2,1)S(1)}, bf16[128,2048]{1,0:T(8,128)(2,1)S(1)}, u32[]{:S(2)}, u32[]{:S(2)}) collective-permute-start(bf16[128,2048]{1,0:T(8,128)(2,1)S(1)} %broadcast_select_fusion.3), channel_id=1, source_target_pairs={{0,32},{32,0},{1,33},{33,1},{2,34},{34,2},{3,35},{35,3},{4,36},{36... | collective-permute-start | bytes 1572872 | tf_op jit(solution)/shard_map/ppermute | solution.py:27
  16.5 18.4 %collective-permute-start.10 = (bf16[2,80,1024]{2,1,0:T(8,128)(2,1)}, bf16[2,80,1024]{2,1,0:T(8,128)(2,1)}, u32[]{:S(2)}, u32[]{:S(2)}) collective-permute-start(bf16[2,80,1024]{2,1,0:T(8,128)(2,1)} %pad_maximum_fusion.10), channel_id=1, source_target_pairs={{0,8},{8,0},{1,9},{9,1},{2,10},{10,2},{3,11},{11,3},{4,12},{12,4},... | collective-permute-start | bytes 983048 | tf_op jit(solution)/shard_map/ppermute | solution.py:27
  18.0 16.9 %collective-permute-start.8 = (bf16[2,96,1024]{2,1,0:T(8,128)(2,1)S(1)}, bf16[2,96,1024]{2,1,0:T(8,128)(2,1)}, u32[]{:S(2)}, u32[]{:S(2)}) collective-permute-start(bf16[2,96,1024]{2,1,0:T(8,128)(2,1)S(1)} %pad_maximum_fusion.8), channel_id=1, source_target_pairs={{0,64},{64,0},{1,65},{65,1},{2,66},{66,2},{3,67},{67,3},{4,68},{68... | collective-permute-start | bytes 1179656 | tf_op jit(solution)/shard_map/ppermute | solution.py:27
  19.3 15.6 %collective-permute-start.9 = (bf16[2,80,1024]{2,1,0:T(8,128)(2,1)}, bf16[2,80,1024]{2,1,0:T(8,128)(2,1)}, u32[]{:S(2)}, u32[]{:S(2)}) collective-permute-start(bf16[2,80,1024]{2,1,0:T(8,128)(2,1)} %pad_maximum_fusion.9), channel_id=1, source_target_pairs={{0,2},{2,0},{1,3},{3,1},{4,6},{6,4},{5,7},{7,5},{8,10},{10,8},{9,1... | collective-permute-start | bytes 983048 | tf_op jit(solution)/shard_map/ppermute | solution.py:27
  20.7 14.2 %collective-permute-start.11 = (bf16[4,128,256]{2,1,0:T(8,128)(2,1)S(1)}, bf16[4,128,256]{2,1,0:T(8,128)(2,1)}, u32[]{:S(2)}, u32[]{:S(2)}) collective-permute-start(bf16[4,128,256]{2,1,0:T(8,128)(2,1)S(1)} %get-tuple-element.58), channel_id=1, source_target_pairs={{0,1},{1,0},{2,3},{3,2},{4,5},{5,4},{6,7},{7,6},{8,9},{9,8},{10,11... | collective-permute-start | bytes 786440 | tf_op jit(solution)/shard_map/ppermute | solution.py:27
  36.6 11.0 %collective-permute-start.13 = (bf16[2,2,128,256]{3,2,1,0:T(8,128)(2,1)S(1)}, bf16[2,2,128,256]{3,2,1,0:T(8,128)(2,1)}, u32[]{:S(2)}, u32[]{:S(2)}) collective-permute-start(bf16[2,2,128,256]{3,2,1,0:T(8,128)(2,1)S(1)} %get-tuple-element.54), channel_id=1, source_target_pairs={{0,6},{2,4},{4,2},{6,0},{1,7},{3,5},{5,3},{7,1},{8,14},{10,12},{12... | collective-permute-start | bytes 786440 | tf_op jit(solution)/shard_map/ppermute | solution.py:56
  43.6 14.0 %collective-permute-start.16 = (bf16[4,80,1024]{2,1,0:T(8,128)(2,1)S(1)}, bf16[4,80,1024]{2,1,0:T(8,128)(2,1)S(1)}, u32[]{:S(2)}, u32[]{:S(2)}) collective-permute-start(bf16[4,80,1024]{2,1,0:T(8,128)(2,1)S(1)} %pad_maximum_fusion.3.refs_4_), channel_id=1, source_target_pairs={{0,64},{64,0},{1,65},{65,1},{2,66},{66,2},{3,67},{67,3},{4,68},{68... | collective-permute-start | bytes 1966088 | tf_op jit(solution)/shard_map/ppermute | solution.py:27
  46.7 13.5 %collective-permute-start.15 = (bf16[4,80,1024]{2,1,0:T(8,128)(2,1)S(1)}, bf16[4,80,1024]{2,1,0:T(8,128)(2,1)S(1)}, u32[]{:S(2)}, u32[]{:S(2)}) collective-permute-start(bf16[4,80,1024]{2,1,0:T(8,128)(2,1)S(1)} %pad_maximum_fusion.2.refs_2_), channel_id=1, source_target_pairs={{0,8},{8,0},{1,9},{9,1},{2,10},{10,2},{3,11},{11,3},{4,12},{12,4},... | collective-permute-start | bytes 1966088 | tf_op jit(solution)/shard_map/ppermute | solution.py:27
  48.6 12.2 %collective-permute-start.18 = (bf16[4,2,128,256]{3,2,1,0:T(8,128)(2,1)S(1)}, bf16[4,2,128,256]{3,2,1,0:T(8,128)(2,1)}, u32[]{:S(2)}, u32[]{:S(2)}) collective-permute-start(bf16[4,2,128,256]{3,2,1,0:T(8,128)(2,1)S(1)} %pad_maximum_fusion.5.refs_8_), channel_id=1, source_target_pairs={{0,24},{8,16},{16,8},{24,0},{1,25},{9,17},{17,9},{25,1},{2,26},{10... | collective-permute-start | bytes 1572872 | tf_op jit(solution)/shard_map/ppermute | solution.py:56
  51.1 12.3 %collective-permute-start.17 = (bf16[4,2,128,256]{3,2,1,0:T(8,128)(2,1)}, bf16[4,2,128,256]{3,2,1,0:T(8,128)(2,1)}, u32[]{:S(2)}, u32[]{:S(2)}) collective-permute-start(bf16[4,2,128,256]{3,2,1,0:T(8,128)(2,1)} %pad_maximum_fusion.4.refs_6_), channel_id=1, source_target_pairs={{0,6},{2,4},{4,2},{6,0},{1,7},{3,5},{5,3},{7,1},{8,14},{10,12},{12... | collective-permute-start | bytes 1572872 | tf_op jit(solution)/shard_map/ppermute | solution.py:56
  54.8 16.9 %collective-permute-start.14 = (bf16[4,96,1024]{2,1,0:T(8,128)(2,1)S(1)}, bf16[4,96,1024]{2,1,0:T(8,128)(2,1)}, u32[]{:S(2)}, u32[]{:S(2)}) collective-permute-start(bf16[4,96,1024]{2,1,0:T(8,128)(2,1)S(1)} %pad_maximum_fusion.1.refs_0_), channel_id=1, source_target_pairs={{0,2},{2,0},{1,3},{3,1},{4,6},{6,4},{5,7},{7,5},{8,10},{10,8},{9,1... | collective-permute-start | bytes 2359304 | tf_op jit(solution)/shard_map/ppermute | solution.py:27
  57.6 14.0 %collective-permute-start.21 = (bf16[4,2,128,256]{3,2,1,0:T(8,128)(2,1)S(1)}, bf16[4,2,128,256]{3,2,1,0:T(8,128)(2,1)}, u32[]{:S(2)}, u32[]{:S(2)}) collective-permute-start(bf16[4,2,128,256]{3,2,1,0:T(8,128)(2,1)S(1)} %pad_maximum_fusion.5.refs_8_), channel_id=1, source_target_pairs={{0,32},{32,0},{1,33},{33,1},{2,34},{34,2},{3,35},{35,3},{4,36},{36... | collective-permute-start | bytes 1572872 | tf_op jit(solution)/shard_map/ppermute | solution.py:27
  60.2 11.5 %collective-permute-start.19 = (bf16[4,2,128,256]{3,2,1,0:T(8,128)(2,1)}, bf16[4,2,128,256]{3,2,1,0:T(8,128)(2,1)}, u32[]{:S(2)}, u32[]{:S(2)}) collective-permute-start(bf16[4,2,128,256]{3,2,1,0:T(8,128)(2,1)} %pad_maximum_fusion.4.refs_6_), channel_id=1, source_target_pairs={{0,32},{32,0},{1,33},{33,1},{2,34},{34,2},{3,35},{35,3},{4,36},{36... | collective-permute-start | bytes 1572872 | tf_op jit(solution)/shard_map/ppermute | solution.py:27
  60.8 10.8 %collective-permute-start.22 = (bf16[4,2,128,256]{3,2,1,0:T(8,128)(2,1)}, bf16[4,2,128,256]{3,2,1,0:T(8,128)(2,1)}, u32[]{:S(2)}, u32[]{:S(2)}) collective-permute-start(bf16[4,2,128,256]{3,2,1,0:T(8,128)(2,1)} %collective-permute-done.18.refs_9_), channel_id=1, source_target_pairs={{0,32},{32,0},{1,33},{33,1},{2,34},{34,2},{3,35},{35,3},{4,36},{36... | collective-permute-start | bytes 1572872 | tf_op jit(solution)/shard_map/ppermute | solution.py:27
  67.3 30.0 %all-to-all-start = ((bf16[16,128,256]{2,1,0:T(8,128)(2,1)}), bf16[16,128,256]{2,1,0:T(8,128)(2,1)}, u32[]{:S(2)}, u32[]{:S(2)}) async-start(bf16[16,128,256]{2,1,0:T(8,128)(2,1)} %bitcast.76), calls=%async_computation | async-start | bytes 2097152 | tf_op jit(solution)/shard_map/all_to_all | solution.py:31
  77.3 14.5 %collective-permute-start.23 = (bf16[512,128]{1,0:T(8,128)(2,1)S(1)}, bf16[512,128]{1,0:T(8,128)(2,1)S(1)}, u32[]{:S(2)}, u32[]{:S(2)}) collective-permute-start(bf16[512,128]{1,0:T(8,128)(2,1)S(1)} %get-tuple-element.53), channel_id=1, source_target_pairs={{0,1},{1,0},{2,3},{3,2},{4,5},{5,4},{6,7},{7,6},{8,9},{9,8},{10,11... | collective-permute-start | bytes 393224 | tf_op jit(solution)/shard_map/ppermute | solution.py:50
  80.6 11.2 %collective-permute-start.24 = (bf16[512,128]{1,0:T(8,128)(2,1)S(1)}, bf16[512,128]{1,0:T(8,128)(2,1)S(1)}, u32[]{:S(2)}, u32[]{:S(2)}) collective-permute-start(bf16[512,128]{1,0:T(8,128)(2,1)S(1)} %get-tuple-element.52), channel_id=1, source_target_pairs={{0,6},{1,7},{2,4},{3,5},{4,2},{5,3},{6,0},{7,1},{8,14},{9,15},{10,... | collective-permute-start | bytes 393224 | tf_op jit(solution)/shard_map/ppermute | solution.py:50
  83.4 13.0 %collective-permute-start.25 = (bf16[512,128]{1,0:T(8,128)(2,1)S(1)}, bf16[512,128]{1,0:T(8,128)(2,1)S(1)}, u32[]{:S(2)}, u32[]{:S(2)}) collective-permute-start(bf16[512,128]{1,0:T(8,128)(2,1)S(1)} %get-tuple-element.51), channel_id=1, source_target_pairs={{0,7},{1,6},{2,5},{3,4},{4,3},{5,2},{6,1},{7,0},{8,15},{9,14},{10,... | collective-permute-start | bytes 393224 | tf_op jit(solution)/shard_map/ppermute | solution.py:50
  83.6 14.2 %collective-permute-start.30 = (bf16[4,80,1024]{2,1,0:T(8,128)(2,1)S(1)}, bf16[4,80,1024]{2,1,0:T(8,128)(2,1)S(1)}, u32[]{:S(2)}, u32[]{:S(2)}) collective-permute-start(bf16[4,80,1024]{2,1,0:T(8,128)(2,1)S(1)} %copy-done.1), channel_id=1, source_target_pairs={{0,32},{32,0},{1,33},{33,1},{2,34},{34,2},{3,35},{35,3},{4,36},{36... | collective-permute-start | bytes 1966088 | tf_op jit(solution)/shard_map/ppermute | solution.py:27
  83.6 14.3 %collective-permute-start.28 = (bf16[4,80,1024]{2,1,0:T(8,128)(2,1)S(1)}, bf16[4,80,1024]{2,1,0:T(8,128)(2,1)}, u32[]{:S(2)}, u32[]{:S(2)}) collective-permute-start(bf16[4,80,1024]{2,1,0:T(8,128)(2,1)S(1)} %pad_maximum_fusion.2.refs_2_), channel_id=1, source_target_pairs={{0,32},{32,0},{1,33},{33,1},{2,34},{34,2},{3,35},{35,3},{4,36},{36... | collective-permute-start | bytes 1966088 | tf_op jit(solution)/shard_map/ppermute | solution.py:27
  182.9 41.0 %all-to-all-start.1 = ((bf16[32,128,256]{2,1,0:T(8,128)(2,1)}), bf16[32,128,256]{2,1,0:T(8,128)(2,1)S(1)}, u32[]{:S(2)}, u32[]{:S(2)}) async-start(bf16[32,128,256]{2,1,0:T(8,128)(2,1)} %shard_map.52), calls=%async_computation.1 | async-start | bytes 4194304 | tf_op jit(solution)/shard_map/all_to_all | solution.py:31
  191.0 17.4 %collective-permute-start.34 = (f32[4,128]{1,0:T(4,128)S(1)}, f32[4,128]{1,0:T(4,128)S(1)}, u32[]{:S(2)}, u32[]{:S(2)}) collective-permute-start(f32[4,128]{1,0:T(4,128)S(1)} %get-tuple-element.70), channel_id=1, source_target_pairs={{0,0},{1,4},{2,8},{3,12},{4,40},{5,44},{6,32},{7,36},{8,16},{9,20}... | collective-permute-start | bytes 6152 | tf_op jit(solution)/shard_map/ppermute | solution.py:311
  191.6 20.2 %collective-permute-start.35 = (f32[4,128]{1,0:T(4,128)S(1)}, f32[4,128]{1,0:T(4,128)S(1)}, u32[]{:S(2)}, u32[]{:S(2)}) collective-permute-start(f32[4,128]{1,0:T(4,128)S(1)} %get-tuple-element.73), channel_id=1, source_target_pairs={{0,1},{1,5},{2,9},{3,13},{4,41},{5,45},{6,33},{7,37},{8,17},{9,21}... | collective-permute-start | bytes 6152 | tf_op jit(solution)/shard_map/ppermute | solution.py:311
  199.2 15.5 %collective-permute-start.36 = (f32[4,128]{1,0:T(4,128)S(1)}, f32[4,128]{1,0:T(4,128)S(1)}, u32[]{:S(2)}, u32[]{:S(2)}) collective-permute-start(f32[4,128]{1,0:T(4,128)S(1)} %get-tuple-element.72), channel_id=1, source_target_pairs={{0,2},{1,6},{2,10},{3,14},{4,42},{5,46},{6,34},{7,38},{8,18},{9,22... | collective-permute-start | bytes 6152 | tf_op jit(solution)/shard_map/ppermute | solution.py:311
  (44 other events, 287.9 us)
